TPU v7x, 256 devices: a whole 4x4x8 slice. The times are simulated.
256 devices in a mesh: grp: 32 (over y, x, core), ctx: 8 (over z).
Axes of the slice: x: 4, y: 4, z: 8, core: 2. Of those that a mesh axis runs over, the one named last changes fastest.
Arguments:
- hidden: bfloat16 [65536, 3584], P(('grp', 'ctx')), may hold values from -6 to 6
- norm_gain: float32 [3584], replicated, may hold values from 0.1 to 1.9
- qkv_weight: bfloat16 [3584, 2304], P('grp'), may hold values from -4.008919 to 4.008919
- qkv_bias: float32 [2304], replicated, may hold values from -3 to 3
- repo_lengths: int32 [32, 6], P('grp'), may hold values from 1 to 1024, 2048 in all within a row
Outputs:
- context: bfloat16 [65536, 1792], P(('grp', 'ctx'))
All inputs are finite; a program needn't handle non-finite values.
Results may differ from a plain program's by a relative error of at most 0.0059.
The roundings to bfloat16 on the way count: a program that leaves them out, or rounds other values in their place, can miss the bound.
Values may be sent and summed in bfloat16 or wider, within the bound.
No kernel may reach another device: no remote copies, remote signals or barrier semaphores. Data moves between devices by JAX's collectives and lax.ppermute only.
A program may use at most 128 MiB of HBM per device.

v0:
```python
import jax
import jax.numpy as jnp
from jax import lax
from jax.sharding import PartitionSpec as P

HEAD_DIM = 128
HEADS = 14
KV_HEADS = 2


rope_base = 1000000.0
norm_eps = 1e-06


def rope_tables(position):
    inv_freq = rope_base ** (-jnp.arange(0, HEAD_DIM, 2, dtype=jnp.float32) / HEAD_DIM)
    angle = position.astype(jnp.float32)[:, None] * inv_freq[None, :]
    angle = jnp.concatenate([angle, angle], axis=-1)
    return (jnp.cos(angle), jnp.sin(angle))


def rotate(values, cosine, sine_part):
    half = HEAD_DIM // 2
    first = values[..., :half]
    second = values[..., half:]
    turned = jnp.concatenate([-second, first], axis=-1)
    return values * cosine[:, None, :] + turned * sine_part[:, None, :]


def body(hidden, norm_gain, qkv_weight, qkv_bias, repo_lengths):
    tok_rows = hidden.shape[0]
    group_heads = HEADS // KV_HEADS
    hidden_f32 = hidden.astype(jnp.float32)
    normed = (
        hidden_f32
        * lax.rsqrt(jnp.mean(hidden_f32 * hidden_f32, axis=1, keepdims=True) + norm_eps)
        * norm_gain[None, :]
    ).astype(jnp.bfloat16)
    projected_f32 = jnp.dot(
        normed,
        lax.all_gather(qkv_weight, "grp", axis=0, tiled=True),
        preferred_element_type=jnp.float32,
    )
    projected = (projected_f32 + qkv_bias[None, :]).astype(jnp.bfloat16)
    lengths = repo_lengths[0]
    tok_index = lax.axis_index("ctx") * tok_rows + jnp.arange(tok_rows, dtype=jnp.int32)
    repo_ends = jnp.cumsum(lengths)
    repo_start = jnp.sum(
        jnp.where(tok_index[:, None] >= repo_ends[None, :], lengths[None, :], 0), axis=1
    )
    cosine, sine_part = rope_tables(tok_index - repo_start)
    q_cols = HEADS * HEAD_DIM
    k_cols = KV_HEADS * HEAD_DIM
    query_f32 = projected[:, :q_cols].astype(jnp.float32).reshape(tok_rows, HEADS, HEAD_DIM)
    key_f32 = (
        projected[:, q_cols : q_cols + k_cols]
        .astype(jnp.float32)
        .reshape(tok_rows, KV_HEADS, HEAD_DIM)
    )
    queries = (
        rotate(query_f32, cosine, sine_part)
        .astype(jnp.bfloat16)
        .reshape(tok_rows, KV_HEADS, group_heads, HEAD_DIM)
    )
    keys = rotate(key_f32, cosine, sine_part).astype(jnp.bfloat16).reshape(tok_rows, k_cols)
    values = projected[:, q_cols + k_cols :]
    row_max = jnp.full((KV_HEADS, group_heads, tok_rows), -1e30, jnp.float32)
    key_piece = lax.all_gather(keys, "ctx", axis=0, tiled=True)
    value_piece = lax.all_gather(values, "ctx", axis=0, tiled=True)
    key_count = key_piece.shape[0]
    key_heads = key_piece.reshape(key_count, KV_HEADS, HEAD_DIM)
    value_heads = value_piece.reshape(key_count, KV_HEADS, HEAD_DIM)
    scores = jnp.einsum(
        "rgho,kgo->ghrk", queries, key_heads, preferred_element_type=jnp.float32
    ) * HEAD_DIM ** (-0.5)
    key_index = jnp.arange(key_count, dtype=jnp.int32)
    allowed = (key_index[None, :] <= tok_index[:, None]) & (
        key_index[None, :] >= repo_start[:, None]
    )
    scores = jnp.where(allowed, scores, -1e30)
    new_max = jnp.maximum(row_max, jnp.max(scores, axis=-1))
    weights = jnp.where(allowed, jnp.exp(scores - new_max[..., None]), 0.0)
    new_total = jnp.sum(weights, axis=-1)
    rounded_weights = weights.astype(jnp.bfloat16)
    new_weighted = jnp.einsum(
        "ghrk,kgo->ghro", rounded_weights, value_heads, preferred_element_type=jnp.float32
    )
    result = new_weighted / new_total[..., None]
    return (
        jnp.transpose(result, (2, 0, 1, 3)).reshape(tok_rows, HEADS * HEAD_DIM).astype(jnp.bfloat16)
    )


def solution(mesh):
    in_specs = (P(("grp", "ctx"), None), P(), P("grp", None), P(), P("grp", None))
    out_specs = P(("grp", "ctx"), None)
    return jax.shard_map(body, mesh=mesh, in_specs=in_specs, out_specs=out_specs, check_vma=False)
```

profile of v0, /device:TPU:6, one launch (start us, length us, event | category | flops | bytes accessed | tf_op | source)
XLA Modules:
  0.0 203.0 jit_solution(906771220540744256)
XLA Ops:
  6.5 0.0 all-gather.4.cloned.1.call-start
  6.5 0.7 all-gather.4.cloned.1.call-update
  7.3 0.0 all-gather.6.cloned.1.call-start
  7.3 0.8 reduce-window.8
  8.2 0.7 select_reduce_fusion
  8.9 0.1 broadcast_multiply_fusion
  9.0 0.5 fusion.26
  9.5 0.1 copy.23
  9.6 0.1 copy.22
  9.7 1.9 fusion.7
  11.6 78.1 %all-gather.4.cloned.1.call-done = bf16[3584,2304]{1,0:T(8,128)(2,1)} async-done(((bf16[112,2304]{1,0:T(8,128)(2,1)}), bf16[3584,2304]{1,0:T(8,128)(2,1)}) %all-gather.4.cloned.1.call-update) | async-done | bytes 16515088 | tf_op jit(solution)/shard_map/all_gather | solution.py:41
  89.7 10.7 %fusion.6 = bf16[256,2304]{1,0:T(8,128)(2,1)S(1)} fusion(bf16[3584,2304]{1,0:T(8,128)(2,1)} %all-gather.4.cloned.1.call-done, bf16[256,3584]{1,0:T(8,128)(2,1)} %param.5, f32[3584]{0:T(1024)} %param.6, f32[256]{0:T(256)S(1)} %add_rsqrt_fusion, f32[2304]{0:T(1024)} %param.8), kind=kOutput, calls=%fused_computation.10 | convolution fusion | flops 4232708096 | bytes 19554304 | tf_op jit(solution)/shard_map/dot_general | solution.py:39
  100.5 0.7 slice_convert_fusion.1
  101.2 0.1 reshape.133
  101.3 0.3 slice_negate_fusion.1
  101.6 0.4 maximum_multiply_fusion.1
  102.0 0.1 mul.111
  102.1 0.7 fusion.24
  102.8 0.0 all-gather.6.cloned.1.call-update
  102.8 0.2 all-gather.8.cloned.1.call-start
  103.0 0.5 fusion.10
  103.6 1.4 slice_convert_fusion
  104.9 1.8 copy.24
  106.7 1.1 slice_negate_fusion
  107.8 0.0 all-gather.8.cloned.1.call-update
  107.9 33.4 %all-gather.6.cloned.1.call-done = bf16[2048,256]{1,0:T(8,128)(2,1)} async-done(((bf16[256,256]{1,0:T(8,128)(2,1)}), bf16[2048,256]{1,0:T(8,128)(2,1)}) %all-gather.6.cloned.1.call-update) | async-done | bytes 1048592 | tf_op jit(solution)/shard_map/all_gather | solution.py:68
  141.3 2.1 %reshape.134 = bf16[2048,2,128]{2,1,0:T(2,128)(2,1)} reshape(bf16[2048,256]{1,0:T(8,128)(2,1)} %all-gather.6.cloned.1.call-done) | data formatting | bytes 2097152 | tf_op jit(solution)/shard_map/reshape | solution.py:71
  143.4 13.5 %fusion = (f32[2,7,256]{2,1,0:T(8,128)S(1)}, f32[2,2048,256,7]{2,1,3,0:T(8,128)}) fusion(pred[256,2048]{0,1:T(8,128)(4,1)S(1)} %fusion.10, f32[256,2,7,64]{0,3,2,1:T(8,128)} %bitcast.48, f32[256,2,7,64]{0,3,2,1:T(8,128)S(1)} %bitcast.47, f32[256,2,7,128]{0,3,2,1:T(8,128)S(1)} %bitcast.45, f32[256,128]{0,1:T(8,128)S(1)} %get-tuple-element.12, ...), kind=kOutput, calls=%fused_computation.2 | convolution fusion | flops 1903358464 | bytes 34879488 | tf_op jit(solution)/shard_map/rgho,kgo->ghrk/dot_general | solution.py:73
  156.9 13.5 %fusion.1 = f32[2,7,256]{2,1,0:T(8,128)S(1)} fusion(f32[2,2048,256,7]{2,1,3,0:T(8,128)} %get-tuple-element.14, f32[2,7,256]{2,1,0:T(8,128)S(1)} %broadcast_maximum_fusion, pred[256,2048]{0,1:T(8,128)(4,1)S(1)} %fusion.10), kind=kLoop, calls=%fused_computation.3 | loop fusion | flops 36696576 | bytes 29913088 | tf_op jit(solution)/shard_map/reduce_sum | solution.py:83
  170.4 9.9 %all-gather.8.cloned.1.call-done = bf16[2048,256]{1,0:T(8,128)(2,1)} async-done(((bf16[256,256]{1,0:T(8,128)(2,1)}), bf16[2048,256]{1,0:T(8,128)(2,1)}) %all-gather.8.cloned.1.call-update) | async-done | bytes 1048592 | tf_op jit(solution)/shard_map/all_gather | solution.py:69
  180.3 1.5 copy.37
  181.8 13.3 %fusion.14 = bf16[256,2,7,128]{0,3,2,1:T(8,128)(2,1)S(1)} fusion(bf16[2048,2,128,1]{0,2,3,1:T(8,128)(2,1)S(1)} %bitcast.51, f32[2,2048,256,7]{2,1,3,0:T(8,128)} %get-tuple-element.14, f32[2,7,256]{2,1,0:T(8,128)S(1)} %broadcast_maximum_fusion, pred[256,2048]{0,1:T(8,128)(4,1)S(1)} %fusion.10, f32[256,2,7]{0,2,1:T(8,128)S(1)} %bitcast.53), kind=kOutput, calls=%fused_computation.21 | convolution fusion | flops 1916665856 | bytes 31879168 | tf_op jit(solution)/shard_map/ghrk,kgo->ghro/dot_general | solution.py:85
  195.1 1.4 copy.30
  (5 shorter events, 0.0 us)
Async XLA Ops:
  6.5 83.2 %all-gather.4.cloned.1.call-start = ((), (), s32[]{:S(2)}) async-start(), calls=%async_computation | async-start | bytes 17031168 | tf_op jit(solution)/shard_map/all_gather | solution.py:41
  7.3 134.0 %all-gather.6.cloned.1.call-start = ((), (), s32[]{:S(2)}) async-start(), calls=%async_computation.1 | async-start | bytes 1179648 | tf_op jit(solution)/shard_map/all_gather | solution.py:68
  102.8 77.5 %all-gather.8.cloned.1.call-start = ((), (), s32[]{:S(2)}) async-start(), calls=%async_computation.2 | async-start | bytes 1179648 | tf_op jit(solution)/shard_map/all_gather | solution.py:69
Sparse Core Ops, SparseCore 0:
  9.9 79.7 all-gather.3
  102.9 38.2 all-gather.5
  143.1 37.1 all-gather.7
where the time goes:
time: 203 us
  waiting for transfers between devices  122 us (60%)
  matrix products  37.5 us (18%)
  other arithmetic  22.6 us (11%)
  between operations  13.2 us (7%)
  local copies, waits for them, and re-layouts  7.21 us (4%)
    all_gather x1, waiting for transfers between devices, body(): lax.all_gather(qkv_weight, 'grp', axis=0, tiled=True)  78.1 us
    all_gather x1, waiting for transfers between devices, body(): key_piece = lax.all_gather(keys, 'ctx', axis=0, tiled=True)  33.4 us
    reduce_sum x1, other arithmetic, body(): new_total = jnp.sum(weights, axis=-1)  13.5 us
    dot_general x1, matrix products, body(): jnp.einsum('rgho,kgo->ghrk', queries, key_heads, preferred_element_type=j...  13.5 us
    dot_general x1, matrix products, body(): jnp.einsum('ghrk,kgo->ghro', rounded_weights, value_heads, preferred_elem...  13.3 us
    dot_general x1, matrix products, body(): jnp.dot(normed, lax.all_gather(qkv_weight, 'grp', axis=0, tiled=True), pr...  10.7 us
    all_gather x1, waiting for transfers between devices, body(): value_piece = lax.all_gather(values, 'ctx', axis=0, tiled=True)  9.88 us
  transfers between devices with their start and end apart: 3, of which 3 were waited for; matrix products, arithmetic and copies ran while one was open for 19% of the time, Pallas kernels for 0%

commit v1 on v0

v1 whole, which is shorter than its diff:
```python
import functools
import math

import jax
import jax.numpy as jnp
from jax import lax
from jax.experimental import pallas as pl
from jax.experimental.pallas import tpu as pltpu
from jax.sharding import Mesh
from jax.sharding import PartitionSpec as P

D = 3584
HEAD_DIM = 128
HEADS = 14
KV_HEADS = 2
GROUP = HEADS // KV_HEADS
LENGTH = 2048
TOK = 256
HALF = 128
ROWS = 512
WROWS = 112
QC = GROUP * HEAD_DIM
WINDOW = 1152
rope_base = 1000000.0
norm_eps = 1e-06
SCALE2 = HEAD_DIM ** (-0.5) * math.log2(math.e)
MASKED = -1e30
SIZES = {"x": 4, "y": 4, "core": 2, "ctx": 8}
ORDER = (0, -1, 1, 2)

ANY = pl.BlockSpec(memory_space=pl.ANY)
VM = pl.BlockSpec(memory_space=pltpu.VMEM)
SM = pl.BlockSpec(memory_space=pltpu.SMEM)


def params():
    return pltpu.CompilerParams(vmem_limit_bytes=48 << 20)


def ring(value, axis, step):
    n = SIZES[axis]
    return lax.ppermute(value, axis, [(i, (i + step) % n) for i in range(n)])


def gather_ring(own, first, second):
    row = jnp.concatenate(
        [own, ring(own, first, 1), ring(own, first, -1), ring(own, first, 2)], 0
    )
    below = ring(row, second, 1)
    above = ring(row, second, -1)
    half = row.shape[0] // 2
    far_top = ring(below[:half], second, 1)
    far_bottom = ring(above[half:], second, -1)
    return jnp.concatenate([row, below, above, far_top, far_bottom], 0)


def norm_kernel(before_ref, own_ref, after_ref, gain_ref, out_ref):
    gain = gain_ref[...]

    def rows(src, at, dst, count):
        value = src[pl.ds(at, count), :].astype(jnp.float32)
        mean = jnp.mean(value * value, axis=1, keepdims=True)
        out_ref[pl.ds(dst, count), :] = (value * lax.rsqrt(mean + norm_eps) * gain).astype(
            jnp.bfloat16
        )

    def run(src, dst, total):
        @pl.loop(0, total // 16)
        def _(i):
            at = pl.multiple_of(i * 16, 16)
            rows(src, at, pl.multiple_of(dst + i * 16, 16), 16)

    run(before_ref, 0, HALF)
    run(own_ref, HALF, TOK)
    run(after_ref, HALF + TOK, HALF)


def norm(before, own, after, gain):
    return pl.pallas_call(
        norm_kernel,
        out_shape=jax.ShapeDtypeStruct((ROWS, D), jnp.bfloat16),
        in_specs=[VM] * 4,
        out_specs=VM,
        compiler_params=params(),
        cost_estimate=pl.CostEstimate(
            flops=8 * ROWS * D, bytes_accessed=4 * ROWS * D, transcendentals=ROWS
        ),
        name="norm",
    )(before, own, after, gain.reshape(1, D))


def rotate(value, cosine, sine):
    return value * cosine + pltpu.roll(value, HEAD_DIM // 2, 1) * sine


def kv_kernel(at_ref, x_ref, k_ref, k_far_ref, v_ref, v_far_ref, bias_ref, cos_ref, sin_ref, out_ref, w_ref, sem):
    copies = []
    for piece, (src, lane) in enumerate(((k_ref, 0), (k_far_ref, 0), (v_ref, 128), (v_far_ref, 128))):
        for block in range(16):
            at = pl.multiple_of(at_ref[piece * 16 + block], 16)
            copy = pltpu.make_async_copy(
                src.at[pl.ds(block * WROWS, WROWS), :],
                w_ref.at[pl.ds(at, WROWS), pl.ds(lane, 128)],
                sem.at[piece * 16 + block],
            )
            copy.start()
            copies.append(copy)
    for copy in copies:
        copy.wait()

    @pl.loop(0, ROWS // 256)
    def _(i):
        rows = pl.ds(pl.multiple_of(i * 256, 256), 256)
        value = jnp.dot(x_ref[rows, :], w_ref[...], preferred_element_type=jnp.float32)
        value = (value + bias_ref[...]).astype(jnp.bfloat16)
        keys = rotate(value[:, :128].astype(jnp.float32), cos_ref[rows, :], sin_ref[rows, :])
        out_ref[rows, 0:128] = keys.astype(jnp.bfloat16)
        out_ref[rows, 128:256] = value[:, 128:]


def kv_project(at, x, pieces, bias, cosine, sine):
    return pl.pallas_call(
        kv_kernel,
        out_shape=jax.ShapeDtypeStruct((ROWS, 256), jnp.bfloat16),
        in_specs=[SM, VM, ANY, ANY, ANY, ANY, VM, VM, VM],
        out_specs=VM,
        scratch_shapes=[pltpu.VMEM((D, 256), jnp.bfloat16), pltpu.SemaphoreType.DMA((64,))],
        compiler_params=params(),
        cost_estimate=pl.CostEstimate(
            flops=2 * ROWS * D * 256, bytes_accessed=2 * (ROWS * D + D * 256), transcendentals=0
        ),
        name="kv_project",
    )(at, x, *pieces, bias, cosine, sine)


Q_CHUNKS = ((0, 256), (256, 256), (512, 256), (768, 128))


def q_kernel(x_ref, w_hbm, bias_ref, cos_ref, sin_ref, out_ref, w_ref, sem):
    copies = []
    for n, (at, wide) in enumerate(Q_CHUNKS):
        copy = pltpu.make_async_copy(
            w_hbm.at[:, pl.ds(at, wide)], w_ref.at[:, pl.ds(at, wide)], sem.at[n]
        )
        copy.start()
        copies.append(copy)
    for (at, wide), copy in zip(Q_CHUNKS, copies):
        copy.wait()

        @pl.loop(0, ROWS // 256)
        def _(i, at=at, wide=wide):
            rows = pl.ds(pl.multiple_of(i * 256, 256), 256)
            value = jnp.dot(
                x_ref[rows, :], w_ref[:, at : at + wide], preferred_element_type=jnp.float32
            )
            value = (value + bias_ref[:, at : at + wide]).astype(jnp.bfloat16).astype(jnp.float32)
            for lane in range(0, wide, 128):
                head = rotate(value[:, lane : lane + 128], cos_ref[rows, :], sin_ref[rows, :])
                out_ref[rows, at + lane : at + lane + 128] = head.astype(jnp.bfloat16)


def q_project(x, weight, bias, cosine, sine):
    return pl.pallas_call(
        q_kernel,
        out_shape=jax.ShapeDtypeStruct((ROWS, QC), jnp.bfloat16),
        in_specs=[VM, ANY, VM, VM, VM],
        out_specs=VM,
        scratch_shapes=[pltpu.VMEM((D, QC), jnp.bfloat16), pltpu.SemaphoreType.DMA((4,))],
        compiler_params=params(),
        cost_estimate=pl.CostEstimate(
            flops=2 * ROWS * D * QC, bytes_accessed=2 * (ROWS * D + D * QC), transcendentals=0
        ),
        name="q_project",
    )(x, weight, bias, cosine, sine)


def attention_kernel(tiles, base_ref, q_ref, kv4_ref, kv2_ref, kv0_ref, pos_ref, start_ref, *rest):
    outs = rest[: len(tiles)]
    kv_ref, score_ref, weight_ref, total_ref = rest[len(tiles) :]
    kv_ref[0:512, :] = kv4_ref[...]
    kv_ref[512:1024, :] = kv2_ref[...]
    kv_ref[1024:1536, :] = kv0_ref[...]
    for tile, out_ref in zip(tiles, outs):
        rows = slice(HALF * tile, HALF * (tile + 1))
        window = slice(HALF * tile, HALF * tile + WINDOW)
        q = jnp.concatenate(
            [q_ref[rows, h * HEAD_DIM : (h + 1) * HEAD_DIM] for h in range(GROUP)], 0
        )
        score_ref[...] = lax.dot_general(
            q,
            kv_ref[window, 0:128],
            (((1,), (1,)), ((), ())),
            preferred_element_type=jnp.float32,
        )
        key = lax.broadcasted_iota(jnp.int32, (HALF, WINDOW), 1) + (base_ref[0] + HALF * tile)
        key = jnp.where(key >= LENGTH, key - LENGTH, key)
        allowed = (key <= pos_ref[rows, :]) & (key >= start_ref[rows, :])
        mask = jnp.where(allowed, 0.0, MASKED)
        for h in range(GROUP):
            part = slice(h * HALF, (h + 1) * HALF)
            score = score_ref[part, :] * SCALE2 + mask
            top = jnp.max(score, axis=1, keepdims=True)
            weight = jnp.exp2(score - top)
            total_ref[part, :] = jnp.broadcast_to(
                jnp.sum(weight, axis=1, keepdims=True), (HALF, HEAD_DIM)
            )
            weight_ref[part, :] = weight.astype(jnp.bfloat16)
        mixed = jnp.dot(
            weight_ref[...], kv_ref[window, 128:256], preferred_element_type=jnp.float32
        )
        mixed = (mixed / total_ref[...]).astype(jnp.bfloat16)
        for h in range(GROUP):
            out_ref[:, h * HEAD_DIM : (h + 1) * HEAD_DIM] = mixed[h * HALF : (h + 1) * HALF]


def attention(tiles, base, q, kv4, kv2, kv0, pos, start):
    n = len(tiles)
    stack = GROUP * HALF
    return pl.pallas_call(
        functools.partial(attention_kernel, tiles),
        out_shape=[jax.ShapeDtypeStruct((HALF, QC), jnp.bfloat16)] * n,
        in_specs=[SM] + [VM] * 6,
        out_specs=[VM] * n,
        scratch_shapes=[
            pltpu.VMEM((1536, 256), jnp.bfloat16),
            pltpu.VMEM((stack, WINDOW), jnp.float32),
            pltpu.VMEM((stack, WINDOW), jnp.bfloat16),
            pltpu.VMEM((stack, HEAD_DIM), jnp.float32),
        ],
        compiler_params=params(),
        cost_estimate=pl.CostEstimate(
            flops=4 * n * stack * WINDOW * HEAD_DIM,
            bytes_accessed=4 << 20,
            transcendentals=n * stack * WINDOW,
        ),
        name="attention",
    )(base, q, kv4, kv2, kv0, pos, start)


def body(hidden, norm_gain, qkv_weight, qkv_bias, repo_lengths):
    z = lax.axis_index("ctx")
    odd = z % 2
    y, x, core = lax.axis_index("y"), lax.axis_index("x"), lax.axis_index("core")

    k_at, v_at = 1792 + odd * 128, 2048 + odd * 128
    k_own = lax.dynamic_slice(qkv_weight, (0, k_at), (WROWS, 128))
    v_own = lax.dynamic_slice(qkv_weight, (0, v_at), (WROWS, 128))
    q_own = lax.dynamic_slice(qkv_weight, (0, odd * QC), (WROWS, QC))
    q_bias = lax.dynamic_slice(qkv_bias, (odd * QC,), (QC,)).reshape(1, QC)
    kv_bias = jnp.concatenate(
        [lax.dynamic_slice(qkv_bias, (k_at,), (128,)), lax.dynamic_slice(qkv_bias, (v_at,), (128,))]
    ).reshape(1, 256)

    q_weight = lax.all_gather(q_own, ("y", "x", "core"), axis=0, tiled=True)
    k_weight = gather_ring(k_own, "x", "y")
    v_weight = gather_ring(v_own, "y", "x")
    before = ring(hidden[TOK - HALF :], "ctx", 1)
    after = ring(hidden[:HALF], "ctx", -1)
    k_far = ring(k_weight, "core", 1)
    v_far = ring(v_weight, "core", 1)

    outer = jnp.repeat(jnp.array(ORDER, jnp.int32), 4)
    inner = jnp.tile(jnp.array(ORDER, jnp.int32), 4)
    k_rows = (((y + outer) % 4) * 4 + (x + inner) % 4) * 2 * WROWS
    v_rows = (((y + inner) % 4) * 4 + (x + outer) % 4) * 2 * WROWS
    here, there = core * WROWS, (1 - core) * WROWS
    at = jnp.concatenate([k_rows + here, k_rows + there, v_rows + here, v_rows + there])

    lengths = repo_lengths[0]
    pos = (z * TOK - HALF + LENGTH + jnp.arange(ROWS, dtype=jnp.int32)) % LENGTH
    start = jnp.zeros((ROWS,), jnp.int32)
    end = jnp.int32(0)
    for r in range(repo_lengths.shape[1]):
        end = end + lengths[r]
        start = start + jnp.where(pos >= end, lengths[r], 0)
    inv_freq = rope_base ** (-jnp.arange(0, HEAD_DIM, 2, dtype=jnp.float32) / HEAD_DIM)
    angle = (pos - start).astype(jnp.float32)[:, None] * inv_freq[None, :]
    cosine, sine = jnp.cos(angle), jnp.sin(angle)
    cosine = jnp.concatenate([cosine, cosine], 1)
    sine = jnp.concatenate([-sine, sine], 1)

    normed = norm(before, hidden, after, norm_gain)
    kv0 = kv_project(at, normed, (k_weight, k_far, v_weight, v_far), kv_bias, cosine, sine)
    kv2 = ring(kv0, "ctx", 2)
    kv4 = ring(kv2, "ctx", 2)
    q = q_project(normed, q_weight, q_bias, cosine, sine)

    base = ((z * TOK - HALF - 1024 + LENGTH) % LENGTH).reshape(1)
    args = (base, q, kv4, kv2, kv0, pos.reshape(ROWS, 1), start.reshape(ROWS, 1))
    back, ahead = attention((0, 3), *args)
    low = ring(ahead, "ctx", 1)
    high = ring(back, "ctx", -1)
    own = jnp.concatenate(attention((1, 2), *args), 0)
    other = jnp.concatenate([low, high], 0)
    return jnp.where(
        odd == 0, jnp.concatenate([own, other], 1), jnp.concatenate([other, own], 1)
    )


def solution(mesh):
    fine = Mesh(mesh.devices.reshape(4, 4, 2, 8), ("y", "x", "core", "ctx"))
    grp = ("y", "x", "core")
    tokens = P(("y", "x", "core", "ctx"), None)
    in_specs = (tokens, P(), P(grp, None), P(), P(grp, None))
    return jax.shard_map(body, mesh=fine, in_specs=in_specs, out_specs=tokens, check_vma=False)
```

time: 203 us -> 122 us (0.60)
  the two profiles are of different devices: /device:TPU:6 before, /device:TPU:2 now
where the time goes in v1:
time: 122 us
  starting transfers between devices  35.8 us (29%)
  Pallas kernels  27.1 us (22%)
  waiting for transfers between devices  20.7 us (17%)
  between operations  17.5 us (14%)
  other arithmetic  10.9 us (9%)
  local copies, waits for them, and re-layouts  9.92 us (8%)
    ppermute x22, starting transfers between devices, ring(): return lax.ppermute(value, axis, [(i, (i + step) % n) for i in range(n)])  35.8 us
    ppermute x22, waiting for transfers between devices, ring(): return lax.ppermute(value, axis, [(i, (i + step) % n) for i in range(n)])  20.7 us
    pallas_call x2, Pallas kernels, attention(): pl.pallas_call(functools.partial(attention_kernel, tiles), out_shape=[jax...  8.8 us
    pallas_call x1, Pallas kernels, q_project(): pl.pallas_call(q_kernel, out_shape=jax.ShapeDtypeStruct((ROWS, QC), jnp.b...  7.25 us
    pallas_call x1, Pallas kernels, norm(): pl.pallas_call(norm_kernel, out_shape=jax.ShapeDtypeStruct((ROWS, D), jnp...  6.32 us
    pallas_call x1, Pallas kernels, kv_project(): pl.pallas_call(kv_kernel, out_shape=jax.ShapeDtypeStruct((ROWS, 256), jnp...  4.76 us
    select_n x1, other arithmetic, body(): pos = (z * TOK - HALF + LENGTH + jnp.arange(ROWS, dtype=jnp.int32)) % LENGTH  4.01 us
    convert_element_type x1, other arithmetic, body(): angle = (pos - start).astype(jnp.float32)[:, None] * inv_freq[None, :]  3.77 us
  transfers between devices with their start and end apart: 23, of which 8 were waited for; matrix products, arithmetic and copies ran while one was open for 13% of the time, Pallas kernels for 19%

profile of v1, /device:TPU:2, one launch (start us, length us, event | category | flops | bytes accessed | tf_op | source)
XLA Modules:
  0.0 122.0 jit_solution(1048453936678169908)
XLA Ops:
  6.5 1.6 %constant_dynamic-slice_fusion.2 = bf16[112,896]{1,0:T(8,128)(2,1)} fusion(bf16[112,2304]{1,0:T(8,128)(2,1)} %param.9, s32[]{:T(128)S(6)} %select_n.165), kind=kLoop, calls=%fused_computation.56 | loop fusion | bytes 401412 | tf_op jit(solution)/shard_map/dynamic_slice | solution.py:248
  8.2 0.8 constant_dynamic-update-slice_fusion.15
  9.0 1.6 %collective-permute-start.2 = (bf16[112,128]{1,0:T(8,128)(2,1)S(1)}, bf16[112,128]{1,0:T(8,128)(2,1)S(1)}, u32[]{:S(2)}, u32[]{:S(2)}) collective-permute-start(bf16[112,128]{1,0:T(8,128)(2,1)S(1)} %get-tuple-element.24), channel_id=1, source_target_pairs={{0,16},{16,32},{32,48},{48,0},{1,17},{17,33},{33,49},{49,1},{2,18}... | collective-permute-start | bytes 86024 | tf_op jit(solution)/shard_map/ppermute | solution.py:42
  10.6 0.9 collective-permute-start.3
  11.4 2.0 %collective-permute-start.4 = (bf16[112,128]{1,0:T(8,128)(2,1)S(1)}, bf16[112,128]{1,0:T(8,128)(2,1)S(1)}, u32[]{:S(2)}, u32[]{:S(2)}) collective-permute-start(bf16[112,128]{1,0:T(8,128)(2,1)S(1)} %get-tuple-element.24), channel_id=1, source_target_pairs={{0,32},{16,48},{32,0},{48,16},{1,33},{17,49},{33,1},{49,17},{2,34}... | collective-permute-start | bytes 86024 | tf_op jit(solution)/shard_map/ppermute | solution.py:42
  13.4 1.4 %collective-permute-start.10 = (bf16[112,128]{1,0:T(8,128)(2,1)S(1)}, bf16[112,128]{1,0:T(8,128)(2,1)S(1)}, u32[]{:S(2)}, u32[]{:S(2)}) collective-permute-start(bf16[112,128]{1,0:T(8,128)(2,1)S(1)} %get-tuple-element.14), channel_id=1, source_target_pairs={{0,64},{64,128},{128,192},{192,0},{1,65},{65,129},{129,193},{193,1... | collective-permute-start | bytes 86024 | tf_op jit(solution)/shard_map/ppermute | solution.py:42
  14.8 1.9 %collective-permute-start.11 = (bf16[112,128]{1,0:T(8,128)(2,1)S(1)}, bf16[112,128]{1,0:T(8,128)(2,1)S(1)}, u32[]{:S(2)}, u32[]{:S(2)}) collective-permute-start(bf16[112,128]{1,0:T(8,128)(2,1)S(1)} %get-tuple-element.14), channel_id=1, source_target_pairs={{0,192},{64,0},{128,64},{192,128},{1,193},{65,1},{129,65},{193,129... | collective-permute-start | bytes 86024 | tf_op jit(solution)/shard_map/ppermute | solution.py:42
  16.6 0.7 broadcast_add_fusion.5
  17.5 0.1 add.288
  17.7 0.1 add.276
  17.8 1.5 %fusion.20 = (s32[1,1]{1,0:T(1,128)}, s32[1,1]{1,0:T(1,128)}, s32[1,1]{1,0:T(1,128)}, s32[1,1]{1,0:T(1,128)}, s32[1,1]{1,0:T(1,128)}, /*index=5*/s32[1,1]{1,0:T(1,128)}) fusion(s32[1,6]{1,0:T(1,128)} %param.11), kind=kLoop, calls=%fused_computation.77 | loop fusion | bytes 48 | tf_op jit(solution)/shard_map/slice | solution.py:274
  23.1 0.8 fusion.19
  23.9 3.8 %subtract_convert_fusion = f32[512]{0:T(512)S(1)} fusion(s32[]{:T(128)} %bitcast.6, s32[]{:T(128)S(6)} %add.272, s32[]{:T(128)} %bitcast.5, s32[]{:T(128)S(6)} %add.270, s32[]{:T(128)} %bitcast.4, s32[]{:T(128)S(6)} %add.268, s32[]{:T(128)} %bitcast.3, s32[]{:T(128)S(6)} %add.266, s32[]{:T(128)} %bitcast.2, s32[]{:T(128)S(6)} %add.264, s32[]{:T(128)} %bitcast.1, ...), kind=kLoop, calls=%fused_computation.48 | loop fusion | flops 15872 | bytes 2096 | tf_op jit(solution)/shard_map/convert_element_type | solution.py:277
  27.7 1.6 %fusion.18 = (bf16[128,3584]{1,0:T(8,128)(2,1)S(1)}, bf16[128,3584]{1,0:T(8,128)(2,1)S(1)}) fusion(bf16[256,3584]{1,0:T(8,128)(2,1)} %own_ref.1), kind=kLoop, calls=%fused_computation.75 | loop fusion | bytes 3670016 | tf_op jit(solution)/shard_map/slice | solution.py:258
  29.4 1.9 %collective-permute-start.12 = (bf16[112,128]{1,0:T(8,128)(2,1)S(1)}, bf16[112,128]{1,0:T(8,128)(2,1)S(1)}, u32[]{:S(2)}, u32[]{:S(2)}) collective-permute-start(bf16[112,128]{1,0:T(8,128)(2,1)S(1)} %get-tuple-element.14), channel_id=1, source_target_pairs={{0,128},{64,192},{128,0},{192,64},{1,129},{65,193},{129,1},{193,65... | collective-permute-start | bytes 86024 | tf_op jit(solution)/shard_map/ppermute | solution.py:42
  31.2 1.9 %collective-permute-start = (bf16[128,3584]{1,0:T(8,128)(2,1)S(1)}, bf16[128,3584]{1,0:T(8,128)(2,1)S(1)}, u32[]{:S(2)}, u32[]{:S(2)}) collective-permute-start(bf16[128,3584]{1,0:T(8,128)(2,1)S(1)} %get-tuple-element.22), channel_id=1, source_target_pairs={{0,1},{1,2},{2,3},{3,4},{4,5},{5,6},{6,7},{7,0},{8,9},{9,10},{10,1... | collective-permute-start | bytes 2752520 | tf_op jit(solution)/shard_map/ppermute | solution.py:42
  33.2 4.1 %collective-permute-start.1 = (bf16[128,3584]{1,0:T(8,128)(2,1)S(1)}, bf16[128,3584]{1,0:T(8,128)(2,1)S(1)}, u32[]{:S(2)}, u32[]{:S(2)}) collective-permute-start(bf16[128,3584]{1,0:T(8,128)(2,1)S(1)} %get-tuple-element.21), channel_id=1, source_target_pairs={{0,7},{1,0},{2,1},{3,2},{4,3},{5,4},{6,5},{7,6},{8,15},{9,8},{10,9... | collective-permute-start | bytes 2752520 | tf_op jit(solution)/shard_map/ppermute | solution.py:42
  37.3 0.8 collective-permute-start.5
  38.0 2.6 %collective-permute-start.6 = (bf16[448,128]{1,0:T(8,128)(2,1)S(1)}, bf16[448,128]{1,0:T(8,128)(2,1)S(1)}, u32[]{:S(2)}, u32[]{:S(2)}) collective-permute-start(bf16[448,128]{1,0:T(8,128)(2,1)S(1)} %pad_maximum_fusion.2), channel_id=1, source_target_pairs={{0,192},{64,0},{128,64},{192,128},{1,193},{65,1},{129,65},{193,129... | collective-permute-start | bytes 344072 | tf_op jit(solution)/shard_map/ppermute | solution.py:42
  40.6 1.1 collective-permute-start.13
  41.8 1.5 %collective-permute-done.5 = bf16[448,128]{1,0:T(8,128)(2,1)S(1)} collective-permute-done((bf16[448,128]{1,0:T(8,128)(2,1)S(1)}, bf16[448,128]{1,0:T(8,128)(2,1)S(1)}, u32[]{:S(2)}, u32[]{:S(2)}) %collective-permute-start.5) | collective-permute-done | bytes 114720 | tf_op jit(solution)/shard_map/ppermute | solution.py:42
  43.3 1.4 %collective-permute-start.14 = (bf16[448,128]{1,0:T(8,128)(2,1)S(1)}, bf16[448,128]{1,0:T(8,128)(2,1)S(1)}, u32[]{:S(2)}, u32[]{:S(2)}) collective-permute-start(bf16[448,128]{1,0:T(8,128)(2,1)S(1)} %pad_maximum_fusion.3), channel_id=1, source_target_pairs={{0,48},{16,0},{32,16},{48,32},{1,49},{17,1},{33,17},{49,33},{2,50}... | collective-permute-start | bytes 344072 | tf_op jit(solution)/shard_map/ppermute | solution.py:42
  44.9 0.6 collective-permute-done.13
  45.5 2.7 %collective-permute-start.8 = (bf16[224,128]{1,0:T(8,128)(2,1)S(1)}, bf16[224,128]{1,0:T(8,128)(2,1)S(1)}, u32[]{:S(2)}, u32[]{:S(2)}) collective-permute-start(bf16[224,128]{1,0:T(8,128)(2,1)S(1)} %slice.61), channel_id=1, source_target_pairs={{0,192},{64,0},{128,64},{192,128},{1,193},{65,1},{129,65},{193,129... | collective-permute-start | bytes 172040 | tf_op jit(solution)/shard_map/ppermute | solution.py:42
  48.2 1.0 collective-permute-start.15
  49.2 1.0 collective-permute-done.7
  50.2 1.1 collective-permute-start.16
  51.4 0.1 collective-permute-start.9
  51.5 2.1 %collective-permute-done.15 = bf16[224,128]{1,0:T(8,128)(2,1)S(1)} collective-permute-done((bf16[224,128]{1,0:T(8,128)(2,1)S(1)}, bf16[224,128]{1,0:T(8,128)(2,1)S(1)}, u32[]{:S(2)}, u32[]{:S(2)}) %collective-permute-start.15) | collective-permute-done | bytes 57376 | tf_op jit(solution)/shard_map/ppermute | solution.py:42
  53.6 2.0 %collective-permute-done.16 = bf16[224,128]{1,0:T(8,128)(2,1)S(1)} collective-permute-done((bf16[224,128]{1,0:T(8,128)(2,1)S(1)}, bf16[224,128]{1,0:T(8,128)(2,1)S(1)}, u32[]{:S(2)}, u32[]{:S(2)}) %collective-permute-start.16) | collective-permute-done | bytes 57376 | tf_op jit(solution)/shard_map/ppermute | solution.py:42
  55.6 0.1 collective-permute-start.17
  55.8 1.0 fusion.4
  56.8 0.2 pad_maximum_fusion
  57.0 6.3 %norm.1.x_ref = bf16[512,3584]{1,0:T(8,128)(2,1)} custom-call(bf16[128,3584]{1,0:T(8,128)(2,1)S(1)} %collective-permute-done.before_ref, bf16[256,3584]{1,0:T(8,128)(2,1)S(1)} %copy-done.1, bf16[128,3584]{1,0:T(8,128)(2,1)S(1)} %collective-permute-done.1.after_ref, f32[1,3584]{1,0:T(1,128)S(1)} %reshape.140.gain_ref), custom_call_target="tpu_custom_call" | custom-call | flops 14680064 | bytes 7340032 | tf_op jit(solution)/shard_map/norm/pallas_call | solution.py:79
  63.3 4.8 %kv_project.1.kv0_ref = bf16[512,256]{1,0:T(8,128)(2,1)S(1)} custom-call(s32[64]{0:T(128)S(1)} %pad_add_fusion.at_ref, bf16[512,3584]{1,0:T(8,128)(2,1)} %norm.1.x_ref, bf16[1792,128]{1,0:T(8,128)(2,1)S(1)} %constant_dynamic-update-slice_fusion.k_ref, bf16[1792,128]{1,0:T(8,128)(2,1)S(1)} %collective-permute-done.9.k_far_ref, ...), custom_call_target="tpu_custom_call" | custom-call | flops 939524096 | bytes 5505024 | tf_op jit(solution)/shard_map/kv_project/pallas_call | solution.py:122
  68.1 1.0 collective-permute-start.18
  69.1 0.8 dynamic_slice.19
  69.9 4.0 %add_select_fusion = (s32[512,1]{1,0:T(8,128)S(1)}, s32[512,1]{1,0:T(8,128)S(1)}) fusion(s32[]{:T(128)S(6)} %add.260, s32[]{:T(128)} %bitcast.6, s32[]{:T(128)S(6)} %add.272, s32[]{:T(128)} %bitcast.5, s32[]{:T(128)S(6)} %add.270, s32[]{:T(128)} %bitcast.4, s32[]{:T(128)S(6)} %add.268, s32[]{:T(128)} %bitcast.3, s32[]{:T(128)S(6)} %add.266, s32[]{:T(128)} %bitcast.2, ...), kind=kLoop, calls=%fused_computation.1 | loop fusion | flops 14848 | bytes 4144 | tf_op jit(solution)/shard_map/jit(remainder)/select_n | solution.py:270
  73.9 10.8 %collective-permute-done.18.kv2_ref = bf16[512,256]{1,0:T(8,128)(2,1)S(1)} collective-permute-done((bf16[512,256]{1,0:T(8,128)(2,1)S(1)}, bf16[512,256]{1,0:T(8,128)(2,1)S(1)}, u32[]{:S(2)}, u32[]{:S(2)}) %collective-permute-start.18) | collective-permute-done | bytes 262176 | tf_op jit(solution)/shard_map/ppermute | solution.py:42
  84.7 5.0 %collective-permute-start.19 = (bf16[512,256]{1,0:T(8,128)(2,1)S(1)}, bf16[512,256]{1,0:T(8,128)(2,1)S(1)}, u32[]{:S(2)}, u32[]{:S(2)}) collective-permute-start(bf16[512,256]{1,0:T(8,128)(2,1)S(1)} %collective-permute-done.18.kv2_ref), channel_id=1, source_target_pairs={{0,2},{1,3},{2,4},{3,5},{4,6},{5,7},{6,0},{7,1},{8,10},{9,11},{10,... | collective-permute-start | bytes 786440 | tf_op jit(solution)/shard_map/ppermute | solution.py:42
  89.7 2.0 %copy-done = bf16[512,3584]{1,0:T(8,128)(2,1)S(1)} copy-done((bf16[512,3584]{1,0:T(8,128)(2,1)S(1)}, bf16[512,3584]{1,0:T(8,128)(2,1)}, u32[]{:S(2)}) %copy-start) | copy-done | bytes 3670040
  91.8 7.3 %q_project.1.q_ref = bf16[512,896]{1,0:T(8,128)(2,1)S(1)} custom-call(bf16[512,3584]{1,0:T(8,128)(2,1)S(1)} %copy-done, bf16[3584,896]{1,0:T(8,128)(2,1)} %all-gather.2.cloned.1.call-done.w_hbm, f32[1,896]{1,0:T(1,128)S(1)} %reshape.141.bias_ref, f32[512,128]{1,0:T(8,128)S(1)} %get-tuple-element.42.cos_ref, f32[512,128]{1,0:T(8,128)S(1)} %get-tuple-element.43.sin_ref), custom_call_target="tpu_custom_call" | custom-call | flops 3288334336 | bytes 10092544 | tf_op jit(solution)/shard_map/q_project/pallas_call | solution.py:163
  99.0 4.4 %attention.3 = (bf16[128,896]{1,0:T(8,128)(2,1)S(1)}, bf16[128,896]{1,0:T(8,128)(2,1)S(1)}) custom-call(s32[1]{0:T(128)} %bitcast.base_ref, bf16[512,896]{1,0:T(8,128)(2,1)S(1)} %q_project.1.q_ref, bf16[512,256]{1,0:T(8,128)(2,1)S(1)} %collective-permute-done.19.kv4_ref, bf16[512,256]{1,0:T(8,128)(2,1)S(1)} %collective-permute-done.18.kv2_ref, ...), custom_call_target="tpu_custom_call" | custom-call | flops 1056964608 | bytes 4194304 | tf_op jit(solution)/shard_map/attention/pallas_call | solution.py:219
  103.5 3.2 %collective-permute-start.21 = (bf16[128,896]{1,0:T(8,128)(2,1)S(1)}, bf16[128,896]{1,0:T(8,128)(2,1)S(1)}, u32[]{:S(2)}, u32[]{:S(2)}) collective-permute-start(bf16[128,896]{1,0:T(8,128)(2,1)S(1)} %get-tuple-element.12), channel_id=1, source_target_pairs={{0,7},{1,0},{2,1},{3,2},{4,3},{5,4},{6,5},{7,6},{8,15},{9,8},{10,9... | collective-permute-start | bytes 688136 | tf_op jit(solution)/shard_map/ppermute | solution.py:42
  106.8 4.4 %attention.2 = (bf16[128,896]{1,0:T(8,128)(2,1)S(1)}, bf16[128,896]{1,0:T(8,128)(2,1)S(1)}) custom-call(s32[1]{0:T(128)} %bitcast.base_ref, bf16[512,896]{1,0:T(8,128)(2,1)S(1)} %q_project.1.q_ref, bf16[512,256]{1,0:T(8,128)(2,1)S(1)} %collective-permute-done.19.kv4_ref, bf16[512,256]{1,0:T(8,128)(2,1)S(1)} %collective-permute-done.18.kv2_ref, ...), custom_call_target="tpu_custom_call" | custom-call | flops 1056964608 | bytes 4194304 | tf_op jit(solution)/shard_map/attention/pallas_call | solution.py:219
  111.2 0.8 collective-permute-done.20
  112.0 1.9 %collective-permute-done.21 = bf16[128,896]{1,0:T(8,128)(2,1)S(1)} collective-permute-done((bf16[128,896]{1,0:T(8,128)(2,1)S(1)}, bf16[128,896]{1,0:T(8,128)(2,1)S(1)}, u32[]{:S(2)}, u32[]{:S(2)}) %collective-permute-start.21) | collective-permute-done | bytes 229408 | tf_op jit(solution)/shard_map/ppermute | solution.py:42
  114.0 1.2 maximum_select_fusion
  (62 shorter events, 1.0 us)
Async XLA Ops:
  6.5 83.2 %all-gather.2.cloned.1.call-start = ((), (), s32[]{:S(2)}) async-start(), calls=%async_computation | async-start | bytes 6623232 | tf_op jit(solution)/shard_map/all_gather | solution.py:254
  9.0 20.4 %collective-permute-start.2 = (bf16[112,128]{1,0:T(8,128)(2,1)S(1)}, bf16[112,128]{1,0:T(8,128)(2,1)S(1)}, u32[]{:S(2)}, u32[]{:S(2)}) collective-permute-start(bf16[112,128]{1,0:T(8,128)(2,1)S(1)} %get-tuple-element.24), channel_id=1, source_target_pairs={{0,16},{16,32},{32,48},{48,0},{1,17},{17,33},{33,49},{49,1},{2,18}... | collective-permute-start | bytes 86024 | tf_op jit(solution)/shard_map/ppermute | solution.py:42
  10.6 20.7 %collective-permute-start.3 = (bf16[112,128]{1,0:T(8,128)(2,1)S(1)}, bf16[112,128]{1,0:T(8,128)(2,1)S(1)}, u32[]{:S(2)}, u32[]{:S(2)}) collective-permute-start(bf16[112,128]{1,0:T(8,128)(2,1)S(1)} %get-tuple-element.24), channel_id=1, source_target_pairs={{0,48},{16,0},{32,16},{48,32},{1,49},{17,1},{33,17},{49,33},{2,50}... | collective-permute-start | bytes 86024 | tf_op jit(solution)/shard_map/ppermute | solution.py:42
  11.4 21.7 %collective-permute-start.4 = (bf16[112,128]{1,0:T(8,128)(2,1)S(1)}, bf16[112,128]{1,0:T(8,128)(2,1)S(1)}, u32[]{:S(2)}, u32[]{:S(2)}) collective-permute-start(bf16[112,128]{1,0:T(8,128)(2,1)S(1)} %get-tuple-element.24), channel_id=1, source_target_pairs={{0,32},{16,48},{32,0},{48,16},{1,33},{17,49},{33,1},{49,17},{2,34}... | collective-permute-start | bytes 86024 | tf_op jit(solution)/shard_map/ppermute | solution.py:42
  13.4 23.8 %collective-permute-start.10 = (bf16[112,128]{1,0:T(8,128)(2,1)S(1)}, bf16[112,128]{1,0:T(8,128)(2,1)S(1)}, u32[]{:S(2)}, u32[]{:S(2)}) collective-permute-start(bf16[112,128]{1,0:T(8,128)(2,1)S(1)} %get-tuple-element.14), channel_id=1, source_target_pairs={{0,64},{64,128},{128,192},{192,0},{1,65},{65,129},{129,193},{193,1... | collective-permute-start | bytes 86024 | tf_op jit(solution)/shard_map/ppermute | solution.py:42
  14.8 23.2 %collective-permute-start.11 = (bf16[112,128]{1,0:T(8,128)(2,1)S(1)}, bf16[112,128]{1,0:T(8,128)(2,1)S(1)}, u32[]{:S(2)}, u32[]{:S(2)}) collective-permute-start(bf16[112,128]{1,0:T(8,128)(2,1)S(1)} %get-tuple-element.14), channel_id=1, source_target_pairs={{0,192},{64,0},{128,64},{192,128},{1,193},{65,1},{129,65},{193,129... | collective-permute-start | bytes 86024 | tf_op jit(solution)/shard_map/ppermute | solution.py:42
  27.7 1.6 %copy-start.2 = (f32[3584]{0:T(1024)S(1)}, f32[3584]{0:T(1024)}, u32[]{:S(2)}) copy-start(f32[3584]{0:T(1024)} %param.8) | copy-start | bytes 43012
  29.4 11.2 %collective-permute-start.12 = (bf16[112,128]{1,0:T(8,128)(2,1)S(1)}, bf16[112,128]{1,0:T(8,128)(2,1)S(1)}, u32[]{:S(2)}, u32[]{:S(2)}) collective-permute-start(bf16[112,128]{1,0:T(8,128)(2,1)S(1)} %get-tuple-element.14), channel_id=1, source_target_pairs={{0,128},{64,192},{128,0},{192,64},{1,129},{65,193},{129,1},{193,65... | collective-permute-start | bytes 86024 | tf_op jit(solution)/shard_map/ppermute | solution.py:42
  31.2 25.8 %collective-permute-start = (bf16[128,3584]{1,0:T(8,128)(2,1)S(1)}, bf16[128,3584]{1,0:T(8,128)(2,1)S(1)}, u32[]{:S(2)}, u32[]{:S(2)}) collective-permute-start(bf16[128,3584]{1,0:T(8,128)(2,1)S(1)} %get-tuple-element.22), channel_id=1, source_target_pairs={{0,1},{1,2},{2,3},{3,4},{4,5},{5,6},{6,7},{7,0},{8,9},{9,10},{10,1... | collective-permute-start | bytes 2752520 | tf_op jit(solution)/shard_map/ppermute | solution.py:42
  33.2 23.8 %collective-permute-start.1 = (bf16[128,3584]{1,0:T(8,128)(2,1)S(1)}, bf16[128,3584]{1,0:T(8,128)(2,1)S(1)}, u32[]{:S(2)}, u32[]{:S(2)}) collective-permute-start(bf16[128,3584]{1,0:T(8,128)(2,1)S(1)} %get-tuple-element.21), channel_id=1, source_target_pairs={{0,7},{1,0},{2,1},{3,2},{4,3},{5,4},{6,5},{7,6},{8,15},{9,8},{10,9... | collective-permute-start | bytes 2752520 | tf_op jit(solution)/shard_map/ppermute | solution.py:42
  37.3 6.1 %collective-permute-start.5 = (bf16[448,128]{1,0:T(8,128)(2,1)S(1)}, bf16[448,128]{1,0:T(8,128)(2,1)S(1)}, u32[]{:S(2)}, u32[]{:S(2)}) collective-permute-start(bf16[448,128]{1,0:T(8,128)(2,1)S(1)} %pad_maximum_fusion.2), channel_id=1, source_target_pairs={{0,64},{64,128},{128,192},{192,0},{1,65},{65,129},{129,193},{193,1... | collective-permute-start | bytes 344072 | tf_op jit(solution)/shard_map/ppermute | solution.py:42
  38.0 6.7 %collective-permute-start.6 = (bf16[448,128]{1,0:T(8,128)(2,1)S(1)}, bf16[448,128]{1,0:T(8,128)(2,1)S(1)}, u32[]{:S(2)}, u32[]{:S(2)}) collective-permute-start(bf16[448,128]{1,0:T(8,128)(2,1)S(1)} %pad_maximum_fusion.2), channel_id=1, source_target_pairs={{0,192},{64,0},{128,64},{192,128},{1,193},{65,1},{129,65},{193,129... | collective-permute-start | bytes 344072 | tf_op jit(solution)/shard_map/ppermute | solution.py:42
  40.6 4.9 %collective-permute-start.13 = (bf16[448,128]{1,0:T(8,128)(2,1)S(1)}, bf16[448,128]{1,0:T(8,128)(2,1)S(1)}, u32[]{:S(2)}, u32[]{:S(2)}) collective-permute-start(bf16[448,128]{1,0:T(8,128)(2,1)S(1)} %pad_maximum_fusion.3), channel_id=1, source_target_pairs={{0,16},{16,32},{32,48},{48,0},{1,17},{17,33},{33,49},{49,1},{2,18}... | collective-permute-start | bytes 344072 | tf_op jit(solution)/shard_map/ppermute | solution.py:42
  43.3 4.9 %collective-permute-start.14 = (bf16[448,128]{1,0:T(8,128)(2,1)S(1)}, bf16[448,128]{1,0:T(8,128)(2,1)S(1)}, u32[]{:S(2)}, u32[]{:S(2)}) collective-permute-start(bf16[448,128]{1,0:T(8,128)(2,1)S(1)} %pad_maximum_fusion.3), channel_id=1, source_target_pairs={{0,48},{16,0},{32,16},{48,32},{1,49},{17,1},{33,17},{49,33},{2,50}... | collective-permute-start | bytes 344072 | tf_op jit(solution)/shard_map/ppermute | solution.py:42
  44.7 5.5 %collective-permute-start.7 = (bf16[224,128]{1,0:T(8,128)(2,1)S(1)}, bf16[224,128]{1,0:T(8,128)(2,1)S(1)}, u32[]{:S(2)}, u32[]{:S(2)}) collective-permute-start(bf16[224,128]{1,0:T(8,128)(2,1)S(1)} %slice.60), channel_id=1, source_target_pairs={{0,64},{64,128},{128,192},{192,0},{1,65},{65,129},{129,193},{193,1... | collective-permute-start | bytes 172040 | tf_op jit(solution)/shard_map/ppermute | solution.py:42
  44.9 12.2 %copy-start.1 = (bf16[256,3584]{1,0:T(8,128)(2,1)S(1)}, bf16[256,3584]{1,0:T(8,128)(2,1)}, u32[]{:S(2)}) copy-start(bf16[256,3584]{1,0:T(8,128)(2,1)} %own_ref.1) | copy-start | bytes 5505028
  45.5 5.9 %collective-permute-start.8 = (bf16[224,128]{1,0:T(8,128)(2,1)S(1)}, bf16[224,128]{1,0:T(8,128)(2,1)S(1)}, u32[]{:S(2)}, u32[]{:S(2)}) collective-permute-start(bf16[224,128]{1,0:T(8,128)(2,1)S(1)} %slice.61), channel_id=1, source_target_pairs={{0,192},{64,0},{128,64},{192,128},{1,193},{65,1},{129,65},{193,129... | collective-permute-start | bytes 172040 | tf_op jit(solution)/shard_map/ppermute | solution.py:42
  48.2 5.3 %collective-permute-start.15 = (bf16[224,128]{1,0:T(8,128)(2,1)S(1)}, bf16[224,128]{1,0:T(8,128)(2,1)S(1)}, u32[]{:S(2)}, u32[]{:S(2)}) collective-permute-start(bf16[224,128]{1,0:T(8,128)(2,1)S(1)} %slice.62), channel_id=1, source_target_pairs={{0,16},{16,32},{32,48},{48,0},{1,17},{17,33},{33,49},{49,1},{2,18}... | collective-permute-start | bytes 172040 | tf_op jit(solution)/shard_map/ppermute | solution.py:42
  50.2 5.4 %collective-permute-start.16 = (bf16[224,128]{1,0:T(8,128)(2,1)S(1)}, bf16[224,128]{1,0:T(8,128)(2,1)S(1)}, u32[]{:S(2)}, u32[]{:S(2)}) collective-permute-start(bf16[224,128]{1,0:T(8,128)(2,1)S(1)} %slice.63), channel_id=1, source_target_pairs={{0,48},{16,0},{32,16},{48,32},{1,49},{17,1},{33,17},{49,33},{2,50}... | collective-permute-start | bytes 172040 | tf_op jit(solution)/shard_map/ppermute | solution.py:42
  51.4 12.0 %collective-permute-start.9 = (bf16[1792,128]{1,0:T(8,128)(2,1)S(1)}, bf16[1792,128]{1,0:T(8,128)(2,1)S(1)}, u32[]{:S(2)}, u32[]{:S(2)}) collective-permute-start(bf16[1792,128]{1,0:T(8,128)(2,1)S(1)} %constant_dynamic-update-slice_fusion.k_ref), channel_id=1, source_target_pairs={{0,8},{8,0},{1,9},{9,1},{2,10},{10,2},{3,11},{11,3},{4,12},{12,4},... | collective-permute-start | bytes 1376264 | tf_op jit(solution)/shard_map/ppermute | solution.py:42
  55.6 7.7 %collective-permute-start.17 = (bf16[1792,128]{1,0:T(8,128)(2,1)S(1)}, bf16[1792,128]{1,0:T(8,128)(2,1)S(1)}, u32[]{:S(2)}, u32[]{:S(2)}) collective-permute-start(bf16[1792,128]{1,0:T(8,128)(2,1)S(1)} %constant_dynamic-update-slice_fusion.8.v_ref), channel_id=1, source_target_pairs={{0,8},{8,0},{1,9},{9,1},{2,10},{10,2},{3,11},{11,3},{4,12},{12,4},... | collective-permute-start | bytes 1376264 | tf_op jit(solution)/shard_map/ppermute | solution.py:42
  68.1 16.6 %collective-permute-start.18 = (bf16[512,256]{1,0:T(8,128)(2,1)S(1)}, bf16[512,256]{1,0:T(8,128)(2,1)S(1)}, u32[]{:S(2)}, u32[]{:S(2)}) collective-permute-start(bf16[512,256]{1,0:T(8,128)(2,1)S(1)} %kv_project.1.kv0_ref), channel_id=1, source_target_pairs={{0,2},{1,3},{2,4},{3,5},{4,6},{5,7},{6,0},{7,1},{8,10},{9,11},{10,... | collective-permute-start | bytes 786440 | tf_op jit(solution)/shard_map/ppermute | solution.py:42
  84.7 14.3 %collective-permute-start.19 = (bf16[512,256]{1,0:T(8,128)(2,1)S(1)}, bf16[512,256]{1,0:T(8,128)(2,1)S(1)}, u32[]{:S(2)}, u32[]{:S(2)}) collective-permute-start(bf16[512,256]{1,0:T(8,128)(2,1)S(1)} %collective-permute-done.18.kv2_ref), channel_id=1, source_target_pairs={{0,2},{1,3},{2,4},{3,5},{4,6},{5,7},{6,0},{7,1},{8,10},{9,11},{10,... | collective-permute-start | bytes 786440 | tf_op jit(solution)/shard_map/ppermute | solution.py:42
  89.7 2.0 %copy-start = (bf16[512,3584]{1,0:T(8,128)(2,1)S(1)}, bf16[512,3584]{1,0:T(8,128)(2,1)}, u32[]{:S(2)}) copy-start(bf16[512,3584]{1,0:T(8,128)(2,1)} %norm.1.x_ref) | copy-start | bytes 11010052
  103.4 8.6 %collective-permute-start.20 = (bf16[128,896]{1,0:T(8,128)(2,1)S(1)}, bf16[128,896]{1,0:T(8,128)(2,1)S(1)}, u32[]{:S(2)}, u32[]{:S(2)}) collective-permute-start(bf16[128,896]{1,0:T(8,128)(2,1)S(1)} %get-tuple-element.11), channel_id=1, source_target_pairs={{0,1},{1,2},{2,3},{3,4},{4,5},{5,6},{6,7},{7,0},{8,9},{9,10},{10,1... | collective-permute-start | bytes 688136 | tf_op jit(solution)/shard_map/ppermute | solution.py:42
  103.5 10.4 %collective-permute-start.21 = (bf16[128,896]{1,0:T(8,128)(2,1)S(1)}, bf16[128,896]{1,0:T(8,128)(2,1)S(1)}, u32[]{:S(2)}, u32[]{:S(2)}) collective-permute-start(bf16[128,896]{1,0:T(8,128)(2,1)S(1)} %get-tuple-element.12), channel_id=1, source_target_pairs={{0,7},{1,0},{2,1},{3,2},{4,3},{5,4},{6,5},{7,6},{8,15},{9,8},{10,9... | collective-permute-start | bytes 688136 | tf_op jit(solution)/shard_map/ppermute | solution.py:42
Sparse Core Ops, SparseCore 0:
  10.0 56.8 all-gather.1

commit v2 on v0

v2 whole, which is shorter than its diff:
```python
import functools
import math

import jax
import jax.numpy as jnp
from jax import lax
from jax.experimental import pallas as pl
from jax.experimental.pallas import tpu as pltpu
from jax.sharding import Mesh
from jax.sharding import PartitionSpec as P

D = 3584
HEAD_DIM = 128
HEADS = 14
KV_HEADS = 2
GROUP = HEADS // KV_HEADS
LENGTH = 2048
TOK = 256
HALF = 128
ROWS = 512
WROWS = 112
REPOS = 6
QC = GROUP * HEAD_DIM
rope_base = 1000000.0
norm_eps = 1e-06
SCALE2 = HEAD_DIM ** (-0.5) * math.log2(math.e)
MASKED = -1e30
SIZES = {"x": 4, "y": 4, "core": 2, "ctx": 8}
ORDER = (0, -1, 1, 2)

VM = pl.BlockSpec(memory_space=pltpu.VMEM)
SM = pl.BlockSpec(memory_space=pltpu.SMEM)


def params(mebibytes):
    return pltpu.CompilerParams(vmem_limit_bytes=mebibytes << 20)


def ring(value, axis, step):
    n = SIZES[axis]
    return lax.ppermute(value, axis, [(i, (i + step) % n) for i in range(n)])


def hop(value, phase, step):
    pairs = []
    for y in range(4):
        for x in range(4):
            for core in range(2):
                to_y, to_x = (y, (x + step) % 4) if core == phase else ((y + step) % 4, x)
                pairs.append(((y * 4 + x) * 2 + core, (to_y * 4 + to_x) * 2 + core))
    return lax.ppermute(value, ("y", "x", "core"), pairs)


def first_phase(own):
    return jnp.concatenate([own, hop(own, 0, 1), hop(own, 0, -1), hop(own, 0, 2)], 0)


def place_weights(info_ref, pieces, chunks, w_refs):
    y, x = info_ref[0], info_ref[1]
    for side in range(2):
        core = info_ref[2] if side == 0 else 1 - info_ref[2]
        block = 0
        for piece in pieces[side]:
            for i in range(piece.shape[0] // WROWS):
                outer, inner = ORDER[block // 4], ORDER[block % 4]
                dy = jnp.where(core == 0, outer, inner)
                dx = jnp.where(core == 0, inner, outer)
                chip = ((y + dy + 4) % 4) * 4 + (x + dx + 4) % 4
                at = pl.multiple_of((chip * 2 + core) * WROWS, 16)
                for (lane, wide), w_ref in zip(chunks, w_refs):
                    w_ref[pl.ds(at, WROWS), :] = piece[
                        i * WROWS : (i + 1) * WROWS, lane : lane + wide
                    ]
                block += 1


def starts(lengths_ref, pos):
    start, end = jnp.zeros_like(pos), 0
    for r in range(REPOS):
        end = end + lengths_ref[0, r]
        start = start + jnp.where(pos >= end, lengths_ref[0, r], 0)
    return start


def norm_rows(src_ref, gain, out_ref, at, total):
    @pl.loop(0, total // 32)
    def _(i):
        value = src_ref[pl.ds(pl.multiple_of(i * 32, 32), 32), :].astype(jnp.float32)
        mean = jnp.mean(value * value, axis=1, keepdims=True)
        value = (value * lax.rsqrt(mean + norm_eps) * gain).astype(jnp.bfloat16)
        out_ref[pl.ds(pl.multiple_of(at + i * 32, 32), 32), :] = value


def prepare_kernel(info_ref, lengths_ref, hidden_ref, gain_ref, freq_ref, out_ref, cos_ref, sin_ref):
    norm_rows(hidden_ref, gain_ref[...], out_ref, 0, TOK)
    base = info_ref[3] * TOK - HALF + LENGTH
    sign = jnp.where(lax.broadcasted_iota(jnp.int32, (1, HEAD_DIM), 1) < HEAD_DIM // 2, -1.0, 1.0)

    @pl.loop(0, ROWS // 64)
    def _(i):
        at = pl.multiple_of(i * 64, 64)
        pos = (lax.broadcasted_iota(jnp.int32, (64, HEAD_DIM), 0) + (base + at)) & (LENGTH - 1)
        angle = (pos - starts(lengths_ref, pos)).astype(jnp.float32) * freq_ref[...]
        cos_ref[pl.ds(at, 64), :] = jnp.cos(angle)
        sin_ref[pl.ds(at, 64), :] = jnp.sin(angle) * sign


def prepare(info, lengths, hidden, gain, freq):
    table = jax.ShapeDtypeStruct((ROWS, HEAD_DIM), jnp.float32)
    return pl.pallas_call(
        prepare_kernel,
        out_shape=[jax.ShapeDtypeStruct((TOK, D), jnp.bfloat16), table, table],
        in_specs=[SM, SM, VM, VM, VM],
        out_specs=[VM] * 3,
        compiler_params=params(12),
        cost_estimate=pl.CostEstimate(
            flops=8 * TOK * D, bytes_accessed=4 * TOK * D, transcendentals=2 * ROWS * HEAD_DIM
        ),
        name="prepare",
    )(info, lengths, hidden, gain.reshape(1, D), freq)


def join_kernel(before_ref, own_ref, after_ref, gain_ref, out_ref):
    gain = gain_ref[...]
    norm_rows(before_ref, gain, out_ref, 0, HALF)
    norm_rows(after_ref, gain, out_ref, HALF + TOK, HALF)
    out_ref[HALF : HALF + TOK, :] = own_ref[...]


def join(before, own, after, gain):
    return pl.pallas_call(
        join_kernel,
        out_shape=jax.ShapeDtypeStruct((ROWS, D), jnp.bfloat16),
        in_specs=[VM] * 4,
        out_specs=VM,
        compiler_params=params(12),
        cost_estimate=pl.CostEstimate(
            flops=8 * TOK * D, bytes_accessed=4 * ROWS * D, transcendentals=TOK
        ),
        name="join",
    )(before, own, after, gain.reshape(1, D))


def rotate(value, cosine, sine):
    return value * cosine + pltpu.roll(value, HEAD_DIM // 2, 1) * sine


KV_CHUNKS = ((0, 256),)
Q_CHUNKS = ((0, 512), (512, 384))


def kv_kernel(count, info_ref, x_ref, bias_ref, cos_ref, sin_ref, *rest):
    out_ref, w_ref = rest[2 * count :]
    place_weights(info_ref, (rest[:count], rest[count : 2 * count]), KV_CHUNKS, (w_ref,))
    value = jnp.dot(x_ref[...], w_ref[...], preferred_element_type=jnp.float32)
    value = (value + bias_ref[...]).astype(jnp.bfloat16)
    keys = rotate(value[:, :128].astype(jnp.float32), cos_ref[...], sin_ref[...])
    out_ref[:, 0:128] = keys.astype(jnp.bfloat16)
    out_ref[:, 128:256] = value[:, 128:]


def q_kernel(count, info_ref, x_ref, bias_ref, cos_ref, sin_ref, *rest):
    out_ref, *w_refs = rest[2 * count :]
    place_weights(info_ref, (rest[:count], rest[count : 2 * count]), Q_CHUNKS, w_refs)
    for (at, wide), w_ref in zip(Q_CHUNKS, w_refs):
        value = jnp.dot(x_ref[...], w_ref[...], preferred_element_type=jnp.float32)
        value = (value + bias_ref[:, at : at + wide]).astype(jnp.bfloat16).astype(jnp.float32)
        for lane in range(0, wide, 128):
            head = rotate(value[:, lane : lane + 128], cos_ref[...], sin_ref[...])
            out_ref[:, at + lane : at + lane + 128] = head.astype(jnp.bfloat16)


def project(kernel, chunks, name, info, x, near, far, bias, cosine, sine):
    count, wide = len(near), sum(w for _, w in chunks)
    return pl.pallas_call(
        functools.partial(kernel, count),
        out_shape=jax.ShapeDtypeStruct((ROWS, wide), jnp.bfloat16),
        in_specs=[SM] + [VM] * (4 + 2 * count),
        out_specs=VM,
        scratch_shapes=[pltpu.VMEM((D, w), jnp.bfloat16) for _, w in chunks],
        compiler_params=params(20),
        cost_estimate=pl.CostEstimate(
            flops=2 * ROWS * D * wide, bytes_accessed=2 * (ROWS * D + D * wide), transcendentals=0
        ),
        name=name,
    )(info, x, bias, cosine, sine, *near, *far)


STACK = GROUP * HALF


def stacked(q_ref, tile):
    rows = slice(HALF * tile, HALF * (tile + 1))
    return jnp.concatenate(
        [q_ref[rows, h * HEAD_DIM : (h + 1) * HEAD_DIM] for h in range(GROUP)], 0
    )


def mask_of(info_ref, lengths_ref, tile, from_row, count):
    base = info_ref[3] * TOK - HALF + LENGTH
    key = lax.broadcasted_iota(jnp.int32, (HALF, count), 1) + (base - 1024 + from_row)
    key = key & (LENGTH - 1)
    pos = (lax.broadcasted_iota(jnp.int32, (HALF, 1), 0) + (base + HALF * tile)) & (LENGTH - 1)
    return jnp.where((key <= pos) & (key >= starts(lengths_ref, pos)), 0.0, MASKED)


def score(q_ref, tile, k, out_ref):
    out_ref[...] = lax.dot_general(
        stacked(q_ref, tile), k, (((1,), (1,)), ((), ())), preferred_element_type=jnp.float32
    )


def wide(column):
    return jnp.broadcast_to(column, (HALF, HEAD_DIM))


def first_kernel(info_ref, lengths_ref, q_ref, kv2_ref, kv0_ref, mix_ref, top_ref, sum_ref, kv_ref, *rest):
    score_refs, weight_refs = rest[:4], rest[4:]
    kv_ref[0:512, :] = kv2_ref[...]
    kv_ref[512:1024, :] = kv0_ref[...]
    counts = [640 + HALF * tile for tile in range(4)]
    score(q_ref, 0, kv_ref[0 : counts[0], 0:128], score_refs[0])
    for tile in range(4):
        if tile < 3:
            score(q_ref, tile + 1, kv_ref[0 : counts[tile + 1], 0:128], score_refs[tile + 1])
        mask = mask_of(info_ref, lengths_ref, tile, 512, counts[tile])
        for h in range(GROUP):
            part = slice(h * HALF, (h + 1) * HALF)
            at = slice(tile * STACK + h * HALF, tile * STACK + (h + 1) * HALF)
            value = score_refs[tile][part, :] * SCALE2 + mask
            top = jnp.max(value, axis=1, keepdims=True)
            weight = jnp.exp2(value - top)
            top_ref[at, :] = wide(top)
            sum_ref[at, :] = wide(jnp.sum(weight, axis=1, keepdims=True))
            weight_refs[tile][part, :] = weight.astype(jnp.bfloat16)
        mix_ref[tile * STACK : (tile + 1) * STACK, :] = jnp.dot(
            weight_refs[tile][...], kv_ref[0 : counts[tile], 128:256], preferred_element_type=jnp.float32
        )


def attention_first(info, lengths, q, kv2, kv0):
    state = jax.ShapeDtypeStruct((4 * STACK, HEAD_DIM), jnp.float32)
    counts = [640 + HALF * tile for tile in range(4)]
    return pl.pallas_call(
        first_kernel,
        out_shape=[state] * 3,
        in_specs=[SM, SM] + [VM] * 3,
        out_specs=[VM] * 3,
        scratch_shapes=[pltpu.VMEM((1024, 256), jnp.bfloat16)]
        + [pltpu.VMEM((STACK, n), jnp.float32) for n in counts]
        + [pltpu.VMEM((STACK, n), jnp.bfloat16) for n in counts],
        compiler_params=params(32),
        cost_estimate=pl.CostEstimate(
            flops=4 * STACK * sum(counts) * HEAD_DIM,
            bytes_accessed=8 << 20,
            transcendentals=STACK * sum(counts),
        ),
        name="attention_first",
    )(info, lengths, q, kv2, kv0)


def last_kernel(tiles, info_ref, lengths_ref, q_ref, kv_ref, mix_ref, top_ref, sum_ref, *rest):
    n = len(tiles)
    outs, score_refs, weight_refs, scale_refs = rest[:n], rest[n : 2 * n], rest[2 * n : 3 * n], rest[3 * n :]
    for tile, score_ref in zip(tiles, score_refs):
        score(q_ref, tile, kv_ref[HALF * tile : 512, 0:128], score_ref)
    for tile, out_ref, score_ref, weight_ref, scale_ref in zip(tiles, outs, score_refs, weight_refs, scale_refs):
        mask = mask_of(info_ref, lengths_ref, tile, HALF * tile, 512 - HALF * tile)
        for h in range(GROUP):
            part = slice(h * HALF, (h + 1) * HALF)
            at = slice(tile * STACK + h * HALF, tile * STACK + (h + 1) * HALF)
            value = score_ref[part, :] * SCALE2 + mask
            old = top_ref[at, 0:1]
            top = jnp.maximum(jnp.max(value, axis=1, keepdims=True), old)
            weight = jnp.exp2(value - top)
            keep = jnp.exp2(old - top)
            total = jnp.sum(weight, axis=1, keepdims=True) + keep * sum_ref[at, 0:1]
            scale_ref[part, 0:128] = wide(keep)
            scale_ref[part, 128:256] = wide(total)
            weight_ref[part, :] = weight.astype(jnp.bfloat16)
        mixed = jnp.dot(
            weight_ref[...], kv_ref[HALF * tile : 512, 128:256], preferred_element_type=jnp.float32
        )
        before = mix_ref[tile * STACK : (tile + 1) * STACK, :]
        mixed = (mixed + before * scale_ref[:, 0:128]) / scale_ref[:, 128:256]
        for h in range(GROUP):
            out_ref[:, h * HEAD_DIM : (h + 1) * HEAD_DIM] = mixed[h * HALF : (h + 1) * HALF].astype(
                jnp.bfloat16
            )


def attention_last(tiles, info, lengths, q, kv4, state):
    n = len(tiles)
    counts = [512 - HALF * tile for tile in tiles]
    return pl.pallas_call(
        functools.partial(last_kernel, tiles),
        out_shape=[jax.ShapeDtypeStruct((HALF, QC), jnp.bfloat16)] * n,
        in_specs=[SM, SM] + [VM] * 5,
        out_specs=[VM] * n,
        scratch_shapes=[pltpu.VMEM((STACK, c), jnp.float32) for c in counts]
        + [pltpu.VMEM((STACK, c), jnp.bfloat16) for c in counts]
        + [pltpu.VMEM((STACK, 256), jnp.float32) for _ in counts],
        compiler_params=params(20),
        cost_estimate=pl.CostEstimate(
            flops=4 * STACK * sum(counts) * HEAD_DIM,
            bytes_accessed=4 << 20,
            transcendentals=STACK * sum(counts),
        ),
        name="attention_last",
    )(info, lengths, q, kv4, *state)


def body(hidden, norm_gain, qkv_weight, qkv_bias, repo_lengths):
    z = lax.axis_index("ctx")
    odd = z % 2
    y, x, core = lax.axis_index("y"), lax.axis_index("x"), lax.axis_index("core")

    k_at, v_at = 1792 + odd * 128, 2048 + odd * 128
    kv_own = jnp.concatenate(
        [
            lax.dynamic_slice(qkv_weight, (0, k_at), (WROWS, 128)),
            lax.dynamic_slice(qkv_weight, (0, v_at), (WROWS, 128)),
        ],
        1,
    )
    kv_own, qkv_weight = lax.optimization_barrier((kv_own, qkv_weight))
    q_own = lax.dynamic_slice(qkv_weight, (0, odd * QC), (WROWS, QC))
    q_bias = lax.dynamic_slice(qkv_bias, (odd * QC,), (QC,)).reshape(1, QC)
    kv_bias = jnp.concatenate(
        [lax.dynamic_slice(qkv_bias, (k_at,), (128,)), lax.dynamic_slice(qkv_bias, (v_at,), (128,))]
    ).reshape(1, 256)

    info = jnp.stack([y, x, core, z]).astype(jnp.int32)
    freq = rope_base ** (-jnp.arange(0, HEAD_DIM, 2, dtype=jnp.float32) / HEAD_DIM)
    freq = jnp.concatenate([freq, freq]).reshape(1, HEAD_DIM)

    kv_row = first_phase(kv_own)
    before = ring(hidden[TOK - HALF :], "ctx", 1)
    after = ring(hidden[:HALF], "ctx", -1)
    q_row = first_phase(q_own)
    normed, cosine, sine = prepare(info, repo_lengths, hidden, norm_gain, freq)

    kv_row, normed, cosine, sine = lax.optimization_barrier((kv_row, normed, cosine, sine))
    kv_near = [kv_row, hop(kv_row, 1, 1), hop(kv_row, 1, -1), hop(kv_row, 1, 2)]
    q_below, q_above = hop(q_row, 1, 1), hop(q_row, 1, -1)
    kv_far = [ring(piece, "core", 1) for piece in kv_near]
    tokens = join(before, normed, after, norm_gain)
    kv0 = project(kv_kernel, KV_CHUNKS, "kv_project", info, tokens, kv_near, kv_far, kv_bias, cosine, sine)
    kv2 = ring(kv0, "ctx", 2)

    q_row, q_below, q_above, _ = lax.optimization_barrier((q_row, q_below, q_above, kv0))
    half = q_row.shape[0] // 2
    q_near = [q_row, q_below, q_above, hop(q_below[:half], 1, 1), hop(q_above[half:], 1, -1)]
    q_far = [ring(piece, "core", 1) for piece in q_near]
    kv4 = ring(kv2, "ctx", 2)
    q = project(q_kernel, Q_CHUNKS, "q_project", info, tokens, q_near, q_far, q_bias, cosine, sine)

    state = attention_first(info, repo_lengths, q, kv2, kv0)
    args = (info, repo_lengths, q, kv4, state)
    back, ahead = attention_last((0, 3), *args)
    low = ring(ahead, "ctx", 1)
    high = ring(back, "ctx", -1)
    own = jnp.concatenate(attention_last((1, 2), *args), 0)
    other = jnp.concatenate([low, high], 0)
    return jnp.where(
        odd == 0, jnp.concatenate([own, other], 1), jnp.concatenate([other, own], 1)
    )


def solution(mesh):
    fine = Mesh(mesh.devices.reshape(4, 4, 2, 8), ("y", "x", "core", "ctx"))
    grp = ("y", "x", "core")
    tokens = P(("y", "x", "core", "ctx"), None)
    in_specs = (tokens, P(), P(grp, None), P(), P(grp, None))
    return jax.shard_map(body, mesh=fine, in_specs=in_specs, out_specs=tokens, check_vma=False)
```

time: 203 us -> 98.6 us (0.49)
  waiting for transfers between devices: 122 us -> 27.4 us
  matrix products: 37.5 us -> 0 us
  starting transfers between devices: 0.26 us -> 30.2 us
  Pallas kernels: 0 us -> 28.6 us
  other arithmetic: 22.6 us -> 1.43 us
  between operations: 13.2 us -> 0.27 us
  local copies, waits for them, and re-layouts: 7.21 us -> 10.3 us
    all_gather x3 -> x0, waiting for transfers between devices: 121 us -> none  [the longest x1 78.1 us: body(): lax.all_gather(qkv_weight, 'grp', axis=0, tiled=True)]
    dot_general x3 -> x0, matrix products: 37.5 us -> none  [the longest x1 13.5 us: body(): jnp.einsum('rgho,kgo->ghrk', queries, key_heads, preferred_element_type=j...]
    ppermute x0 -> x28, starting transfers between devices: none -> 30.2 us  [the longest x13 19.8 us: hop(): return lax.ppermute(value, ('y', 'x', 'core'), pairs)]
    pallas_call x0 -> x7, Pallas kernels: none -> 28.6 us  [the longest x2 8.71 us: project(): pl.pallas_call(functools.partial(kernel, count), out_shape=jax.ShapeDtype...]
    ppermute x0 -> x28, waiting for transfers between devices: none -> 27.4 us  [the longest x13 15.3 us: hop(): return lax.ppermute(value, ('y', 'x', 'core'), pairs)]
    reduce_sum x3 -> x0, other arithmetic: 16.2 us -> none  [the longest x1 13.5 us: body(): new_total = jnp.sum(weights, axis=-1)]
    slice x0 -> x3, local copies, waits for them, and re-layouts: none -> 4.88 us  [the longest x1 2.82 us: body(): after = ring(hidden[:HALF], 'ctx', -1)]
    reshape x3 -> x2, local copies, waits for them, and re-layouts: 3.76 us -> 0.02 us  [the longest x1 0.01 us: prepare(): gain.reshape(1, D)]
  transfers between devices with their start and end apart: 3 -> 28, of which waited for: 3 -> 9; matrix products, arithmetic and copies ran while one was open for 19% -> 8% of each run, Pallas kernels for 0% -> 24%
where the time goes in v2:
time: 98.6 us; the launch traced here: 98.2 us
  starting transfers between devices  30.2 us (31%)
  Pallas kernels  28.6 us (29%)
  waiting for transfers between devices  27.4 us (28%)
  local copies, waits for them, and re-layouts  10.3 us (10%)
  other arithmetic  1.43 us (1%)
    ppermute x13, starting transfers between devices, hop(): return lax.ppermute(value, ('y', 'x', 'core'), pairs)  19.8 us
    ppermute x13, waiting for transfers between devices, hop(): return lax.ppermute(value, ('y', 'x', 'core'), pairs)  15.3 us
    ppermute x15, waiting for transfers between devices, ring(): return lax.ppermute(value, axis, [(i, (i + step) % n) for i in range(n)])  12.1 us
    ppermute x15, starting transfers between devices, ring(): return lax.ppermute(value, axis, [(i, (i + step) % n) for i in range(n)])  10.4 us
    pallas_call x2, Pallas kernels, project(): pl.pallas_call(functools.partial(kernel, count), out_shape=jax.ShapeDtype...  8.71 us
    pallas_call x2, Pallas kernels, attention_last(): pl.pallas_call(functools.partial(last_kernel, tiles), out_shape=[jax.Shap...  8.06 us
    pallas_call x1, Pallas kernels, attention_first(): pl.pallas_call(first_kernel, out_shape=[state] * 3, in_specs=[SM, SM] + [...  6.17 us
    pallas_call x1, Pallas kernels, prepare(): pl.pallas_call(prepare_kernel, out_shape=[jax.ShapeDtypeStruct((TOK, D),...  3.09 us
  transfers between devices with their start and end apart: 28, of which 9 were waited for; matrix products, arithmetic and copies ran while one was open for 8% of the time, Pallas kernels for 24%

profile of v2, /device:TPU:6, one launch (start us, length us, event | category | flops | bytes accessed | tf_op | source)
XLA Modules:
  0.0 98.2 jit_solution(15008910292311142257)
XLA Ops:
  0.0 0.8 constant_dynamic-slice_fusion.2
  0.8 2.3 %collective-permute-start.1 = (bf16[112,256]{1,0:T(8,128)(2,1)S(1)}, bf16[112,256]{1,0:T(8,128)(2,1)S(1)}, u32[]{:S(2)}, u32[]{:S(2)}) collective-permute-start(bf16[112,256]{1,0:T(8,128)(2,1)S(1)} %pad_maximum_fusion.2), channel_id=1, source_target_pairs={{0,16},{8,72},{16,32},{24,88},{32,48},{40,104},{48,0},{56,120},{64... | collective-permute-start | bytes 172040 | tf_op jit(solution)/shard_map/ppermute | solution.py:51
  3.1 1.6 %collective-permute-start.3 = (bf16[112,256]{1,0:T(8,128)(2,1)S(1)}, bf16[112,256]{1,0:T(8,128)(2,1)S(1)}, u32[]{:S(2)}, u32[]{:S(2)}) collective-permute-start(bf16[112,256]{1,0:T(8,128)(2,1)S(1)} %pad_maximum_fusion.2), channel_id=1, source_target_pairs={{0,32},{8,136},{16,48},{24,152},{32,0},{40,168},{48,16},{56,184},{... | collective-permute-start | bytes 172040 | tf_op jit(solution)/shard_map/ppermute | solution.py:51
  4.7 2.8 %fusion = (bf16[128,3584]{1,0:T(8,128)(2,1)}, bf16[128,3584]{1,0:T(8,128)(2,1)}) fusion(bf16[256,3584]{1,0:T(8,128)(2,1)} %hidden_ref.1), kind=kLoop, calls=%fused_computation.15 | loop fusion | bytes 3670016 | tf_op jit(solution)/shard_map/slice | solution.py:339
  7.5 1.6 %collective-permute-start = (bf16[128,3584]{1,0:T(8,128)(2,1)}, bf16[128,3584]{1,0:T(8,128)(2,1)S(1)}, u32[]{:S(2)}, u32[]{:S(2)}) collective-permute-start(bf16[128,3584]{1,0:T(8,128)(2,1)} %get-tuple-element.44), channel_id=1, source_target_pairs={{0,1},{1,2},{2,3},{3,4},{4,5},{5,6},{6,7},{7,0},{8,9},{9,10},{10,1... | collective-permute-start | bytes 2752520 | tf_op jit(solution)/shard_map/ppermute | solution.py:41
  9.1 3.9 %collective-permute-start.4 = (bf16[128,3584]{1,0:T(8,128)(2,1)}, bf16[128,3584]{1,0:T(8,128)(2,1)}, u32[]{:S(2)}, u32[]{:S(2)}) collective-permute-start(bf16[128,3584]{1,0:T(8,128)(2,1)} %get-tuple-element.43), channel_id=1, source_target_pairs={{0,7},{1,0},{2,1},{3,2},{4,3},{5,4},{6,5},{7,6},{8,15},{9,8},{10,9... | collective-permute-start | bytes 2752520 | tf_op jit(solution)/shard_map/ppermute | solution.py:41
  13.0 1.0 constant_dynamic-slice_fusion
  14.0 0.1 maximum_bitcast_fusion.freq_ref
  14.1 2.1 %collective-permute-start.5 = (bf16[112,896]{1,0:T(8,128)(2,1)S(1)}, bf16[112,896]{1,0:T(8,128)(2,1)S(1)}, u32[]{:S(2)}, u32[]{:S(2)}) collective-permute-start(bf16[112,896]{1,0:T(8,128)(2,1)S(1)} %constant_dynamic-slice_fusion), channel_id=1, source_target_pairs={{0,16},{8,72},{16,32},{24,88},{32,48},{40,104},{48,0},{56,120},{64... | collective-permute-start | bytes 602120 | tf_op jit(solution)/shard_map/ppermute | solution.py:51
  16.2 0.1 pad_add_fusion.info_ref
  16.3 3.1 %prepare.1 = (bf16[256,3584]{1,0:T(8,128)(2,1)S(1)}, f32[512,128]{1,0:T(8,128)S(1)}, f32[512,128]{1,0:T(8,128)S(1)}) custom-call(s32[4]{0:T(128)S(1)} %pad_add_fusion.info_ref, s32[1,6]{1,0:T(1,128)S(1)} %copy-done.3, bf16[256,3584]{1,0:T(8,128)(2,1)S(1)} %copy-done.2, f32[1,3584]{1,0:T(1,128)S(1)} %reshape.13.gain_ref, ...), custom_call_target="tpu_custom_call" | custom-call | flops 7340032 | bytes 3670016 | tf_op jit(solution)/shard_map/prepare/pallas_call | solution.py:110
  19.4 0.1 collective-permute-start.6
  19.5 2.0 %collective-permute-start.7 = (bf16[112,896]{1,0:T(8,128)(2,1)S(1)}, bf16[112,896]{1,0:T(8,128)(2,1)S(1)}, u32[]{:S(2)}, u32[]{:S(2)}) collective-permute-start(bf16[112,896]{1,0:T(8,128)(2,1)S(1)} %constant_dynamic-slice_fusion), channel_id=1, source_target_pairs={{0,32},{8,136},{16,48},{24,152},{32,0},{40,168},{48,16},{56,184},{... | collective-permute-start | bytes 602120 | tf_op jit(solution)/shard_map/ppermute | solution.py:51
  21.6 1.7 %collective-permute-start.10 = (bf16[448,256]{1,0:T(8,128)(2,1)S(1)}, bf16[448,256]{1,0:T(8,128)(2,1)S(1)}, u32[]{:S(2)}, u32[]{:S(2)}) collective-permute-start(bf16[448,256]{1,0:T(8,128)(2,1)S(1)} %pad_maximum_fusion.1.rest_0_), channel_id=1, source_target_pairs={{0,64},{8,24},{16,80},{24,40},{32,96},{40,56},{48,112},{56,8},{64,... | collective-permute-start | bytes 688136 | tf_op jit(solution)/shard_map/ppermute | solution.py:51
  23.2 5.3 %collective-permute-done.6 = bf16[112,896]{1,0:T(8,128)(2,1)S(1)} collective-permute-done((bf16[112,896]{1,0:T(8,128)(2,1)S(1)}, bf16[112,896]{1,0:T(8,128)(2,1)S(1)}, u32[]{:S(2)}, u32[]{:S(2)}) %collective-permute-start.6) | collective-permute-done | bytes 200736 | tf_op jit(solution)/shard_map/ppermute | solution.py:51
  28.5 3.0 %collective-permute-start.11 = (bf16[448,256]{1,0:T(8,128)(2,1)S(1)}, bf16[448,256]{1,0:T(8,128)(2,1)S(1)}, u32[]{:S(2)}, u32[]{:S(2)}) collective-permute-start(bf16[448,256]{1,0:T(8,128)(2,1)S(1)} %pad_maximum_fusion.1.rest_0_), channel_id=1, source_target_pairs={{0,192},{8,56},{16,208},{24,8},{32,224},{40,24},{48,240},{56,40},{... | collective-permute-start | bytes 688136 | tf_op jit(solution)/shard_map/ppermute | solution.py:51
  31.6 1.5 %collective-permute-start.12 = (bf16[448,256]{1,0:T(8,128)(2,1)S(1)}, bf16[448,256]{1,0:T(8,128)(2,1)S(1)}, u32[]{:S(2)}, u32[]{:S(2)}) collective-permute-start(bf16[448,256]{1,0:T(8,128)(2,1)S(1)} %pad_maximum_fusion.1.rest_0_), channel_id=1, source_target_pairs={{0,128},{8,40},{16,144},{24,56},{32,160},{40,8},{48,176},{56,24},{... | collective-permute-start | bytes 688136 | tf_op jit(solution)/shard_map/ppermute | solution.py:51
  33.1 4.5 %collective-permute-done.11.rest_2_ = bf16[448,256]{1,0:T(8,128)(2,1)S(1)} collective-permute-done((bf16[448,256]{1,0:T(8,128)(2,1)S(1)}, bf16[448,256]{1,0:T(8,128)(2,1)S(1)}, u32[]{:S(2)}, u32[]{:S(2)}) %collective-permute-start.11) | collective-permute-done | bytes 229408 | tf_op jit(solution)/shard_map/ppermute | solution.py:51
  37.6 1.5 %collective-permute-done.12.rest_3_ = bf16[448,256]{1,0:T(8,128)(2,1)S(1)} collective-permute-done((bf16[448,256]{1,0:T(8,128)(2,1)S(1)}, bf16[448,256]{1,0:T(8,128)(2,1)S(1)}, u32[]{:S(2)}, u32[]{:S(2)}) %collective-permute-start.12) | collective-permute-done | bytes 229408 | tf_op jit(solution)/shard_map/ppermute | solution.py:51
  39.1 2.2 %collective-permute-start.9 = (bf16[448,896]{1,0:T(8,128)(2,1)S(1)}, bf16[448,896]{1,0:T(8,128)(2,1)}, u32[]{:S(2)}, u32[]{:S(2)}) collective-permute-start(bf16[448,896]{1,0:T(8,128)(2,1)S(1)} %pad_maximum_fusion.rest_0_), channel_id=1, source_target_pairs={{0,192},{8,56},{16,208},{24,8},{32,224},{40,24},{48,240},{56,40},{... | collective-permute-start | bytes 2408456 | tf_op jit(solution)/shard_map/ppermute | solution.py:51
  41.3 0.5 collective-permute-start.15
  41.8 0.3 collective-permute-start.16
  42.0 0.8 fusion.1
  42.8 2.6 %join.1.x_ref = bf16[512,3584]{1,0:T(8,128)(2,1)S(1)} custom-call(bf16[128,3584]{1,0:T(8,128)(2,1)S(1)} %collective-permute-done.before_ref, bf16[256,3584]{1,0:T(8,128)(2,1)S(1)} %get-tuple-element.28.own_ref, bf16[128,3584]{1,0:T(8,128)(2,1)} %collective-permute-done.4.after_ref, f32[1,3584]{1,0:T(1,128)S(1)} %reshape.13.gain_ref), custom_call_target="tpu_custom_call" | custom-call | flops 7340032 | bytes 7340032 | tf_op jit(solution)/shard_map/join/pallas_call | solution.py:131
  45.5 2.0 %kv_project.1.kv0_ref = bf16[512,256]{1,0:T(8,128)(2,1)S(1)} custom-call(s32[4]{0:T(128)S(1)} %pad_add_fusion.info_ref, bf16[512,3584]{1,0:T(8,128)(2,1)S(1)} %join.1.x_ref, f32[1,256]{1,0:T(1,128)S(1)} %bitcast.7, f32[512,128]{1,0:T(8,128)S(1)} %get-tuple-element.29.cos_ref, f32[512,128]{1,0:T(8,128)S(1)} %get-tuple-element.30.sin_ref, ...), custom_call_target="tpu_custom_call" | custom-call | flops 939524096 | bytes 5505024 | tf_op jit(solution)/shard_map/kv_project/pallas_call | solution.py:175
  47.5 0.1 collective-permute-start.24
  47.5 3.9 %collective-permute-done.8.rest_1_ = bf16[448,896]{1,0:T(8,128)(2,1)} collective-permute-done((bf16[448,896]{1,0:T(8,128)(2,1)S(1)}, bf16[448,896]{1,0:T(8,128)(2,1)}, u32[]{:S(2)}, u32[]{:S(2)}) %collective-permute-start.8) | collective-permute-done | bytes 802848 | tf_op jit(solution)/shard_map/ppermute | solution.py:51
  51.5 1.0 %slice.14 = bf16[224,896]{1,0:T(8,128)(2,1)S(1)} slice(bf16[448,896]{1,0:T(8,128)(2,1)} %collective-permute-done.8.rest_1_), slice={[0:224], [0:896]} | slice | bytes 802816 | tf_op jit(solution)/shard_map/slice | solution.py:353
  52.5 0.1 collective-permute-start.20
  52.6 1.5 %collective-permute-start.17 = (bf16[224,896]{1,0:T(8,128)(2,1)S(1)}, bf16[224,896]{1,0:T(8,128)(2,1)}, u32[]{:S(2)}, u32[]{:S(2)}) collective-permute-start(bf16[224,896]{1,0:T(8,128)(2,1)S(1)} %slice.14), channel_id=1, source_target_pairs={{0,64},{8,24},{16,80},{24,40},{32,96},{40,56},{48,112},{56,8},{64,... | collective-permute-start | bytes 1204232 | tf_op jit(solution)/shard_map/ppermute | solution.py:51
  54.1 1.0 %slice.15 = bf16[224,896]{1,0:T(8,128)(2,1)S(1)} slice(bf16[448,896]{1,0:T(8,128)(2,1)} %collective-permute-done.9.rest_2_), slice={[224:448], [0:896]} | slice | bytes 802816 | tf_op jit(solution)/shard_map/slice | solution.py:353
  55.2 1.9 %collective-permute-start.18 = (bf16[224,896]{1,0:T(8,128)(2,1)S(1)}, bf16[224,896]{1,0:T(8,128)(2,1)}, u32[]{:S(2)}, u32[]{:S(2)}) collective-permute-start(bf16[224,896]{1,0:T(8,128)(2,1)S(1)} %slice.15), channel_id=1, source_target_pairs={{0,192},{8,56},{16,208},{24,8},{32,224},{40,24},{48,240},{56,40},{... | collective-permute-start | bytes 1204232 | tf_op jit(solution)/shard_map/ppermute | solution.py:51
  57.1 6.7 %collective-permute-done.24.kv2_ref = bf16[512,256]{1,0:T(8,128)(2,1)} collective-permute-done((bf16[512,256]{1,0:T(8,128)(2,1)S(1)}, bf16[512,256]{1,0:T(8,128)(2,1)}, u32[]{:S(2)}, u32[]{:S(2)}) %collective-permute-start.24) | collective-permute-done | bytes 262176 | tf_op jit(solution)/shard_map/ppermute | solution.py:41
  63.8 0.5 collective-permute-start.22
  64.3 0.1 collective-permute-start.23
  64.4 0.8 dynamic_slice.20
  65.2 1.8 %collective-permute-done.22.rest_8_ = bf16[224,896]{1,0:T(8,128)(2,1)} collective-permute-done((bf16[224,896]{1,0:T(8,128)(2,1)}, bf16[224,896]{1,0:T(8,128)(2,1)}, u32[]{:S(2)}, u32[]{:S(2)}) %collective-permute-start.22) | collective-permute-done | bytes 401440 | tf_op jit(solution)/shard_map/ppermute | solution.py:41
  67.0 0.6 collective-permute-done.23.rest_9_
  67.6 2.0 %copy-done.1 = bf16[512,3584]{1,0:T(8,128)(2,1)S(1)} copy-done((bf16[512,3584]{1,0:T(8,128)(2,1)S(1)}, bf16[512,3584]{1,0:T(8,128)(2,1)}, u32[]{:S(2)}) %copy-start.1) | copy-done | bytes 3670040
  69.7 6.7 %q_project.1.q_ref = bf16[512,896]{1,0:T(8,128)(2,1)S(1)} custom-call(s32[4]{0:T(128)S(1)} %pad_add_fusion.info_ref, bf16[512,3584]{1,0:T(8,128)(2,1)S(1)} %copy-done.1, f32[1,896]{1,0:T(1,128)S(1)} %reshape.15.bias_ref, f32[512,128]{1,0:T(8,128)S(1)} %get-tuple-element.29.cos_ref, f32[512,128]{1,0:T(8,128)S(1)} %get-tuple-element.30.sin_ref, ...), custom_call_target="tpu_custom_call" | custom-call | flops 3288334336 | bytes 10092544 | tf_op jit(solution)/shard_map/q_project/pallas_call | solution.py:175
  76.4 6.2 %attention_first.1 = (f32[3584,128]{1,0:T(8,128)S(1)}, f32[3584,128]{1,0:T(8,128)S(1)}, f32[3584,128]{1,0:T(8,128)S(1)}) custom-call(s32[4]{0:T(128)S(1)} %pad_add_fusion.info_ref, s32[1,6]{1,0:T(1,128)S(1)} %copy-done.3, bf16[512,896]{1,0:T(8,128)(2,1)S(1)} %q_project.1.q_ref, bf16[512,256]{1,0:T(8,128)(2,1)} %collective-permute-done.24.kv2_ref, ...), custom_call_target="tpu_custom_call" | custom-call | flops 1526726656 | bytes 8388608 | tf_op jit(solution)/shard_map/attention_first/pallas_call | solution.py:244
  82.6 4.7 %attention_last.3 = (bf16[128,896]{1,0:T(8,128)(2,1)S(1)}, bf16[128,896]{1,0:T(8,128)(2,1)S(1)}) custom-call(s32[4]{0:T(128)S(1)} %pad_add_fusion.info_ref, s32[1,6]{1,0:T(1,128)S(1)} %copy-done.3, bf16[512,896]{1,0:T(8,128)(2,1)S(1)} %q_project.1.q_ref, bf16[512,256]{1,0:T(8,128)(2,1)S(1)} %collective-permute-done.25.kv_ref, ...), custom_call_target="tpu_custom_call" | custom-call | flops 293601280 | bytes 4194304 | tf_op jit(solution)/shard_map/attention_last/pallas_call | solution.py:295
  87.3 0.1 collective-permute-start.26
  87.4 3.2 %collective-permute-start.27 = (bf16[128,896]{1,0:T(8,128)(2,1)S(1)}, bf16[128,896]{1,0:T(8,128)(2,1)S(1)}, u32[]{:S(2)}, u32[]{:S(2)}) collective-permute-start(bf16[128,896]{1,0:T(8,128)(2,1)S(1)} %get-tuple-element.42), channel_id=1, source_target_pairs={{0,7},{1,0},{2,1},{3,2},{4,3},{5,4},{6,5},{7,6},{8,15},{9,8},{10,9... | collective-permute-start | bytes 688136 | tf_op jit(solution)/shard_map/ppermute | solution.py:41
  90.7 3.3 %attention_last.2 = (bf16[128,896]{1,0:T(8,128)(2,1)S(1)}, bf16[128,896]{1,0:T(8,128)(2,1)S(1)}) custom-call(s32[4]{0:T(128)S(1)} %pad_add_fusion.info_ref, s32[1,6]{1,0:T(1,128)S(1)} %copy-done.3, bf16[512,896]{1,0:T(8,128)(2,1)S(1)} %q_project.1.q_ref, bf16[512,256]{1,0:T(8,128)(2,1)S(1)} %collective-permute-done.25.kv_ref, ...), custom_call_target="tpu_custom_call" | custom-call | flops 293601280 | bytes 4194304 | tf_op jit(solution)/shard_map/attention_last/pallas_call | solution.py:295
  94.0 2.2 %collective-permute-done.26 = bf16[128,896]{1,0:T(8,128)(2,1)S(1)} collective-permute-done((bf16[128,896]{1,0:T(8,128)(2,1)S(1)}, bf16[128,896]{1,0:T(8,128)(2,1)S(1)}, u32[]{:S(2)}, u32[]{:S(2)}) %collective-permute-start.26) | collective-permute-done | bytes 229408 | tf_op jit(solution)/shard_map/ppermute | solution.py:41
  96.3 0.7 collective-permute-done.27
  97.0 1.2 %maximum_select_fusion = bf16[256,1792]{1,0:T(8,128)(2,1)} fusion(bf16[256,896]{1,0:T(8,128)(2,1)S(1)} %constant_dynamic-update-slice_fusion.2, bf16[256,896]{1,0:T(8,128)(2,1)S(1)} %constant_dynamic-update-slice_fusion, pred[]{:T(512)S(6)} %eq.5), kind=kLoop, calls=%fused_computation | loop fusion | flops 4128768 | bytes 1835009 | tf_op jit(solution)/shard_map/jit(_where)/select_n | solution.py:365
  (46 shorter events, 0.3 us)
Async XLA Ops:
  0.8 12.2 %copy-start.4 = (f32[3584]{0:T(1024)S(1)}, f32[3584]{0:T(1024)}, u32[]{:S(2)}) copy-start(f32[3584]{0:T(1024)} %param.6) | copy-start | bytes 43012
  0.8 15.5 %copy-start.2 = (bf16[256,3584]{1,0:T(8,128)(2,1)S(1)}, bf16[256,3584]{1,0:T(8,128)(2,1)}, u32[]{:S(2)}) copy-start(bf16[256,3584]{1,0:T(8,128)(2,1)} %hidden_ref.1) | copy-start | bytes 5505028
  0.8 15.5 %copy-start.3 = (s32[1,6]{1,0:T(1,128)S(1)}, s32[1,6]{1,0:T(1,128)}, u32[]{:S(2)}) copy-start(s32[1,6]{1,0:T(1,128)} %lengths_ref.7) | copy-start | bytes 76
  0.8 13.3 %collective-permute-start.1 = (bf16[112,256]{1,0:T(8,128)(2,1)S(1)}, bf16[112,256]{1,0:T(8,128)(2,1)S(1)}, u32[]{:S(2)}, u32[]{:S(2)}) collective-permute-start(bf16[112,256]{1,0:T(8,128)(2,1)S(1)} %pad_maximum_fusion.2), channel_id=1, source_target_pairs={{0,16},{8,72},{16,32},{24,88},{32,48},{40,104},{48,0},{56,120},{64... | collective-permute-start | bytes 172040 | tf_op jit(solution)/shard_map/ppermute | solution.py:51
  3.1 16.3 %collective-permute-start.2 = (bf16[112,256]{1,0:T(8,128)(2,1)S(1)}, bf16[112,256]{1,0:T(8,128)(2,1)S(1)}, u32[]{:S(2)}, u32[]{:S(2)}) collective-permute-start(bf16[112,256]{1,0:T(8,128)(2,1)S(1)} %pad_maximum_fusion.2), channel_id=1, source_target_pairs={{0,48},{8,200},{16,0},{24,216},{32,16},{40,232},{48,32},{56,248},{... | collective-permute-start | bytes 172040 | tf_op jit(solution)/shard_map/ppermute | solution.py:51
  3.1 16.4 %collective-permute-start.3 = (bf16[112,256]{1,0:T(8,128)(2,1)S(1)}, bf16[112,256]{1,0:T(8,128)(2,1)S(1)}, u32[]{:S(2)}, u32[]{:S(2)}) collective-permute-start(bf16[112,256]{1,0:T(8,128)(2,1)S(1)} %pad_maximum_fusion.2), channel_id=1, source_target_pairs={{0,32},{8,136},{16,48},{24,152},{32,0},{40,168},{48,16},{56,184},{... | collective-permute-start | bytes 172040 | tf_op jit(solution)/shard_map/ppermute | solution.py:51
  7.5 33.8 %collective-permute-start = (bf16[128,3584]{1,0:T(8,128)(2,1)}, bf16[128,3584]{1,0:T(8,128)(2,1)S(1)}, u32[]{:S(2)}, u32[]{:S(2)}) collective-permute-start(bf16[128,3584]{1,0:T(8,128)(2,1)} %get-tuple-element.44), channel_id=1, source_target_pairs={{0,1},{1,2},{2,3},{3,4},{4,5},{5,6},{6,7},{7,0},{8,9},{9,10},{10,1... | collective-permute-start | bytes 2752520 | tf_op jit(solution)/shard_map/ppermute | solution.py:41
  9.1 32.7 %collective-permute-start.4 = (bf16[128,3584]{1,0:T(8,128)(2,1)}, bf16[128,3584]{1,0:T(8,128)(2,1)}, u32[]{:S(2)}, u32[]{:S(2)}) collective-permute-start(bf16[128,3584]{1,0:T(8,128)(2,1)} %get-tuple-element.43), channel_id=1, source_target_pairs={{0,7},{1,0},{2,1},{3,2},{4,3},{5,4},{6,5},{7,6},{8,15},{9,8},{10,9... | collective-permute-start | bytes 2752520 | tf_op jit(solution)/shard_map/ppermute | solution.py:41
  14.1 7.5 %collective-permute-start.5 = (bf16[112,896]{1,0:T(8,128)(2,1)S(1)}, bf16[112,896]{1,0:T(8,128)(2,1)S(1)}, u32[]{:S(2)}, u32[]{:S(2)}) collective-permute-start(bf16[112,896]{1,0:T(8,128)(2,1)S(1)} %constant_dynamic-slice_fusion), channel_id=1, source_target_pairs={{0,16},{8,72},{16,32},{24,88},{32,48},{40,104},{48,0},{56,120},{64... | collective-permute-start | bytes 602120 | tf_op jit(solution)/shard_map/ppermute | solution.py:51
  19.4 9.2 %collective-permute-start.6 = (bf16[112,896]{1,0:T(8,128)(2,1)S(1)}, bf16[112,896]{1,0:T(8,128)(2,1)S(1)}, u32[]{:S(2)}, u32[]{:S(2)}) collective-permute-start(bf16[112,896]{1,0:T(8,128)(2,1)S(1)} %constant_dynamic-slice_fusion), channel_id=1, source_target_pairs={{0,48},{8,200},{16,0},{24,216},{32,16},{40,232},{48,32},{56,248},{... | collective-permute-start | bytes 602120 | tf_op jit(solution)/shard_map/ppermute | solution.py:51
  19.5 12.1 %collective-permute-start.7 = (bf16[112,896]{1,0:T(8,128)(2,1)S(1)}, bf16[112,896]{1,0:T(8,128)(2,1)S(1)}, u32[]{:S(2)}, u32[]{:S(2)}) collective-permute-start(bf16[112,896]{1,0:T(8,128)(2,1)S(1)} %constant_dynamic-slice_fusion), channel_id=1, source_target_pairs={{0,32},{8,136},{16,48},{24,152},{32,0},{40,168},{48,16},{56,184},{... | collective-permute-start | bytes 602120 | tf_op jit(solution)/shard_map/ppermute | solution.py:51
  21.6 11.5 %collective-permute-start.10 = (bf16[448,256]{1,0:T(8,128)(2,1)S(1)}, bf16[448,256]{1,0:T(8,128)(2,1)S(1)}, u32[]{:S(2)}, u32[]{:S(2)}) collective-permute-start(bf16[448,256]{1,0:T(8,128)(2,1)S(1)} %pad_maximum_fusion.1.rest_0_), channel_id=1, source_target_pairs={{0,64},{8,24},{16,80},{24,40},{32,96},{40,56},{48,112},{56,8},{64,... | collective-permute-start | bytes 688136 | tf_op jit(solution)/shard_map/ppermute | solution.py:51
  28.5 9.0 %collective-permute-start.11 = (bf16[448,256]{1,0:T(8,128)(2,1)S(1)}, bf16[448,256]{1,0:T(8,128)(2,1)S(1)}, u32[]{:S(2)}, u32[]{:S(2)}) collective-permute-start(bf16[448,256]{1,0:T(8,128)(2,1)S(1)} %pad_maximum_fusion.1.rest_0_), channel_id=1, source_target_pairs={{0,192},{8,56},{16,208},{24,8},{32,224},{40,24},{48,240},{56,40},{... | collective-permute-start | bytes 688136 | tf_op jit(solution)/shard_map/ppermute | solution.py:51
  31.6 7.5 %collective-permute-start.12 = (bf16[448,256]{1,0:T(8,128)(2,1)S(1)}, bf16[448,256]{1,0:T(8,128)(2,1)S(1)}, u32[]{:S(2)}, u32[]{:S(2)}) collective-permute-start(bf16[448,256]{1,0:T(8,128)(2,1)S(1)} %pad_maximum_fusion.1.rest_0_), channel_id=1, source_target_pairs={{0,128},{8,40},{16,144},{24,56},{32,160},{40,8},{48,176},{56,24},{... | collective-permute-start | bytes 688136 | tf_op jit(solution)/shard_map/ppermute | solution.py:51
  33.0 8.2 %collective-permute-start.13 = (bf16[448,256]{1,0:T(8,128)(2,1)S(1)}, bf16[448,256]{1,0:T(8,128)(2,1)S(1)}, u32[]{:S(2)}, u32[]{:S(2)}) collective-permute-start(bf16[448,256]{1,0:T(8,128)(2,1)S(1)} %pad_maximum_fusion.1.rest_0_), channel_id=1, source_target_pairs={{0,8},{8,0},{1,9},{9,1},{2,10},{10,2},{3,11},{11,3},{4,12},{12,4},... | collective-permute-start | bytes 688136 | tf_op jit(solution)/shard_map/ppermute | solution.py:41
  37.6 13.9 %collective-permute-start.8 = (bf16[448,896]{1,0:T(8,128)(2,1)S(1)}, bf16[448,896]{1,0:T(8,128)(2,1)}, u32[]{:S(2)}, u32[]{:S(2)}) collective-permute-start(bf16[448,896]{1,0:T(8,128)(2,1)S(1)} %pad_maximum_fusion.rest_0_), channel_id=1, source_target_pairs={{0,64},{8,24},{16,80},{24,40},{32,96},{40,56},{48,112},{56,8},{64,... | collective-permute-start | bytes 2408456 | tf_op jit(solution)/shard_map/ppermute | solution.py:51
  39.1 12.4 %collective-permute-start.9 = (bf16[448,896]{1,0:T(8,128)(2,1)S(1)}, bf16[448,896]{1,0:T(8,128)(2,1)}, u32[]{:S(2)}, u32[]{:S(2)}) collective-permute-start(bf16[448,896]{1,0:T(8,128)(2,1)S(1)} %pad_maximum_fusion.rest_0_), channel_id=1, source_target_pairs={{0,192},{8,56},{16,208},{24,8},{32,224},{40,24},{48,240},{56,40},{... | collective-permute-start | bytes 2408456 | tf_op jit(solution)/shard_map/ppermute | solution.py:51
  41.3 4.2 %collective-permute-start.14 = (bf16[448,256]{1,0:T(8,128)(2,1)S(1)}, bf16[448,256]{1,0:T(8,128)(2,1)S(1)}, u32[]{:S(2)}, u32[]{:S(2)}) collective-permute-start(bf16[448,256]{1,0:T(8,128)(2,1)S(1)} %collective-permute-done.10.rest_1_), channel_id=1, source_target_pairs={{0,8},{8,0},{1,9},{9,1},{2,10},{10,2},{3,11},{11,3},{4,12},{12,4},... | collective-permute-start | bytes 688136 | tf_op jit(solution)/shard_map/ppermute | solution.py:41
  41.3 4.2 %collective-permute-start.15 = (bf16[448,256]{1,0:T(8,128)(2,1)S(1)}, bf16[448,256]{1,0:T(8,128)(2,1)S(1)}, u32[]{:S(2)}, u32[]{:S(2)}) collective-permute-start(bf16[448,256]{1,0:T(8,128)(2,1)S(1)} %collective-permute-done.11.rest_2_), channel_id=1, source_target_pairs={{0,8},{8,0},{1,9},{9,1},{2,10},{10,2},{3,11},{11,3},{4,12},{12,4},... | collective-permute-start | bytes 688136 | tf_op jit(solution)/shard_map/ppermute | solution.py:41
  41.8 3.7 %collective-permute-start.16 = (bf16[448,256]{1,0:T(8,128)(2,1)S(1)}, bf16[448,256]{1,0:T(8,128)(2,1)S(1)}, u32[]{:S(2)}, u32[]{:S(2)}) collective-permute-start(bf16[448,256]{1,0:T(8,128)(2,1)S(1)} %collective-permute-done.12.rest_3_), channel_id=1, source_target_pairs={{0,8},{8,0},{1,9},{9,1},{2,10},{10,2},{3,11},{11,3},{4,12},{12,4},... | collective-permute-start | bytes 688136 | tf_op jit(solution)/shard_map/ppermute | solution.py:41
  45.4 2.0 %copy-start = (bf16[512,3584]{1,0:T(8,128)(2,1)}, bf16[512,3584]{1,0:T(8,128)(2,1)S(1)}, u32[]{:S(2)}) copy-start(bf16[512,3584]{1,0:T(8,128)(2,1)S(1)} %join.1.x_ref) | copy-start | bytes 11010052
  47.5 16.4 %collective-permute-start.24 = (bf16[512,256]{1,0:T(8,128)(2,1)S(1)}, bf16[512,256]{1,0:T(8,128)(2,1)}, u32[]{:S(2)}, u32[]{:S(2)}) collective-permute-start(bf16[512,256]{1,0:T(8,128)(2,1)S(1)} %kv_project.1.kv0_ref), channel_id=1, source_target_pairs={{0,2},{1,3},{2,4},{3,5},{4,6},{5,7},{6,0},{7,1},{8,10},{9,11},{10,... | collective-permute-start | bytes 786440 | tf_op jit(solution)/shard_map/ppermute | solution.py:41
  52.5 15.1 %collective-permute-start.20 = (bf16[448,896]{1,0:T(8,128)(2,1)}, bf16[448,896]{1,0:T(8,128)(2,1)S(1)}, u32[]{:S(2)}, u32[]{:S(2)}) collective-permute-start(bf16[448,896]{1,0:T(8,128)(2,1)} %collective-permute-done.8.rest_1_), channel_id=1, source_target_pairs={{0,8},{8,0},{1,9},{9,1},{2,10},{10,2},{3,11},{11,3},{4,12},{12,4},... | collective-permute-start | bytes 2408456 | tf_op jit(solution)/shard_map/ppermute | solution.py:41
  52.6 11.2 %collective-permute-start.17 = (bf16[224,896]{1,0:T(8,128)(2,1)S(1)}, bf16[224,896]{1,0:T(8,128)(2,1)}, u32[]{:S(2)}, u32[]{:S(2)}) collective-permute-start(bf16[224,896]{1,0:T(8,128)(2,1)S(1)} %slice.14), channel_id=1, source_target_pairs={{0,64},{8,24},{16,80},{24,40},{32,96},{40,56},{48,112},{56,8},{64,... | collective-permute-start | bytes 1204232 | tf_op jit(solution)/shard_map/ppermute | solution.py:51
  55.2 9.2 %collective-permute-start.18 = (bf16[224,896]{1,0:T(8,128)(2,1)S(1)}, bf16[224,896]{1,0:T(8,128)(2,1)}, u32[]{:S(2)}, u32[]{:S(2)}) collective-permute-start(bf16[224,896]{1,0:T(8,128)(2,1)S(1)} %slice.15), channel_id=1, source_target_pairs={{0,192},{8,56},{16,208},{24,8},{32,224},{40,24},{48,240},{56,40},{... | collective-permute-start | bytes 1204232 | tf_op jit(solution)/shard_map/ppermute | solution.py:51
  57.1 10.5 %collective-permute-start.19 = (bf16[448,896]{1,0:T(8,128)(2,1)S(1)}, bf16[448,896]{1,0:T(8,128)(2,1)S(1)}, u32[]{:S(2)}, u32[]{:S(2)}) collective-permute-start(bf16[448,896]{1,0:T(8,128)(2,1)S(1)} %pad_maximum_fusion.rest_0_), channel_id=1, source_target_pairs={{0,8},{8,0},{1,9},{9,1},{2,10},{10,2},{3,11},{11,3},{4,12},{12,4},... | collective-permute-start | bytes 2408456 | tf_op jit(solution)/shard_map/ppermute | solution.py:41
  63.8 3.8 %collective-permute-start.21 = (bf16[448,896]{1,0:T(8,128)(2,1)}, bf16[448,896]{1,0:T(8,128)(2,1)}, u32[]{:S(2)}, u32[]{:S(2)}) collective-permute-start(bf16[448,896]{1,0:T(8,128)(2,1)} %collective-permute-done.9.rest_2_), channel_id=1, source_target_pairs={{0,8},{8,0},{1,9},{9,1},{2,10},{10,2},{3,11},{11,3},{4,12},{12,4},... | collective-permute-start | bytes 2408456 | tf_op jit(solution)/shard_map/ppermute | solution.py:41
  63.8 3.2 %collective-permute-start.22 = (bf16[224,896]{1,0:T(8,128)(2,1)}, bf16[224,896]{1,0:T(8,128)(2,1)}, u32[]{:S(2)}, u32[]{:S(2)}) collective-permute-start(bf16[224,896]{1,0:T(8,128)(2,1)} %collective-permute-done.17.rest_3_), channel_id=1, source_target_pairs={{0,8},{8,0},{1,9},{9,1},{2,10},{10,2},{3,11},{11,3},{4,12},{12,4},... | collective-permute-start | bytes 1204232 | tf_op jit(solution)/shard_map/ppermute | solution.py:41
  64.3 3.3 %collective-permute-start.23 = (bf16[224,896]{1,0:T(8,128)(2,1)}, bf16[224,896]{1,0:T(8,128)(2,1)}, u32[]{:S(2)}, u32[]{:S(2)}) collective-permute-start(bf16[224,896]{1,0:T(8,128)(2,1)} %collective-permute-done.18.rest_4_), channel_id=1, source_target_pairs={{0,8},{8,0},{1,9},{9,1},{2,10},{10,2},{3,11},{11,3},{4,12},{12,4},... | collective-permute-start | bytes 1204232 | tf_op jit(solution)/shard_map/ppermute | solution.py:41
  67.0 15.5 %collective-permute-start.25 = (bf16[512,256]{1,0:T(8,128)(2,1)}, bf16[512,256]{1,0:T(8,128)(2,1)S(1)}, u32[]{:S(2)}, u32[]{:S(2)}) collective-permute-start(bf16[512,256]{1,0:T(8,128)(2,1)} %collective-permute-done.24.kv2_ref), channel_id=1, source_target_pairs={{0,2},{1,3},{2,4},{3,5},{4,6},{5,7},{6,0},{7,1},{8,10},{9,11},{10,... | collective-permute-start | bytes 786440 | tf_op jit(solution)/shard_map/ppermute | solution.py:41
  67.6 2.0 %copy-start.1 = (bf16[512,3584]{1,0:T(8,128)(2,1)S(1)}, bf16[512,3584]{1,0:T(8,128)(2,1)}, u32[]{:S(2)}) copy-start(bf16[512,3584]{1,0:T(8,128)(2,1)} %copy-done) | copy-start | bytes 11010052
  87.3 8.9 %collective-permute-start.26 = (bf16[128,896]{1,0:T(8,128)(2,1)S(1)}, bf16[128,896]{1,0:T(8,128)(2,1)S(1)}, u32[]{:S(2)}, u32[]{:S(2)}) collective-permute-start(bf16[128,896]{1,0:T(8,128)(2,1)S(1)} %get-tuple-element.41), channel_id=1, source_target_pairs={{0,1},{1,2},{2,3},{3,4},{4,5},{5,6},{6,7},{7,0},{8,9},{9,10},{10,1... | collective-permute-start | bytes 688136 | tf_op jit(solution)/shard_map/ppermute | solution.py:41
  87.4 9.5 %collective-permute-start.27 = (bf16[128,896]{1,0:T(8,128)(2,1)S(1)}, bf16[128,896]{1,0:T(8,128)(2,1)S(1)}, u32[]{:S(2)}, u32[]{:S(2)}) collective-permute-start(bf16[128,896]{1,0:T(8,128)(2,1)S(1)} %get-tuple-element.42), channel_id=1, source_target_pairs={{0,7},{1,0},{2,1},{3,2},{4,3},{5,4},{6,5},{7,6},{8,15},{9,8},{10,9... | collective-permute-start | bytes 688136 | tf_op jit(solution)/shard_map/ppermute | solution.py:41

commit v3 on v2

v3 whole, which is shorter than its diff:
```python
import functools
import math

import jax
import jax.numpy as jnp
from jax import lax
from jax.experimental import pallas as pl
from jax.experimental.pallas import tpu as pltpu
from jax.sharding import Mesh
from jax.sharding import PartitionSpec as P

D = 3584
HEAD_DIM = 128
HEADS = 14
KV_HEADS = 2
GROUP = HEADS // KV_HEADS
LENGTH = 2048
TOK = 256
HALF = 128
ROWS = 512
WROWS = 112
REPOS = 6
QC = GROUP * HEAD_DIM
rope_base = 1000000.0
norm_eps = 1e-06
SCALE2 = HEAD_DIM ** (-0.5) * math.log2(math.e)
MASKED = -1e30
SIZES = {"x": 4, "y": 4, "core": 2, "ctx": 8}
ORDER = (0, -1, 1, 2)

SMALL = pl.CostEstimate(flops=1, bytes_accessed=1, transcendentals=0)
ANY = pl.BlockSpec(memory_space=pl.ANY)
HBM = pl.BlockSpec(memory_space=pltpu.HBM)
VM = pl.BlockSpec(memory_space=pltpu.VMEM)
SM = pl.BlockSpec(memory_space=pltpu.SMEM)


def params(mebibytes):
    return pltpu.CompilerParams(vmem_limit_bytes=mebibytes << 20)


def ring(value, axis, step):
    n = SIZES[axis]
    return lax.ppermute(value, axis, [(i, (i + step) % n) for i in range(n)])


def hop(value, phase, step):
    pairs = []
    for y in range(4):
        for x in range(4):
            for core in range(2):
                to_y, to_x = (y, (x + step) % 4) if core == phase else ((y + step) % 4, x)
                pairs.append(((y * 4 + x) * 2 + core, (to_y * 4 + to_x) * 2 + core))
    return lax.ppermute(value, ("y", "x", "core"), pairs)


def place_weights(info_ref, pieces, chunks, w_refs):
    y, x = info_ref[0], info_ref[1]
    for side in range(2):
        core = info_ref[2] if side == 0 else 1 - info_ref[2]
        block = 0
        for piece in pieces[side]:
            for i in range(piece.shape[0] // WROWS):
                outer, inner = ORDER[block // 4], ORDER[block % 4]
                dy = jnp.where(core == 0, outer, inner)
                dx = jnp.where(core == 0, inner, outer)
                chip = ((y + dy + 4) % 4) * 4 + (x + dx + 4) % 4
                at = pl.multiple_of((chip * 2 + core) * WROWS, 16)
                for (lane, wide), w_ref in zip(chunks, w_refs):
                    w_ref[pl.ds(at, WROWS), :] = piece[
                        i * WROWS : (i + 1) * WROWS, lane : lane + wide
                    ]
                block += 1


def starts(lengths_ref, pos):
    start, end = jnp.zeros_like(pos), 0
    for r in range(REPOS):
        end = end + lengths_ref[0, r]
        start = start + jnp.where(pos >= end, lengths_ref[0, r], 0)
    return start


def cut_kernel(info_ref, weight_ref, out_ref, sem):
    odd = info_ref[3] % 2
    copies = []
    for n, (src, dst, wide) in enumerate(
        ((1792 + odd * 128, 0, 128), (2048 + odd * 128, 128, 128), (odd * QC, 256, QC))
    ):
        copy = pltpu.make_async_copy(
            weight_ref.at[:, pl.ds(pl.multiple_of(src, 128), wide)],
            out_ref.at[:, pl.ds(dst, wide)],
            sem.at[n],
        )
        copy.start()
        copies.append(copy)
    for copy in copies:
        copy.wait()


def cut(info, weight):
    return pl.pallas_call(
        cut_kernel,
        out_shape=jax.ShapeDtypeStruct((WROWS, 256 + QC), jnp.bfloat16),
        in_specs=[SM, HBM],
        out_specs=VM,
        scratch_shapes=[pltpu.SemaphoreType.DMA((3,))],
        compiler_params=params(4),
        cost_estimate=SMALL,
        name="cut",
    )(info, weight)


def output_kernel(info_ref, own_top_ref, own_low_ref, other_top_ref, other_low_ref, out_ref, sem):
    odd = info_ref[3] % 2
    own_at = pl.multiple_of(odd * QC, 128)
    other_at = pl.multiple_of((1 - odd) * QC, 128)
    copies = []
    for n, (src_ref, row, at) in enumerate(
        (
            (own_top_ref, 0, own_at),
            (own_low_ref, HALF, own_at),
            (other_top_ref, 0, other_at),
            (other_low_ref, HALF, other_at),
        )
    ):
        copy = pltpu.make_async_copy(
            src_ref, out_ref.at[pl.ds(row, HALF), pl.ds(at, QC)], sem.at[n]
        )
        copy.start()
        copies.append(copy)
    for copy in copies:
        copy.wait()


def output(info, *parts):
    return pl.pallas_call(
        output_kernel,
        out_shape=jax.ShapeDtypeStruct((TOK, 2 * QC), jnp.bfloat16),
        in_specs=[SM] + [VM] * 4,
        out_specs=ANY,
        scratch_shapes=[pltpu.SemaphoreType.DMA((4,))],
        compiler_params=params(4),
        cost_estimate=SMALL,
        name="output",
    )(info, *parts)


def split_kernel(*refs):
    blocks, (kv_ref, q_ref) = refs[:4], refs[4:]
    for n, block_ref in enumerate(blocks):
        kv_ref[n * WROWS : (n + 1) * WROWS, :] = block_ref[:, 0:256]
        q_ref[n * WROWS : (n + 1) * WROWS, :] = block_ref[:, 256:]


def split(blocks):
    return pl.pallas_call(
        split_kernel,
        out_shape=[
            jax.ShapeDtypeStruct((4 * WROWS, 256), jnp.bfloat16),
            jax.ShapeDtypeStruct((4 * WROWS, QC), jnp.bfloat16),
        ],
        in_specs=[VM] * 4,
        out_specs=[VM] * 2,
        compiler_params=params(4),
        cost_estimate=SMALL,
        name="split",
    )(*blocks)


def norm_kernel(hidden_ref, gain_ref, low_ref, high_ref):
    gain = jnp.concatenate([gain_ref[n : n + 1, :] for n in range(D // 128)], 1)
    for half, out_ref in enumerate((low_ref, high_ref)):

        @pl.loop(0, HALF // 32)
        def _(i, half=half, out_ref=out_ref):
            at = pl.multiple_of(i * 32, 32)
            value = hidden_ref[pl.ds(half * HALF + at, 32), :].astype(jnp.float32)
            mean = jnp.mean(value * value, axis=1, keepdims=True)
            value = value * lax.rsqrt(mean + norm_eps) * gain
            out_ref[pl.ds(at, 32), :] = value.astype(jnp.bfloat16)


def norm(hidden, gain):
    return pl.pallas_call(
        norm_kernel,
        out_shape=[jax.ShapeDtypeStruct((HALF, D), jnp.bfloat16)] * 2,
        in_specs=[VM, VM],
        out_specs=[VM] * 2,
        compiler_params=params(12),
        cost_estimate=SMALL,
        name="norm",
    )(hidden, gain.reshape(D // 128, 128))


def tables_kernel(info_ref, lengths_ref, freq_ref, cos_ref, sin_ref):
    base = info_ref[3] * TOK - HALF + LENGTH
    sign = jnp.where(lax.broadcasted_iota(jnp.int32, (1, HEAD_DIM), 1) < HEAD_DIM // 2, -1.0, 1.0)

    @pl.loop(0, ROWS // 64)
    def _(i):
        at = pl.multiple_of(i * 64, 64)
        pos = (lax.broadcasted_iota(jnp.int32, (64, HEAD_DIM), 0) + (base + at)) & (LENGTH - 1)
        angle = (pos - starts(lengths_ref, pos)).astype(jnp.float32) * freq_ref[...]
        cos_ref[pl.ds(at, 64), :] = jnp.cos(angle)
        sin_ref[pl.ds(at, 64), :] = jnp.sin(angle) * sign


def tables(info, lengths, freq):
    return pl.pallas_call(
        tables_kernel,
        out_shape=[jax.ShapeDtypeStruct((ROWS, HEAD_DIM), jnp.float32)] * 2,
        in_specs=[SM, SM, VM],
        out_specs=[VM] * 2,
        compiler_params=params(4),
        cost_estimate=SMALL,
        name="tables",
    )(info, lengths, freq)


def rotate(value, cosine, sine):
    return value * cosine + pltpu.roll(value, HEAD_DIM // 2, 1) * sine


KV_CHUNKS = ((0, 256),)
Q_CHUNKS = ((0, 512), (512, 384))


def kv_kernel(count, info_ref, bias_ref, cos_ref, sin_ref, *rest):
    tokens, rest = rest[:4], rest[4:]
    out_ref, x_ref, w_ref = rest[2 * count :]
    place_weights(info_ref, (rest[:count], rest[count : 2 * count]), KV_CHUNKS, (w_ref,))
    for n, src_ref in enumerate(tokens):
        x_ref[n * HALF : (n + 1) * HALF, :] = src_ref[...]
    value = jnp.dot(x_ref[...], w_ref[...], preferred_element_type=jnp.float32)
    odd = info_ref[3] % 2
    k_at, v_at = (pl.multiple_of(at + odd * 128, 128) for at in (1792, 2048))
    bias = jnp.concatenate([bias_ref[:, pl.ds(k_at, 128)], bias_ref[:, pl.ds(v_at, 128)]], 1)
    value = (value + bias).astype(jnp.bfloat16)
    keys = rotate(value[:, :128].astype(jnp.float32), cos_ref[...], sin_ref[...])
    out_ref[:, 0:128] = keys.astype(jnp.bfloat16)
    out_ref[:, 128:256] = value[:, 128:]


def kv_project(info, tokens, near, far, bias, cosine, sine):
    count = len(near)
    return pl.pallas_call(
        functools.partial(kv_kernel, count),
        out_shape=[
            jax.ShapeDtypeStruct((ROWS, 256), jnp.bfloat16),
            jax.ShapeDtypeStruct((ROWS, D), jnp.bfloat16),
        ],
        in_specs=[SM] + [VM] * (7 + 2 * count),
        out_specs=[VM] * 2,
        scratch_shapes=[pltpu.VMEM((D, 256), jnp.bfloat16)],
        compiler_params=params(8),
        cost_estimate=SMALL,
        name="kv_project",
    )(info, bias, cosine, sine, *tokens, *near, *far)


def q_kernel(count, info_ref, x_ref, bias_ref, cos_ref, sin_ref, *rest):
    out_ref, *w_refs = rest[2 * count :]
    place_weights(info_ref, (rest[:count], rest[count : 2 * count]), Q_CHUNKS, w_refs)
    for (at, wide), w_ref in zip(Q_CHUNKS, w_refs):
        value = jnp.dot(x_ref[...], w_ref[...], preferred_element_type=jnp.float32)
        bias = bias_ref[:, pl.ds(pl.multiple_of((info_ref[3] % 2) * QC + at, 128), wide)]
        value = (value + bias).astype(jnp.bfloat16).astype(jnp.float32)
        for lane in range(0, wide, 128):
            head = rotate(value[:, lane : lane + 128], cos_ref[...], sin_ref[...])
            out_ref[:, at + lane : at + lane + 128] = head.astype(jnp.bfloat16)


def q_project(info, x, near, far, bias, cosine, sine):
    count = len(near)
    return pl.pallas_call(
        functools.partial(q_kernel, count),
        out_shape=jax.ShapeDtypeStruct((ROWS, QC), jnp.bfloat16),
        in_specs=[SM] + [VM] * (4 + 2 * count),
        out_specs=VM,
        scratch_shapes=[pltpu.VMEM((D, w), jnp.bfloat16) for _, w in Q_CHUNKS],
        compiler_params=params(14),
        cost_estimate=SMALL,
        name="q_project",
    )(info, x, bias, cosine, sine, *near, *far)


STACK = GROUP * HALF


def stacked(q_ref, tile):
    rows = slice(HALF * tile, HALF * (tile + 1))
    return jnp.concatenate(
        [q_ref[rows, h * HEAD_DIM : (h + 1) * HEAD_DIM] for h in range(GROUP)], 0
    )


def mask_of(info_ref, lengths_ref, tile, from_row, count):
    base = info_ref[3] * TOK - HALF + LENGTH
    key = lax.broadcasted_iota(jnp.int32, (HALF, count), 1) + (base - 1024 + from_row)
    key = key & (LENGTH - 1)
    pos = (lax.broadcasted_iota(jnp.int32, (HALF, 1), 0) + (base + HALF * tile)) & (LENGTH - 1)
    return jnp.where((key <= pos) & (key >= starts(lengths_ref, pos)), 0.0, MASKED)


def score(q_ref, tile, k, out_ref):
    out_ref[...] = lax.dot_general(
        stacked(q_ref, tile), k, (((1,), (1,)), ((), ())), preferred_element_type=jnp.float32
    )


def soften(score_ref, mask, part, top, weight_ref):
    for lane in range(0, mask.shape[1], 128):
        lanes = slice(lane, lane + 128)
        weight = jnp.exp2(score_ref[part, lanes] * SCALE2 + mask[:, lanes] - top)
        weight_ref[part, lanes] = weight.astype(jnp.bfloat16)


def top_of(score_ref, mask, part):
    best = score_ref[part, 0:128] * SCALE2 + mask[:, 0:128]
    for lane in range(128, mask.shape[1], 128):
        lanes = slice(lane, lane + 128)
        best = jnp.maximum(best, score_ref[part, lanes] * SCALE2 + mask[:, lanes])
    return jnp.broadcast_to(jnp.max(best, axis=1, keepdims=True), (HALF, HEAD_DIM))


def load_values(v_ref, *blocks):
    at = 0
    for block in blocks:
        v_ref[at : at + block.shape[0], 0:128] = block[:, 128:256]
        at += block.shape[0]
    v_ref[:, 128:256] = jnp.ones((at, 128), jnp.bfloat16)


def weigh(tiles, kept, from_row, q_ref, k_ref, v_ref, score_refs, weight_refs, info_ref, lengths_ref):
    def keys(n):
        first = max(from_row, HALF * tiles[n]) - from_row
        return slice(first, first + kept[n])

    score(q_ref, tiles[0], k_ref[keys(0), :], score_refs[0])
    for n, tile in enumerate(tiles):
        if n + 1 < len(tiles):
            score(q_ref, tiles[n + 1], k_ref[keys(n + 1), :], score_refs[n + 1])
        mask = mask_of(info_ref, lengths_ref, tile, max(from_row, HALF * tile), kept[n])
        tops = []
        for h in range(GROUP):
            part = slice(h * HALF, (h + 1) * HALF)
            top = top_of(score_refs[n], mask, part)
            tops.append(top)
            soften(score_refs[n], mask, part, top, weight_refs[n])
        yield n, tops, jnp.dot(weight_refs[n][...], v_ref[keys(n), :], preferred_element_type=jnp.float32)


def first_kernel(tiles, info_ref, lengths_ref, q_ref, kv2_ref, kv0_ref, mix_ref, top_ref, k_ref, v_ref, *rest):
    kept, n = [640 + HALF * tile for tile in tiles], len(tiles)
    k_ref[0:512, :] = kv2_ref[:, 0:128]
    k_ref[512:1024, :] = kv0_ref[:, 0:128]
    load_values(v_ref, kv2_ref, kv0_ref)
    for n, tops, mixed in weigh(
        tiles, kept, 512, q_ref, k_ref, v_ref, rest[:n], rest[n:], info_ref, lengths_ref
    ):
        for h, top in enumerate(tops):
            top_ref[n * STACK + h * HALF : n * STACK + (h + 1) * HALF, :] = top
        mix_ref[n * STACK : (n + 1) * STACK, :] = mixed


def attention_first(tiles, info, lengths, q, kv2, kv0):
    n, kept = len(tiles), [640 + HALF * tile for tile in tiles]
    return pl.pallas_call(
        functools.partial(first_kernel, tiles),
        out_shape=[
            jax.ShapeDtypeStruct((n * STACK, 256), jnp.float32),
            jax.ShapeDtypeStruct((n * STACK, 128), jnp.float32),
        ],
        in_specs=[SM, SM] + [VM] * 3,
        out_specs=[VM] * 2,
        scratch_shapes=[pltpu.VMEM((1024, 128), jnp.bfloat16), pltpu.VMEM((1024, 256), jnp.bfloat16)]
        + [pltpu.VMEM((STACK, c), jnp.float32) for c in kept]
        + [pltpu.VMEM((STACK, c), jnp.bfloat16) for c in kept],
        compiler_params=params(18),
        cost_estimate=SMALL,
        name="attention_first",
    )(info, lengths, q, kv2, kv0)


def full_kernel(tiles, info_ref, lengths_ref, q_ref, kv4_ref, kv2_ref, kv0_ref, *rest):
    n = len(tiles)
    outs, k_ref, v_ref, rest = rest[:n], rest[n], rest[n + 1], rest[n + 2 :]
    for at, block in enumerate((kv4_ref, kv2_ref, kv0_ref)):
        k_ref[at * 512 : (at + 1) * 512, :] = block[:, 0:128]
    load_values(v_ref, kv4_ref, kv2_ref, kv0_ref)
    for n, _, mixed in weigh(
        tiles, [1152] * n, 0, q_ref, k_ref, v_ref, rest[:n], rest[n:], info_ref, lengths_ref
    ):
        value = (mixed[:, 0:128] / mixed[:, 128:256]).astype(jnp.bfloat16)
        for h in range(GROUP):
            outs[n][:, h * HEAD_DIM : (h + 1) * HEAD_DIM] = value[h * HALF : (h + 1) * HALF]


def attention_full(tiles, info, lengths, q, kv4, kv2, kv0):
    n = len(tiles)
    return pl.pallas_call(
        functools.partial(full_kernel, tiles),
        out_shape=[jax.ShapeDtypeStruct((HALF, QC), jnp.bfloat16)] * n,
        in_specs=[SM, SM] + [VM] * 4,
        out_specs=[VM] * n,
        scratch_shapes=[pltpu.VMEM((1536, 128), jnp.bfloat16), pltpu.VMEM((1536, 256), jnp.bfloat16)]
        + [pltpu.VMEM((STACK, 1152), jnp.float32)] * n
        + [pltpu.VMEM((STACK, 1152), jnp.bfloat16)] * n,
        compiler_params=params(22),
        cost_estimate=SMALL,
        name="attention_full",
    )(info, lengths, q, kv4, kv2, kv0)


def last_kernel(tiles, info_ref, lengths_ref, q_ref, kv_ref, mix_ref, top_ref, *rest):
    n = len(tiles)
    outs, v_ref = rest[:n], rest[n]
    score_refs, weight_refs, keep_refs = rest[n + 1 : 2 * n + 1], rest[2 * n + 1 : 3 * n + 1], rest[3 * n + 1 :]
    load_values(v_ref, kv_ref)
    for tile, score_ref in zip(tiles, score_refs):
        score(q_ref, tile, kv_ref[HALF * tile : 512, 0:128], score_ref)
    for at, (tile, out_ref, score_ref, weight_ref, keep_ref) in enumerate(
        zip(tiles, outs, score_refs, weight_refs, keep_refs)
    ):
        mask = mask_of(info_ref, lengths_ref, tile, HALF * tile, 512 - HALF * tile)
        for h in range(GROUP):
            part = slice(h * HALF, (h + 1) * HALF)
            old = top_ref[at * STACK + h * HALF : at * STACK + (h + 1) * HALF, :]
            top = jnp.maximum(top_of(score_ref, mask, part), old)
            keep_ref[part, :] = jnp.exp2(old - top)
            soften(score_ref, mask, part, top, weight_ref)
        mixed = jnp.dot(
            weight_ref[...], v_ref[HALF * tile : 512, :], preferred_element_type=jnp.float32
        )
        for h in range(GROUP):
            part = slice(h * HALF, (h + 1) * HALF)
            before = mix_ref[at * STACK + h * HALF : at * STACK + (h + 1) * HALF, :]
            keep = keep_ref[part, :]
            total = mixed[part, 128:256] + before[:, 128:256] * keep
            value = (mixed[part, 0:128] + before[:, 0:128] * keep) / total
            out_ref[:, h * HEAD_DIM : (h + 1) * HEAD_DIM] = value.astype(jnp.bfloat16)


def attention_last(tiles, info, lengths, q, kv4, state):
    n = len(tiles)
    counts = [512 - HALF * tile for tile in tiles]
    return pl.pallas_call(
        functools.partial(last_kernel, tiles),
        out_shape=[jax.ShapeDtypeStruct((HALF, QC), jnp.bfloat16)] * n,
        in_specs=[SM, SM] + [VM] * 4,
        out_specs=[VM] * n,
        scratch_shapes=[pltpu.VMEM((512, 256), jnp.bfloat16)]
        + [pltpu.VMEM((STACK, c), jnp.float32) for c in counts]
        + [pltpu.VMEM((STACK, c), jnp.bfloat16) for c in counts]
        + [pltpu.VMEM((STACK, 128), jnp.float32) for _ in counts],
        compiler_params=params(12),
        cost_estimate=SMALL,
        name="attention_last",
    )(info, lengths, q, kv4, *state)


def body(hidden, norm_gain, qkv_weight, qkv_bias, repo_lengths):
    z = lax.axis_index("ctx")
    y, x, core = lax.axis_index("y"), lax.axis_index("x"), lax.axis_index("core")
    info = jnp.stack([y, x, core, z]).astype(jnp.int32)
    freq = rope_base ** (-jnp.arange(0, HEAD_DIM, 2, dtype=jnp.float32) / HEAD_DIM)
    freq = jnp.concatenate([freq, freq]).reshape(1, HEAD_DIM)
    bias = qkv_bias.reshape(1, -1)

    own = cut(info, qkv_weight)
    blocks = [own, hop(own, 0, 1), hop(own, 0, -1), hop(own, 0, 2)]
    low, high = norm(hidden, norm_gain)
    kv_row, q_row = split(blocks)
    before = ring(high, "ctx", 1)
    after = ring(low, "ctx", -1)

    kv_row, low, high = lax.optimization_barrier((kv_row, low, high))
    kv_near = [kv_row, hop(kv_row, 1, 1), hop(kv_row, 1, -1), hop(kv_row, 1, 2)]
    q_near = [q_row, hop(q_row, 1, 1), hop(q_row, 1, -1), hop(q_row, 1, 2)]
    cosine, sine = tables(info, repo_lengths, freq)
    *kv_near, cosine, sine = lax.optimization_barrier((*kv_near, cosine, sine))
    kv_near[3], before, after = lax.optimization_barrier((kv_near[3], before, after))
    kv_far = [ring(piece, "core", 1) for piece in kv_near]
    kv0, normed = kv_project(info, (before, low, high, after), kv_near, kv_far, bias, cosine, sine)
    kv2 = ring(kv0, "ctx", 2)

    *q_near, kv2 = lax.optimization_barrier((*q_near, kv2))
    kv4 = ring(kv2, "ctx", 2)
    q_far = [ring(piece, "core", 1) for piece in q_near]
    q = q_project(info, normed, q_near, q_far, bias, cosine, sine)

    state = attention_first((0, 3), info, repo_lengths, q, kv2, kv0)
    back, ahead = attention_last((0, 3), info, repo_lengths, q, kv4, state)
    other_top = ring(ahead, "ctx", 1)
    other_low = ring(back, "ctx", -1)
    own_top, own_low = attention_full((1, 2), info, repo_lengths, q, kv4, kv2, kv0)
    return output(info, own_top, own_low, other_top, other_low)


def solution(mesh):
    fine = Mesh(mesh.devices.reshape(4, 4, 2, 8), ("y", "x", "core", "ctx"))
    grp = ("y", "x", "core")
    tokens = P(("y", "x", "core", "ctx"), None)
    in_specs = (tokens, P(), P(grp, None), P(), P(grp, None))
    return jax.shard_map(body, mesh=fine, in_specs=in_specs, out_specs=tokens, check_vma=False)
```

time: 98.6 us -> 86.6 us (0.88)
  local copies, waits for them, and re-layouts: 10.3 us -> 2.23 us
  waiting for transfers between devices: 27.4 us -> 33.6 us
  Pallas kernels: 28.6 us -> 23.3 us
  starting transfers between devices: 30.2 us -> 26 us
  other arithmetic: 1.43 us -> 0.16 us
    pallas_call x2 -> x1, Pallas kernels: 8.06 us -> 2.01 us  [attention_last(): pl.pallas_call(functools.partial(last_kernel, tiles), out_shape=[jax.Shap...]
    ppermute x13 -> x9, starting transfers between devices: 19.8 us -> 14.5 us  [hop(): return lax.ppermute(value, ('y', 'x', 'core'), pairs)]
    slice x3 -> x0, local copies, waits for them, and re-layouts: 4.88 us -> none  [the longest x1 2.82 us: body(): after = ring(hidden[:HALF], 'ctx', -1)]
    ppermute x13 -> x9, waiting for transfers between devices: 15.3 us -> 19.4 us  [hop(): return lax.ppermute(value, ('y', 'x', 'core'), pairs)]
    dynamic_slice x4 -> x0, local copies, waits for them, and re-layouts: 3.26 us -> none  [the longest x1 0.95 us: body(): q_own = lax.dynamic_slice(qkv_weight, (0, odd * QC), (WROWS, QC))]
    ppermute x15 -> x14, waiting for transfers between devices: 12.1 us -> 14.2 us  [ring(): return lax.ppermute(value, axis, [(i, (i + step) % n) for i in range(n)])]
    select_n x1 -> x0, other arithmetic: 1.16 us -> none  [body(): jnp.where(odd == 0, jnp.concatenate([own, other], 1), jnp.concatenate([ot...]
    ppermute x15 -> x14, starting transfers between devices: 10.4 us -> 11.5 us  [ring(): return lax.ppermute(value, axis, [(i, (i + step) % n) for i in range(n)])]
  transfers between devices with their start and end apart: 28 -> 23, of which waited for: 9 -> 14; matrix products, arithmetic and copies ran while one was open for 8% -> 0% of each run, Pallas kernels for 24% -> 22%
where the time goes in v3:
time: 86.6 us; the launch traced here: 85.6 us
  waiting for transfers between devices  33.6 us (39%)
  starting transfers between devices  26 us (30%)
  Pallas kernels  23.3 us (27%)
  local copies, waits for them, and re-layouts  2.23 us (3%)
    ppermute x9, waiting for transfers between devices, hop(): return lax.ppermute(value, ('y', 'x', 'core'), pairs)  19.4 us
    ppermute x9, starting transfers between devices, hop(): return lax.ppermute(value, ('y', 'x', 'core'), pairs)  14.5 us
    ppermute x14, waiting for transfers between devices, ring(): return lax.ppermute(value, axis, [(i, (i + step) % n) for i in range(n)])  14.2 us
    ppermute x14, starting transfers between devices, ring(): return lax.ppermute(value, axis, [(i, (i + step) % n) for i in range(n)])  11.5 us
    pallas_call x1, Pallas kernels, q_project(): pl.pallas_call(functools.partial(q_kernel, count), out_shape=jax.ShapeDty...  5.16 us
    pallas_call x1, Pallas kernels, attention_full(): pl.pallas_call(functools.partial(full_kernel, tiles), out_shape=[jax.Shap...  4.68 us
    pallas_call x1, Pallas kernels, attention_first(): pl.pallas_call(functools.partial(first_kernel, tiles), out_shape=[jax.Sha...  3.47 us
    pallas_call x1, Pallas kernels, kv_project(): pl.pallas_call(functools.partial(kv_kernel, count), out_shape=[jax.ShapeD...  2.64 us
  transfers between devices with their start and end apart: 23, of which 14 were waited for; matrix products, arithmetic and copies ran while one was open for 0% of the time, Pallas kernels for 22%

profile of v3, /device:TPU:6, one launch (start us, length us, event | category | flops | bytes accessed | tf_op | source)
XLA Modules:
  0.0 85.6 jit_solution(9197985100361575650)
XLA Ops:
  0.0 1.5 %copy-done = bf16[256,3584]{1,0:T(8,128)(2,1)S(1)} copy-done((bf16[256,3584]{1,0:T(8,128)(2,1)S(1)}, bf16[256,3584]{1,0:T(8,128)(2,1)}, u32[]{:S(2)}) %copy-start) | copy-done | bytes 1835032
  1.5 0.7 copy-done.2
  2.2 1.3 %norm.1 = (bf16[128,3584]{1,0:T(8,128)(2,1)S(1)}, bf16[128,3584]{1,0:T(8,128)(2,1)S(1)}) custom-call(bf16[256,3584]{1,0:T(8,128)(2,1)S(1)} %copy-done, f32[28,128]{1,0:T(8,128)S(1)} %bitcast.7), custom_call_target="tpu_custom_call" | custom-call | flops 1 | bytes 1 | tf_op jit(solution)/shard_map/norm/pallas_call | solution.py:185
  3.5 2.0 %collective-permute-start.6 = (bf16[128,3584]{1,0:T(8,128)(2,1)S(1)}, bf16[128,3584]{1,0:T(8,128)(2,1)S(1)}, u32[]{:S(2)}, u32[]{:S(2)}) collective-permute-start(bf16[128,3584]{1,0:T(8,128)(2,1)S(1)} %get-tuple-element.47.rest_2_), channel_id=1, source_target_pairs={{0,1},{1,2},{2,3},{3,4},{4,5},{5,6},{6,7},{7,0},{8,9},{9,10},{10,1... | collective-permute-start | bytes 2752520 | tf_op jit(solution)/shard_map/ppermute | solution.py:44
  5.5 4.0 %collective-permute-start.7 = (bf16[128,3584]{1,0:T(8,128)(2,1)S(1)}, bf16[128,3584]{1,0:T(8,128)(2,1)}, u32[]{:S(2)}, u32[]{:S(2)}) collective-permute-start(bf16[128,3584]{1,0:T(8,128)(2,1)S(1)} %get-tuple-element.46.rest_1_), channel_id=1, source_target_pairs={{0,7},{1,0},{2,1},{3,2},{4,3},{5,4},{6,5},{7,6},{8,15},{9,8},{10,9... | collective-permute-start | bytes 2752520 | tf_op jit(solution)/shard_map/ppermute | solution.py:44
  9.5 0.1 pad_add_fusion.info_ref
  9.6 0.6 cut.1.refs_0_
  10.2 0.6 collective-permute-start
  10.8 1.5 %collective-permute-start.1 = (bf16[112,1152]{1,0:T(8,128)(2,1)S(1)}, bf16[112,1152]{1,0:T(8,128)(2,1)S(1)}, u32[]{:S(2)}, u32[]{:S(2)}) collective-permute-start(bf16[112,1152]{1,0:T(8,128)(2,1)S(1)} %cut.1.refs_0_), channel_id=1, source_target_pairs={{0,48},{8,200},{16,0},{24,216},{32,16},{40,232},{48,32},{56,248},{... | collective-permute-start | bytes 774152 | tf_op jit(solution)/shard_map/ppermute | solution.py:54
  12.4 1.4 %collective-permute-start.2 = (bf16[112,1152]{1,0:T(8,128)(2,1)S(1)}, bf16[112,1152]{1,0:T(8,128)(2,1)S(1)}, u32[]{:S(2)}, u32[]{:S(2)}) collective-permute-start(bf16[112,1152]{1,0:T(8,128)(2,1)S(1)} %cut.1.refs_0_), channel_id=1, source_target_pairs={{0,32},{8,136},{16,48},{24,152},{32,0},{40,168},{48,16},{56,184},{... | collective-permute-start | bytes 774152 | tf_op jit(solution)/shard_map/ppermute | solution.py:54
  13.8 2.9 %collective-permute-done.refs_1_ = bf16[112,1152]{1,0:T(8,128)(2,1)S(1)} collective-permute-done((bf16[112,1152]{1,0:T(8,128)(2,1)S(1)}, bf16[112,1152]{1,0:T(8,128)(2,1)S(1)}, u32[]{:S(2)}, u32[]{:S(2)}) %collective-permute-start) | collective-permute-done | bytes 258080 | tf_op jit(solution)/shard_map/ppermute | solution.py:54
  16.7 4.5 %collective-permute-done.1.refs_2_ = bf16[112,1152]{1,0:T(8,128)(2,1)S(1)} collective-permute-done((bf16[112,1152]{1,0:T(8,128)(2,1)S(1)}, bf16[112,1152]{1,0:T(8,128)(2,1)S(1)}, u32[]{:S(2)}, u32[]{:S(2)}) %collective-permute-start.1) | collective-permute-done | bytes 258080 | tf_op jit(solution)/shard_map/ppermute | solution.py:54
  21.1 0.1 split.1
  21.2 1.7 %collective-permute-start.3 = (bf16[448,256]{1,0:T(8,128)(2,1)S(1)}, bf16[448,256]{1,0:T(8,128)(2,1)S(1)}, u32[]{:S(2)}, u32[]{:S(2)}) collective-permute-start(bf16[448,256]{1,0:T(8,128)(2,1)S(1)} %get-tuple-element.49.rest_4_), channel_id=1, source_target_pairs={{0,64},{8,24},{16,80},{24,40},{32,96},{40,56},{48,112},{56,8},{64,... | collective-permute-start | bytes 688136 | tf_op jit(solution)/shard_map/ppermute | solution.py:54
  22.8 1.7 %collective-permute-start.4 = (bf16[448,256]{1,0:T(8,128)(2,1)S(1)}, bf16[448,256]{1,0:T(8,128)(2,1)S(1)}, u32[]{:S(2)}, u32[]{:S(2)}) collective-permute-start(bf16[448,256]{1,0:T(8,128)(2,1)S(1)} %get-tuple-element.49.rest_4_), channel_id=1, source_target_pairs={{0,192},{8,56},{16,208},{24,8},{32,224},{40,24},{48,240},{56,40},{... | collective-permute-start | bytes 688136 | tf_op jit(solution)/shard_map/ppermute | solution.py:54
  24.5 2.0 %collective-permute-start.5 = (bf16[448,256]{1,0:T(8,128)(2,1)S(1)}, bf16[448,256]{1,0:T(8,128)(2,1)S(1)}, u32[]{:S(2)}, u32[]{:S(2)}) collective-permute-start(bf16[448,256]{1,0:T(8,128)(2,1)S(1)} %get-tuple-element.49.rest_4_), channel_id=1, source_target_pairs={{0,128},{8,40},{16,144},{24,56},{32,160},{40,8},{48,176},{56,24},{... | collective-permute-start | bytes 688136 | tf_op jit(solution)/shard_map/ppermute | solution.py:54
  26.5 2.0 %collective-permute-done.3.rest_5_ = bf16[448,256]{1,0:T(8,128)(2,1)S(1)} collective-permute-done((bf16[448,256]{1,0:T(8,128)(2,1)S(1)}, bf16[448,256]{1,0:T(8,128)(2,1)S(1)}, u32[]{:S(2)}, u32[]{:S(2)}) %collective-permute-start.3) | collective-permute-done | bytes 229408 | tf_op jit(solution)/shard_map/ppermute | solution.py:54
  28.5 0.4 collective-permute-start.12
  28.9 5.3 %collective-permute-start.13 = (bf16[448,896]{1,0:T(8,128)(2,1)S(1)}, bf16[448,896]{1,0:T(8,128)(2,1)S(1)}, u32[]{:S(2)}, u32[]{:S(2)}) collective-permute-start(bf16[448,896]{1,0:T(8,128)(2,1)S(1)} %get-tuple-element.56.rest_0_), channel_id=1, source_target_pairs={{0,192},{8,56},{16,208},{24,8},{32,224},{40,24},{48,240},{56,40},{... | collective-permute-start | bytes 2408456 | tf_op jit(solution)/shard_map/ppermute | solution.py:54
  34.2 0.1 maximum_bitcast_fusion.freq_ref
  34.3 1.8 %tables.1 = (f32[512,128]{1,0:T(8,128)S(1)}, f32[512,128]{1,0:T(8,128)S(1)}) custom-call(s32[4]{0:T(128)S(1)} %pad_add_fusion.info_ref, s32[1,6]{1,0:T(1,128)S(1)} %copy-done.3, f32[1,128]{1,0:T(1,128)S(1)} %maximum_bitcast_fusion.freq_ref), custom_call_target="tpu_custom_call" | custom-call | flops 1 | bytes 1 | tf_op jit(solution)/shard_map/tables/pallas_call | solution.py:210
  36.1 0.1 collective-permute-start.10
  36.2 0.5 collective-permute-start.8
  36.7 1.0 %collective-permute-done.10.rest_10_ = bf16[448,256]{1,0:T(8,128)(2,1)S(1)} collective-permute-done((bf16[448,256]{1,0:T(8,128)(2,1)S(1)}, bf16[448,256]{1,0:T(8,128)(2,1)S(1)}, u32[]{:S(2)}, u32[]{:S(2)}) %collective-permute-start.10) | collective-permute-done | bytes 229408 | tf_op jit(solution)/shard_map/ppermute | solution.py:44
  37.7 0.1 collective-permute-start.9
  37.8 0.2 collective-permute-done.8.rest_8_
  38.0 0.2 collective-permute-start.11
  38.2 1.0 %collective-permute-done.9.rest_9_ = bf16[448,256]{1,0:T(8,128)(2,1)S(1)} collective-permute-done((bf16[448,256]{1,0:T(8,128)(2,1)S(1)}, bf16[448,256]{1,0:T(8,128)(2,1)S(1)}, u32[]{:S(2)}, u32[]{:S(2)}) %collective-permute-start.9) | collective-permute-done | bytes 229408 | tf_op jit(solution)/shard_map/ppermute | solution.py:44
  39.2 0.3 collective-permute-done.11.rest_11_
  39.5 2.6 %kv_project.1 = (bf16[512,256]{1,0:T(8,128)(2,1)S(1)}, bf16[512,3584]{1,0:T(8,128)(2,1)S(1)}) custom-call(s32[4]{0:T(128)S(1)} %pad_add_fusion.info_ref, f32[1,2304]{1,0:T(1,128)S(1)} %reshape.9.bias_ref, f32[512,128]{1,0:T(8,128)S(1)} %get-tuple-element.42.cos_ref, f32[512,128]{1,0:T(8,128)S(1)} %get-tuple-element.43.sin_ref, ...), custom_call_target="tpu_custom_call" | custom-call | flops 1 | bytes 1 | tf_op jit(solution)/shard_map/kv_project/pallas_call | solution.py:247
  42.1 0.3 collective-permute-start.15
  42.4 10.1 %collective-permute-done.13.rest_2_ = bf16[448,896]{1,0:T(8,128)(2,1)S(1)} collective-permute-done((bf16[448,896]{1,0:T(8,128)(2,1)S(1)}, bf16[448,896]{1,0:T(8,128)(2,1)S(1)}, u32[]{:S(2)}, u32[]{:S(2)}) %collective-permute-start.13) | collective-permute-done | bytes 802848 | tf_op jit(solution)/shard_map/ppermute | solution.py:54
  52.5 6.0 %collective-permute-done.15.kv2_ref = bf16[512,256]{1,0:T(8,128)(2,1)S(1)} collective-permute-done((bf16[512,256]{1,0:T(8,128)(2,1)S(1)}, bf16[512,256]{1,0:T(8,128)(2,1)S(1)}, u32[]{:S(2)}, u32[]{:S(2)}) %collective-permute-start.15) | collective-permute-done | bytes 262176 | tf_op jit(solution)/shard_map/ppermute | solution.py:44
  58.5 0.5 collective-permute-start.17
  59.0 0.0 collective-permute-start.18
  59.0 0.5 collective-permute-start.19
  59.5 1.3 %collective-permute-done.16.rest_4_ = bf16[448,896]{1,0:T(8,128)(2,1)S(1)} collective-permute-done((bf16[448,896]{1,0:T(8,128)(2,1)S(1)}, bf16[448,896]{1,0:T(8,128)(2,1)S(1)}, u32[]{:S(2)}, u32[]{:S(2)}) %collective-permute-start.16) | collective-permute-done | bytes 802848 | tf_op jit(solution)/shard_map/ppermute | solution.py:44
  60.8 1.1 %collective-permute-done.17.rest_5_ = bf16[448,896]{1,0:T(8,128)(2,1)S(1)} collective-permute-done((bf16[448,896]{1,0:T(8,128)(2,1)S(1)}, bf16[448,896]{1,0:T(8,128)(2,1)S(1)}, u32[]{:S(2)}, u32[]{:S(2)}) %collective-permute-start.17) | collective-permute-done | bytes 802848 | tf_op jit(solution)/shard_map/ppermute | solution.py:44
  62.0 1.1 %collective-permute-done.18.rest_6_ = bf16[448,896]{1,0:T(8,128)(2,1)S(1)} collective-permute-done((bf16[448,896]{1,0:T(8,128)(2,1)S(1)}, bf16[448,896]{1,0:T(8,128)(2,1)S(1)}, u32[]{:S(2)}, u32[]{:S(2)}) %collective-permute-start.18) | collective-permute-done | bytes 802848 | tf_op jit(solution)/shard_map/ppermute | solution.py:44
  63.1 1.1 %collective-permute-done.19.rest_7_ = bf16[448,896]{1,0:T(8,128)(2,1)S(1)} collective-permute-done((bf16[448,896]{1,0:T(8,128)(2,1)S(1)}, bf16[448,896]{1,0:T(8,128)(2,1)S(1)}, u32[]{:S(2)}, u32[]{:S(2)}) %collective-permute-start.19) | collective-permute-done | bytes 802848 | tf_op jit(solution)/shard_map/ppermute | solution.py:44
  64.3 5.2 %q_project.1.q_ref = bf16[512,896]{1,0:T(8,128)(2,1)S(1)} custom-call(s32[4]{0:T(128)S(1)} %pad_add_fusion.info_ref, bf16[512,3584]{1,0:T(8,128)(2,1)S(1)} %get-tuple-element.53.x_ref, f32[1,2304]{1,0:T(1,128)S(1)} %reshape.9.bias_ref, f32[512,128]{1,0:T(8,128)S(1)} %get-tuple-element.42.cos_ref, f32[512,128]{1,0:T(8,128)S(1)} %get-tuple-element.43.sin_ref, ...), custom_call_target="tpu_custom_call" | custom-call | flops 1 | bytes 1 | tf_op jit(solution)/shard_map/q_project/pallas_call | solution.py:276
  69.4 3.5 %attention_first.1 = (f32[1792,256]{1,0:T(8,128)S(1)}, f32[1792,128]{1,0:T(8,128)S(1)}) custom-call(s32[4]{0:T(128)S(1)} %pad_add_fusion.info_ref, s32[1,6]{1,0:T(1,128)S(1)} %copy-done.3, bf16[512,896]{1,0:T(8,128)(2,1)S(1)} %q_project.1.q_ref, bf16[512,256]{1,0:T(8,128)(2,1)S(1)} %collective-permute-done.15.kv2_ref, ...), custom_call_target="tpu_custom_call" | custom-call | flops 1 | bytes 1 | tf_op jit(solution)/shard_map/attention_first/pallas_call | solution.py:369
  72.9 2.0 %attention_last.1 = (bf16[128,896]{1,0:T(8,128)(2,1)S(1)}, bf16[128,896]{1,0:T(8,128)(2,1)S(1)}) custom-call(s32[4]{0:T(128)S(1)} %pad_add_fusion.info_ref, s32[1,6]{1,0:T(1,128)S(1)} %copy-done.3, bf16[512,896]{1,0:T(8,128)(2,1)S(1)} %q_project.1.q_ref, bf16[512,256]{1,0:T(8,128)(2,1)S(1)} %collective-permute-done.20.kv4_ref.kv_ref, ...), custom_call_target="tpu_custom_call" | custom-call | flops 1 | bytes 1 | tf_op jit(solution)/shard_map/attention_last/pallas_call | solution.py:448
  74.9 0.1 collective-permute-start.21
  75.0 3.2 %collective-permute-start.22 = (bf16[128,896]{1,0:T(8,128)(2,1)S(1)}, bf16[128,896]{1,0:T(8,128)(2,1)S(1)}, u32[]{:S(2)}, u32[]{:S(2)}) collective-permute-start(bf16[128,896]{1,0:T(8,128)(2,1)S(1)} %get-tuple-element.66), channel_id=1, source_target_pairs={{0,7},{1,0},{2,1},{3,2},{4,3},{5,4},{6,5},{7,6},{8,15},{9,8},{10,9... | collective-permute-start | bytes 688136 | tf_op jit(solution)/shard_map/ppermute | solution.py:44
  78.3 4.7 %attention_full.1 = (bf16[128,896]{1,0:T(8,128)(2,1)S(1)}, bf16[128,896]{1,0:T(8,128)(2,1)S(1)}) custom-call(s32[4]{0:T(128)S(1)} %pad_add_fusion.info_ref, s32[1,6]{1,0:T(1,128)S(1)} %copy-done.3, bf16[512,896]{1,0:T(8,128)(2,1)S(1)} %q_project.1.q_ref, bf16[512,256]{1,0:T(8,128)(2,1)S(1)} %collective-permute-done.20.kv4_ref.kv_ref, ...), custom_call_target="tpu_custom_call" | custom-call | flops 1 | bytes 1 | tf_op jit(solution)/shard_map/attention_full/pallas_call | solution.py:402
  83.0 0.9 %collective-permute-done.21.other_top_ref = bf16[128,896]{1,0:T(8,128)(2,1)S(1)} collective-permute-done((bf16[128,896]{1,0:T(8,128)(2,1)S(1)}, bf16[128,896]{1,0:T(8,128)(2,1)S(1)}, u32[]{:S(2)}, u32[]{:S(2)}) %collective-permute-start.21) | collective-permute-done | bytes 229408 | tf_op jit(solution)/shard_map/ppermute | solution.py:44
  83.9 1.5 %output.1 = bf16[256,1792]{1,0:T(8,128)(2,1)} custom-call(s32[4]{0:T(128)S(1)} %pad_add_fusion.info_ref, bf16[128,896]{1,0:T(8,128)(2,1)S(1)} %get-tuple-element.61.own_top_ref, bf16[128,896]{1,0:T(8,128)(2,1)S(1)} %get-tuple-element.62.own_low_ref, bf16[128,896]{1,0:T(8,128)(2,1)S(1)} %collective-permute-done.21.other_top_ref, ...), custom_call_target="tpu_custom_call" | custom-call | flops 1 | bytes 1 | tf_op jit(solution)/shard_map/output/pallas_call | solution.py:137
  (22 shorter events, 0.1 us)
Async XLA Ops:
  0.0 1.5 %copy-start = (bf16[256,3584]{1,0:T(8,128)(2,1)S(1)}, bf16[256,3584]{1,0:T(8,128)(2,1)}, u32[]{:S(2)}) copy-start(bf16[256,3584]{1,0:T(8,128)(2,1)} %hidden_ref.1) | copy-start | bytes 5505028
  1.5 0.7 copy-start.2
  2.2 7.4 %copy-start.1 = (bf16[112,2304]{1,0:T(8,128)(2,1)S(1)}, bf16[112,2304]{1,0:T(8,128)(2,1)}, u32[]{:S(2)}) copy-start(bf16[112,2304]{1,0:T(8,128)(2,1)} %weight_ref.1) | copy-start | bytes 1548292
  2.2 32.1 %copy-start.3 = (s32[1,6]{1,0:T(1,128)S(1)}, s32[1,6]{1,0:T(1,128)}, u32[]{:S(2)}) copy-start(s32[1,6]{1,0:T(1,128)} %lengths_ref.7) | copy-start | bytes 76
  2.2 36.0 %copy-start.4 = (f32[2304]{0:T(1024)S(1)}, f32[2304]{0:T(1024)}, u32[]{:S(2)}) copy-start(f32[2304]{0:T(1024)} %param.8) | copy-start | bytes 27652
  3.5 32.6 %collective-permute-start.6 = (bf16[128,3584]{1,0:T(8,128)(2,1)S(1)}, bf16[128,3584]{1,0:T(8,128)(2,1)S(1)}, u32[]{:S(2)}, u32[]{:S(2)}) collective-permute-start(bf16[128,3584]{1,0:T(8,128)(2,1)S(1)} %get-tuple-element.47.rest_2_), channel_id=1, source_target_pairs={{0,1},{1,2},{2,3},{3,4},{4,5},{5,6},{6,7},{7,0},{8,9},{9,10},{10,1... | collective-permute-start | bytes 2752520 | tf_op jit(solution)/shard_map/ppermute | solution.py:44
  5.5 30.7 %collective-permute-start.7 = (bf16[128,3584]{1,0:T(8,128)(2,1)S(1)}, bf16[128,3584]{1,0:T(8,128)(2,1)}, u32[]{:S(2)}, u32[]{:S(2)}) collective-permute-start(bf16[128,3584]{1,0:T(8,128)(2,1)S(1)} %get-tuple-element.46.rest_1_), channel_id=1, source_target_pairs={{0,7},{1,0},{2,1},{3,2},{4,3},{5,4},{6,5},{7,6},{8,15},{9,8},{10,9... | collective-permute-start | bytes 2752520 | tf_op jit(solution)/shard_map/ppermute | solution.py:44
  10.2 6.4 %collective-permute-start = (bf16[112,1152]{1,0:T(8,128)(2,1)S(1)}, bf16[112,1152]{1,0:T(8,128)(2,1)S(1)}, u32[]{:S(2)}, u32[]{:S(2)}) collective-permute-start(bf16[112,1152]{1,0:T(8,128)(2,1)S(1)} %cut.1.refs_0_), channel_id=1, source_target_pairs={{0,16},{8,72},{16,32},{24,88},{32,48},{40,104},{48,0},{56,120},{64... | collective-permute-start | bytes 774152 | tf_op jit(solution)/shard_map/ppermute | solution.py:54
  10.8 10.3 %collective-permute-start.1 = (bf16[112,1152]{1,0:T(8,128)(2,1)S(1)}, bf16[112,1152]{1,0:T(8,128)(2,1)S(1)}, u32[]{:S(2)}, u32[]{:S(2)}) collective-permute-start(bf16[112,1152]{1,0:T(8,128)(2,1)S(1)} %cut.1.refs_0_), channel_id=1, source_target_pairs={{0,48},{8,200},{16,0},{24,216},{32,16},{40,232},{48,32},{56,248},{... | collective-permute-start | bytes 774152 | tf_op jit(solution)/shard_map/ppermute | solution.py:54
  12.4 8.8 %collective-permute-start.2 = (bf16[112,1152]{1,0:T(8,128)(2,1)S(1)}, bf16[112,1152]{1,0:T(8,128)(2,1)S(1)}, u32[]{:S(2)}, u32[]{:S(2)}) collective-permute-start(bf16[112,1152]{1,0:T(8,128)(2,1)S(1)} %cut.1.refs_0_), channel_id=1, source_target_pairs={{0,32},{8,136},{16,48},{24,152},{32,0},{40,168},{48,16},{56,184},{... | collective-permute-start | bytes 774152 | tf_op jit(solution)/shard_map/ppermute | solution.py:54
  21.2 7.3 %collective-permute-start.3 = (bf16[448,256]{1,0:T(8,128)(2,1)S(1)}, bf16[448,256]{1,0:T(8,128)(2,1)S(1)}, u32[]{:S(2)}, u32[]{:S(2)}) collective-permute-start(bf16[448,256]{1,0:T(8,128)(2,1)S(1)} %get-tuple-element.49.rest_4_), channel_id=1, source_target_pairs={{0,64},{8,24},{16,80},{24,40},{32,96},{40,56},{48,112},{56,8},{64,... | collective-permute-start | bytes 688136 | tf_op jit(solution)/shard_map/ppermute | solution.py:54
  22.8 6.0 %collective-permute-start.4 = (bf16[448,256]{1,0:T(8,128)(2,1)S(1)}, bf16[448,256]{1,0:T(8,128)(2,1)S(1)}, u32[]{:S(2)}, u32[]{:S(2)}) collective-permute-start(bf16[448,256]{1,0:T(8,128)(2,1)S(1)} %get-tuple-element.49.rest_4_), channel_id=1, source_target_pairs={{0,192},{8,56},{16,208},{24,8},{32,224},{40,24},{48,240},{56,40},{... | collective-permute-start | bytes 688136 | tf_op jit(solution)/shard_map/ppermute | solution.py:54
  24.5 9.7 %collective-permute-start.5 = (bf16[448,256]{1,0:T(8,128)(2,1)S(1)}, bf16[448,256]{1,0:T(8,128)(2,1)S(1)}, u32[]{:S(2)}, u32[]{:S(2)}) collective-permute-start(bf16[448,256]{1,0:T(8,128)(2,1)S(1)} %get-tuple-element.49.rest_4_), channel_id=1, source_target_pairs={{0,128},{8,40},{16,144},{24,56},{32,160},{40,8},{48,176},{56,24},{... | collective-permute-start | bytes 688136 | tf_op jit(solution)/shard_map/ppermute | solution.py:54
  28.5 13.9 %collective-permute-start.12 = (bf16[448,896]{1,0:T(8,128)(2,1)S(1)}, bf16[448,896]{1,0:T(8,128)(2,1)S(1)}, u32[]{:S(2)}, u32[]{:S(2)}) collective-permute-start(bf16[448,896]{1,0:T(8,128)(2,1)S(1)} %get-tuple-element.56.rest_0_), channel_id=1, source_target_pairs={{0,64},{8,24},{16,80},{24,40},{32,96},{40,56},{48,112},{56,8},{64,... | collective-permute-start | bytes 2408456 | tf_op jit(solution)/shard_map/ppermute | solution.py:54
  28.9 23.6 %collective-permute-start.13 = (bf16[448,896]{1,0:T(8,128)(2,1)S(1)}, bf16[448,896]{1,0:T(8,128)(2,1)S(1)}, u32[]{:S(2)}, u32[]{:S(2)}) collective-permute-start(bf16[448,896]{1,0:T(8,128)(2,1)S(1)} %get-tuple-element.56.rest_0_), channel_id=1, source_target_pairs={{0,192},{8,56},{16,208},{24,8},{32,224},{40,24},{48,240},{56,40},{... | collective-permute-start | bytes 2408456 | tf_op jit(solution)/shard_map/ppermute | solution.py:54
  34.2 18.3 %collective-permute-start.14 = (bf16[448,896]{1,0:T(8,128)(2,1)S(1)}, bf16[448,896]{1,0:T(8,128)(2,1)S(1)}, u32[]{:S(2)}, u32[]{:S(2)}) collective-permute-start(bf16[448,896]{1,0:T(8,128)(2,1)S(1)} %get-tuple-element.56.rest_0_), channel_id=1, source_target_pairs={{0,128},{8,40},{16,144},{24,56},{32,160},{40,8},{48,176},{56,24},{... | collective-permute-start | bytes 2408456 | tf_op jit(solution)/shard_map/ppermute | solution.py:54
  36.1 1.6 %collective-permute-start.10 = (bf16[448,256]{1,0:T(8,128)(2,1)S(1)}, bf16[448,256]{1,0:T(8,128)(2,1)S(1)}, u32[]{:S(2)}, u32[]{:S(2)}) collective-permute-start(bf16[448,256]{1,0:T(8,128)(2,1)S(1)} %collective-permute-done.4.rest_6_), channel_id=1, source_target_pairs={{0,8},{8,0},{1,9},{9,1},{2,10},{10,2},{3,11},{11,3},{4,12},{12,4},... | collective-permute-start | bytes 688136 | tf_op jit(solution)/shard_map/ppermute | solution.py:44
  36.2 1.8 %collective-permute-start.8 = (bf16[448,256]{1,0:T(8,128)(2,1)S(1)}, bf16[448,256]{1,0:T(8,128)(2,1)S(1)}, u32[]{:S(2)}, u32[]{:S(2)}) collective-permute-start(bf16[448,256]{1,0:T(8,128)(2,1)S(1)} %get-tuple-element.49.rest_4_), channel_id=1, source_target_pairs={{0,8},{8,0},{1,9},{9,1},{2,10},{10,2},{3,11},{11,3},{4,12},{12,4},... | collective-permute-start | bytes 688136 | tf_op jit(solution)/shard_map/ppermute | solution.py:44
  37.7 1.5 %collective-permute-start.9 = (bf16[448,256]{1,0:T(8,128)(2,1)S(1)}, bf16[448,256]{1,0:T(8,128)(2,1)S(1)}, u32[]{:S(2)}, u32[]{:S(2)}) collective-permute-start(bf16[448,256]{1,0:T(8,128)(2,1)S(1)} %collective-permute-done.3.rest_5_), channel_id=1, source_target_pairs={{0,8},{8,0},{1,9},{9,1},{2,10},{10,2},{3,11},{11,3},{4,12},{12,4},... | collective-permute-start | bytes 688136 | tf_op jit(solution)/shard_map/ppermute | solution.py:44
  38.0 1.5 %collective-permute-start.11 = (bf16[448,256]{1,0:T(8,128)(2,1)S(1)}, bf16[448,256]{1,0:T(8,128)(2,1)S(1)}, u32[]{:S(2)}, u32[]{:S(2)}) collective-permute-start(bf16[448,256]{1,0:T(8,128)(2,1)S(1)} %collective-permute-done.5.rest_7_), channel_id=1, source_target_pairs={{0,8},{8,0},{1,9},{9,1},{2,10},{10,2},{3,11},{11,3},{4,12},{12,4},... | collective-permute-start | bytes 688136 | tf_op jit(solution)/shard_map/ppermute | solution.py:44
  42.1 16.4 %collective-permute-start.15 = (bf16[512,256]{1,0:T(8,128)(2,1)S(1)}, bf16[512,256]{1,0:T(8,128)(2,1)S(1)}, u32[]{:S(2)}, u32[]{:S(2)}) collective-permute-start(bf16[512,256]{1,0:T(8,128)(2,1)S(1)} %get-tuple-element.55.kv0_ref), channel_id=1, source_target_pairs={{0,2},{1,3},{2,4},{3,5},{4,6},{5,7},{6,0},{7,1},{8,10},{9,11},{10,... | collective-permute-start | bytes 786440 | tf_op jit(solution)/shard_map/ppermute | solution.py:44
  58.5 2.3 %collective-permute-start.16 = (bf16[448,896]{1,0:T(8,128)(2,1)S(1)}, bf16[448,896]{1,0:T(8,128)(2,1)S(1)}, u32[]{:S(2)}, u32[]{:S(2)}) collective-permute-start(bf16[448,896]{1,0:T(8,128)(2,1)S(1)} %get-tuple-element.56.rest_0_), channel_id=1, source_target_pairs={{0,8},{8,0},{1,9},{9,1},{2,10},{10,2},{3,11},{11,3},{4,12},{12,4},... | collective-permute-start | bytes 2408456 | tf_op jit(solution)/shard_map/ppermute | solution.py:44
  58.5 3.5 %collective-permute-start.17 = (bf16[448,896]{1,0:T(8,128)(2,1)S(1)}, bf16[448,896]{1,0:T(8,128)(2,1)S(1)}, u32[]{:S(2)}, u32[]{:S(2)}) collective-permute-start(bf16[448,896]{1,0:T(8,128)(2,1)S(1)} %collective-permute-done.12.rest_1_), channel_id=1, source_target_pairs={{0,8},{8,0},{1,9},{9,1},{2,10},{10,2},{3,11},{11,3},{4,12},{12,4},... | collective-permute-start | bytes 2408456 | tf_op jit(solution)/shard_map/ppermute | solution.py:44
  59.0 4.1 %collective-permute-start.18 = (bf16[448,896]{1,0:T(8,128)(2,1)S(1)}, bf16[448,896]{1,0:T(8,128)(2,1)S(1)}, u32[]{:S(2)}, u32[]{:S(2)}) collective-permute-start(bf16[448,896]{1,0:T(8,128)(2,1)S(1)} %collective-permute-done.13.rest_2_), channel_id=1, source_target_pairs={{0,8},{8,0},{1,9},{9,1},{2,10},{10,2},{3,11},{11,3},{4,12},{12,4},... | collective-permute-start | bytes 2408456 | tf_op jit(solution)/shard_map/ppermute | solution.py:44
  59.0 5.2 %collective-permute-start.19 = (bf16[448,896]{1,0:T(8,128)(2,1)S(1)}, bf16[448,896]{1,0:T(8,128)(2,1)S(1)}, u32[]{:S(2)}, u32[]{:S(2)}) collective-permute-start(bf16[448,896]{1,0:T(8,128)(2,1)S(1)} %collective-permute-done.14.rest_3_), channel_id=1, source_target_pairs={{0,8},{8,0},{1,9},{9,1},{2,10},{10,2},{3,11},{11,3},{4,12},{12,4},... | collective-permute-start | bytes 2408456 | tf_op jit(solution)/shard_map/ppermute | solution.py:44
  59.5 13.4 %collective-permute-start.20 = (bf16[512,256]{1,0:T(8,128)(2,1)S(1)}, bf16[512,256]{1,0:T(8,128)(2,1)S(1)}, u32[]{:S(2)}, u32[]{:S(2)}) collective-permute-start(bf16[512,256]{1,0:T(8,128)(2,1)S(1)} %collective-permute-done.15.kv2_ref), channel_id=1, source_target_pairs={{0,2},{1,3},{2,4},{3,5},{4,6},{5,7},{6,0},{7,1},{8,10},{9,11},{10,... | collective-permute-start | bytes 786440 | tf_op jit(solution)/shard_map/ppermute | solution.py:44
  74.9 8.9 %collective-permute-start.21 = (bf16[128,896]{1,0:T(8,128)(2,1)S(1)}, bf16[128,896]{1,0:T(8,128)(2,1)S(1)}, u32[]{:S(2)}, u32[]{:S(2)}) collective-permute-start(bf16[128,896]{1,0:T(8,128)(2,1)S(1)} %get-tuple-element.65), channel_id=1, source_target_pairs={{0,1},{1,2},{2,3},{3,4},{4,5},{5,6},{6,7},{7,0},{8,9},{9,10},{10,1... | collective-permute-start | bytes 688136 | tf_op jit(solution)/shard_map/ppermute | solution.py:44
  75.0 8.8 %collective-permute-start.22 = (bf16[128,896]{1,0:T(8,128)(2,1)S(1)}, bf16[128,896]{1,0:T(8,128)(2,1)S(1)}, u32[]{:S(2)}, u32[]{:S(2)}) collective-permute-start(bf16[128,896]{1,0:T(8,128)(2,1)S(1)} %get-tuple-element.66), channel_id=1, source_target_pairs={{0,7},{1,0},{2,1},{3,2},{4,3},{5,4},{6,5},{7,6},{8,15},{9,8},{10,9... | collective-permute-start | bytes 688136 | tf_op jit(solution)/shard_map/ppermute | solution.py:44

commit v4 on v3

--- a/solution.py
+++ b/solution.py
@@ -471,6 +471,8 @@
     own = cut(info, qkv_weight)
     blocks = [own, hop(own, 0, 1), hop(own, 0, -1), hop(own, 0, 2)]
     low, high = norm(hidden, norm_gain)
+    cosine, sine = tables(info, repo_lengths, freq)
+    blocks[3], cosine, sine = lax.optimization_barrier((blocks[3], cosine, sine))
     kv_row, q_row = split(blocks)
     before = ring(high, "ctx", 1)
     after = ring(low, "ctx", -1)
@@ -478,8 +480,6 @@
     kv_row, low, high = lax.optimization_barrier((kv_row, low, high))
     kv_near = [kv_row, hop(kv_row, 1, 1), hop(kv_row, 1, -1), hop(kv_row, 1, 2)]
     q_near = [q_row, hop(q_row, 1, 1), hop(q_row, 1, -1), hop(q_row, 1, 2)]
-    cosine, sine = tables(info, repo_lengths, freq)
-    *kv_near, cosine, sine = lax.optimization_barrier((*kv_near, cosine, sine))
     kv_near[3], before, after = lax.optimization_barrier((kv_near[3], before, after))
     kv_far = [ring(piece, "core", 1) for piece in kv_near]
     kv0, normed = kv_project(info, (before, low, high, after), kv_near, kv_far, bias, cosine, sine)

time: 86.6 us -> 84.8 us (0.979)
    ppermute x14, waiting for transfers between devices: 14.2 us -> 12.8 us  [ring(): return lax.ppermute(value, axis, [(i, (i + step) % n) for i in range(n)])]
    ppermute x9, waiting for transfers between devices: 19.4 us -> 20.5 us  [hop(): return lax.ppermute(value, ('y', 'x', 'core'), pairs)]
  transfers between devices with their start and end apart: 23 -> 23, of which waited for: 14 -> 17; matrix products, arithmetic and copies ran while one was open for 0% -> 0% of each run, Pallas kernels for 22% -> 22%
where the time goes in v4:
time: 84.8 us; the launch traced here: 84.6 us
  waiting for transfers between devices  33.3 us (39%)
  starting transfers between devices  25.3 us (30%)
  Pallas kernels  23.3 us (27%)
  local copies, waits for them, and re-layouts  2.25 us (3%)
    ppermute x9, waiting for transfers between devices, hop(): return lax.ppermute(value, ('y', 'x', 'core'), pairs)  20.5 us
    ppermute x9, starting transfers between devices, hop(): return lax.ppermute(value, ('y', 'x', 'core'), pairs)  13.9 us
    ppermute x14, waiting for transfers between devices, ring(): return lax.ppermute(value, axis, [(i, (i + step) % n) for i in range(n)])  12.8 us
    ppermute x14, starting transfers between devices, ring(): return lax.ppermute(value, axis, [(i, (i + step) % n) for i in range(n)])  11.4 us
    pallas_call x1, Pallas kernels, q_project(): pl.pallas_call(functools.partial(q_kernel, count), out_shape=jax.ShapeDty...  5.15 us
    pallas_call x1, Pallas kernels, attention_full(): pl.pallas_call(functools.partial(full_kernel, tiles), out_shape=[jax.Shap...  4.68 us
    pallas_call x1, Pallas kernels, attention_first(): pl.pallas_call(functools.partial(first_kernel, tiles), out_shape=[jax.Sha...  3.47 us
    pallas_call x1, Pallas kernels, kv_project(): pl.pallas_call(functools.partial(kv_kernel, count), out_shape=[jax.ShapeD...  2.64 us
  transfers between devices with their start and end apart: 23, of which 17 were waited for; matrix products, arithmetic and copies ran while one was open for 0% of the time, Pallas kernels for 22%

profile of v4, /device:TPU:6, one launch (start us, length us, event | category | flops | bytes accessed | tf_op | source)
XLA Modules:
  0.0 84.6 jit_solution(17957595374195352587)
XLA Ops:
  0.0 1.5 %copy-done = bf16[256,3584]{1,0:T(8,128)(2,1)S(1)} copy-done((bf16[256,3584]{1,0:T(8,128)(2,1)S(1)}, bf16[256,3584]{1,0:T(8,128)(2,1)}, u32[]{:S(2)}) %copy-start) | copy-done | bytes 1835032
  1.5 0.7 copy-done.2
  2.2 1.3 %norm.1 = (bf16[128,3584]{1,0:T(8,128)(2,1)S(1)}, bf16[128,3584]{1,0:T(8,128)(2,1)S(1)}) custom-call(bf16[256,3584]{1,0:T(8,128)(2,1)S(1)} %copy-done, f32[28,128]{1,0:T(8,128)S(1)} %bitcast.7), custom_call_target="tpu_custom_call" | custom-call | flops 1 | bytes 1 | tf_op jit(solution)/shard_map/norm/pallas_call | solution.py:185
  3.5 2.0 %collective-permute-start.4 = (bf16[128,3584]{1,0:T(8,128)(2,1)S(1)}, bf16[128,3584]{1,0:T(8,128)(2,1)S(1)}, u32[]{:S(2)}, u32[]{:S(2)}) collective-permute-start(bf16[128,3584]{1,0:T(8,128)(2,1)S(1)} %get-tuple-element.44.rest_2_), channel_id=1, source_target_pairs={{0,1},{1,2},{2,3},{3,4},{4,5},{5,6},{6,7},{7,0},{8,9},{9,10},{10,1... | collective-permute-start | bytes 2752520 | tf_op jit(solution)/shard_map/ppermute | solution.py:44
  5.5 4.0 %collective-permute-start.5 = (bf16[128,3584]{1,0:T(8,128)(2,1)S(1)}, bf16[128,3584]{1,0:T(8,128)(2,1)}, u32[]{:S(2)}, u32[]{:S(2)}) collective-permute-start(bf16[128,3584]{1,0:T(8,128)(2,1)S(1)} %get-tuple-element.43.rest_1_), channel_id=1, source_target_pairs={{0,7},{1,0},{2,1},{3,2},{4,3},{5,4},{6,5},{7,6},{8,15},{9,8},{10,9... | collective-permute-start | bytes 2752520 | tf_op jit(solution)/shard_map/ppermute | solution.py:44
  9.6 0.1 pad_add_fusion.info_ref
  9.6 0.6 cut.1.refs_0_
  10.3 1.5 %collective-permute-start = (bf16[112,1152]{1,0:T(8,128)(2,1)S(1)}, bf16[112,1152]{1,0:T(8,128)(2,1)S(1)}, u32[]{:S(2)}, u32[]{:S(2)}) collective-permute-start(bf16[112,1152]{1,0:T(8,128)(2,1)S(1)} %cut.1.refs_0_), channel_id=1, source_target_pairs={{0,32},{8,136},{16,48},{24,152},{32,0},{40,168},{48,16},{56,184},{... | collective-permute-start | bytes 774152 | tf_op jit(solution)/shard_map/ppermute | solution.py:54
  11.8 2.1 %collective-permute-start.1 = (bf16[112,1152]{1,0:T(8,128)(2,1)S(1)}, bf16[112,1152]{1,0:T(8,128)(2,1)S(1)}, u32[]{:S(2)}, u32[]{:S(2)}) collective-permute-start(bf16[112,1152]{1,0:T(8,128)(2,1)S(1)} %cut.1.refs_0_), channel_id=1, source_target_pairs={{0,16},{8,72},{16,32},{24,88},{32,48},{40,104},{48,0},{56,120},{64... | collective-permute-start | bytes 774152 | tf_op jit(solution)/shard_map/ppermute | solution.py:54
  13.9 0.1 maximum_bitcast_fusion.freq_ref
  13.9 1.8 %tables.1 = (f32[512,128]{1,0:T(8,128)S(1)}, f32[512,128]{1,0:T(8,128)S(1)}) custom-call(s32[4]{0:T(128)S(1)} %pad_add_fusion.info_ref, s32[1,6]{1,0:T(1,128)S(1)} %copy-done.3, f32[1,128]{1,0:T(1,128)S(1)} %maximum_bitcast_fusion.freq_ref), custom_call_target="tpu_custom_call" | custom-call | flops 1 | bytes 1 | tf_op jit(solution)/shard_map/tables/pallas_call | solution.py:210
  15.8 2.4 %collective-permute-done.refs_3_ = bf16[112,1152]{1,0:T(8,128)(2,1)S(1)} collective-permute-done((bf16[112,1152]{1,0:T(8,128)(2,1)S(1)}, bf16[112,1152]{1,0:T(8,128)(2,1)S(1)}, u32[]{:S(2)}, u32[]{:S(2)}) %collective-permute-start) | collective-permute-done | bytes 258080 | tf_op jit(solution)/shard_map/ppermute | solution.py:54
  18.2 0.6 collective-permute-done.1.refs_1_
  18.8 2.6 %collective-permute-done.2.refs_2_ = bf16[112,1152]{1,0:T(8,128)(2,1)S(1)} collective-permute-done((bf16[112,1152]{1,0:T(8,128)(2,1)S(1)}, bf16[112,1152]{1,0:T(8,128)(2,1)S(1)}, u32[]{:S(2)}, u32[]{:S(2)}) %collective-permute-start.2) | collective-permute-done | bytes 258080 | tf_op jit(solution)/shard_map/ppermute | solution.py:54
  21.5 3.3 %collective-permute-start.3 = (bf16[448,256]{1,0:T(8,128)(2,1)S(1)}, bf16[448,256]{1,0:T(8,128)(2,1)S(1)}, u32[]{:S(2)}, u32[]{:S(2)}) collective-permute-start(bf16[448,256]{1,0:T(8,128)(2,1)S(1)} %get-tuple-element.41.rest_4_), channel_id=1, source_target_pairs={{0,128},{8,40},{16,144},{24,56},{32,160},{40,8},{48,176},{56,24},{... | collective-permute-start | bytes 688136 | tf_op jit(solution)/shard_map/ppermute | solution.py:54
  24.8 1.1 %collective-permute-start.7 = (bf16[448,256]{1,0:T(8,128)(2,1)S(1)}, bf16[448,256]{1,0:T(8,128)(2,1)S(1)}, u32[]{:S(2)}, u32[]{:S(2)}) collective-permute-start(bf16[448,256]{1,0:T(8,128)(2,1)S(1)} %get-tuple-element.41.rest_4_), channel_id=1, source_target_pairs={{0,192},{8,56},{16,208},{24,8},{32,224},{40,24},{48,240},{56,40},{... | collective-permute-start | bytes 688136 | tf_op jit(solution)/shard_map/ppermute | solution.py:54
  25.8 1.0 %collective-permute-start.6 = (bf16[448,256]{1,0:T(8,128)(2,1)S(1)}, bf16[448,256]{1,0:T(8,128)(2,1)S(1)}, u32[]{:S(2)}, u32[]{:S(2)}) collective-permute-start(bf16[448,256]{1,0:T(8,128)(2,1)S(1)} %get-tuple-element.41.rest_4_), channel_id=1, source_target_pairs={{0,64},{8,24},{16,80},{24,40},{32,96},{40,56},{48,112},{56,8},{64,... | collective-permute-start | bytes 688136 | tf_op jit(solution)/shard_map/ppermute | solution.py:54
  26.8 2.3 %collective-permute-done.3.rest_7_ = bf16[448,256]{1,0:T(8,128)(2,1)S(1)} collective-permute-done((bf16[448,256]{1,0:T(8,128)(2,1)S(1)}, bf16[448,256]{1,0:T(8,128)(2,1)S(1)}, u32[]{:S(2)}, u32[]{:S(2)}) %collective-permute-start.3) | collective-permute-done | bytes 229408 | tf_op jit(solution)/shard_map/ppermute | solution.py:54
  29.1 1.7 %collective-permute-start.12 = (bf16[448,896]{1,0:T(8,128)(2,1)S(1)}, bf16[448,896]{1,0:T(8,128)(2,1)S(1)}, u32[]{:S(2)}, u32[]{:S(2)}) collective-permute-start(bf16[448,896]{1,0:T(8,128)(2,1)S(1)} %get-tuple-element.50.rest_0_), channel_id=1, source_target_pairs={{0,64},{8,24},{16,80},{24,40},{32,96},{40,56},{48,112},{56,8},{64,... | collective-permute-start | bytes 2408456 | tf_op jit(solution)/shard_map/ppermute | solution.py:54
  30.8 1.1 %collective-permute-done.7.rest_6_ = bf16[448,256]{1,0:T(8,128)(2,1)S(1)} collective-permute-done((bf16[448,256]{1,0:T(8,128)(2,1)S(1)}, bf16[448,256]{1,0:T(8,128)(2,1)S(1)}, u32[]{:S(2)}, u32[]{:S(2)}) %collective-permute-start.7) | collective-permute-done | bytes 229408 | tf_op jit(solution)/shard_map/ppermute | solution.py:54
  31.9 2.7 %collective-permute-start.13 = (bf16[448,896]{1,0:T(8,128)(2,1)S(1)}, bf16[448,896]{1,0:T(8,128)(2,1)S(1)}, u32[]{:S(2)}, u32[]{:S(2)}) collective-permute-start(bf16[448,896]{1,0:T(8,128)(2,1)S(1)} %get-tuple-element.50.rest_0_), channel_id=1, source_target_pairs={{0,192},{8,56},{16,208},{24,8},{32,224},{40,24},{48,240},{56,40},{... | collective-permute-start | bytes 2408456 | tf_op jit(solution)/shard_map/ppermute | solution.py:54
  34.6 0.6 collective-permute-start.14
  35.2 0.5 collective-permute-start.10
  35.7 1.0 %collective-permute-done.8.rest_8_ = bf16[448,256]{1,0:T(8,128)(2,1)S(1)} collective-permute-done((bf16[448,256]{1,0:T(8,128)(2,1)S(1)}, bf16[448,256]{1,0:T(8,128)(2,1)S(1)}, u32[]{:S(2)}, u32[]{:S(2)}) %collective-permute-start.8) | collective-permute-done | bytes 229408 | tf_op jit(solution)/shard_map/ppermute | solution.py:44
  36.7 0.1 collective-permute-start.9
  36.8 0.2 collective-permute-done.10.rest_10_
  37.0 0.2 collective-permute-start.11
  37.2 1.0 %collective-permute-done.9.rest_9_ = bf16[448,256]{1,0:T(8,128)(2,1)S(1)} collective-permute-done((bf16[448,256]{1,0:T(8,128)(2,1)S(1)}, bf16[448,256]{1,0:T(8,128)(2,1)S(1)}, u32[]{:S(2)}, u32[]{:S(2)}) %collective-permute-start.9) | collective-permute-done | bytes 229408 | tf_op jit(solution)/shard_map/ppermute | solution.py:44
  38.2 0.3 collective-permute-done.11.rest_11_
  38.5 2.6 %kv_project.1 = (bf16[512,256]{1,0:T(8,128)(2,1)S(1)}, bf16[512,3584]{1,0:T(8,128)(2,1)S(1)}) custom-call(s32[4]{0:T(128)S(1)} %pad_add_fusion.info_ref, f32[1,2304]{1,0:T(1,128)S(1)} %reshape.9.bias_ref, f32[512,128]{1,0:T(8,128)S(1)} %get-tuple-element.35.cos_ref, f32[512,128]{1,0:T(8,128)S(1)} %get-tuple-element.36.sin_ref, ...), custom_call_target="tpu_custom_call" | custom-call | flops 1 | bytes 1 | tf_op jit(solution)/shard_map/kv_project/pallas_call | solution.py:247
  41.1 0.3 collective-permute-start.15
  41.4 1.0 %collective-permute-done.12.rest_1_ = bf16[448,896]{1,0:T(8,128)(2,1)S(1)} collective-permute-done((bf16[448,896]{1,0:T(8,128)(2,1)S(1)}, bf16[448,896]{1,0:T(8,128)(2,1)S(1)}, u32[]{:S(2)}, u32[]{:S(2)}) %collective-permute-start.12) | collective-permute-done | bytes 802848 | tf_op jit(solution)/shard_map/ppermute | solution.py:54
  42.5 10.4 %collective-permute-done.13.rest_2_ = bf16[448,896]{1,0:T(8,128)(2,1)S(1)} collective-permute-done((bf16[448,896]{1,0:T(8,128)(2,1)S(1)}, bf16[448,896]{1,0:T(8,128)(2,1)S(1)}, u32[]{:S(2)}, u32[]{:S(2)}) %collective-permute-start.13) | collective-permute-done | bytes 802848 | tf_op jit(solution)/shard_map/ppermute | solution.py:54
  52.9 4.6 %collective-permute-done.15.kv2_ref = bf16[512,256]{1,0:T(8,128)(2,1)S(1)} collective-permute-done((bf16[512,256]{1,0:T(8,128)(2,1)S(1)}, bf16[512,256]{1,0:T(8,128)(2,1)S(1)}, u32[]{:S(2)}, u32[]{:S(2)}) %collective-permute-start.15) | collective-permute-done | bytes 262176 | tf_op jit(solution)/shard_map/ppermute | solution.py:44
  57.5 0.5 collective-permute-start.17
  58.0 0.5 collective-permute-start.19
  58.5 1.3 %collective-permute-done.16.rest_4_ = bf16[448,896]{1,0:T(8,128)(2,1)S(1)} collective-permute-done((bf16[448,896]{1,0:T(8,128)(2,1)S(1)}, bf16[448,896]{1,0:T(8,128)(2,1)S(1)}, u32[]{:S(2)}, u32[]{:S(2)}) %collective-permute-start.16) | collective-permute-done | bytes 802848 | tf_op jit(solution)/shard_map/ppermute | solution.py:44
  59.8 1.1 %collective-permute-done.17.rest_5_ = bf16[448,896]{1,0:T(8,128)(2,1)S(1)} collective-permute-done((bf16[448,896]{1,0:T(8,128)(2,1)S(1)}, bf16[448,896]{1,0:T(8,128)(2,1)S(1)}, u32[]{:S(2)}, u32[]{:S(2)}) %collective-permute-start.17) | collective-permute-done | bytes 802848 | tf_op jit(solution)/shard_map/ppermute | solution.py:44
  61.0 1.1 %collective-permute-done.18.rest_6_ = bf16[448,896]{1,0:T(8,128)(2,1)S(1)} collective-permute-done((bf16[448,896]{1,0:T(8,128)(2,1)S(1)}, bf16[448,896]{1,0:T(8,128)(2,1)S(1)}, u32[]{:S(2)}, u32[]{:S(2)}) %collective-permute-start.18) | collective-permute-done | bytes 802848 | tf_op jit(solution)/shard_map/ppermute | solution.py:44
  62.1 1.1 %collective-permute-done.19.rest_7_ = bf16[448,896]{1,0:T(8,128)(2,1)S(1)} collective-permute-done((bf16[448,896]{1,0:T(8,128)(2,1)S(1)}, bf16[448,896]{1,0:T(8,128)(2,1)S(1)}, u32[]{:S(2)}, u32[]{:S(2)}) %collective-permute-start.19) | collective-permute-done | bytes 802848 | tf_op jit(solution)/shard_map/ppermute | solution.py:44
  63.3 5.2 %q_project.1.q_ref = bf16[512,896]{1,0:T(8,128)(2,1)S(1)} custom-call(s32[4]{0:T(128)S(1)} %pad_add_fusion.info_ref, bf16[512,3584]{1,0:T(8,128)(2,1)S(1)} %get-tuple-element.47.x_ref, f32[1,2304]{1,0:T(1,128)S(1)} %reshape.9.bias_ref, f32[512,128]{1,0:T(8,128)S(1)} %get-tuple-element.35.cos_ref, f32[512,128]{1,0:T(8,128)S(1)} %get-tuple-element.36.sin_ref, ...), custom_call_target="tpu_custom_call" | custom-call | flops 1 | bytes 1 | tf_op jit(solution)/shard_map/q_project/pallas_call | solution.py:276
  68.4 3.5 %attention_first.1 = (f32[1792,256]{1,0:T(8,128)S(1)}, f32[1792,128]{1,0:T(8,128)S(1)}) custom-call(s32[4]{0:T(128)S(1)} %pad_add_fusion.info_ref, s32[1,6]{1,0:T(1,128)S(1)} %copy-done.3, bf16[512,896]{1,0:T(8,128)(2,1)S(1)} %q_project.1.q_ref, bf16[512,256]{1,0:T(8,128)(2,1)S(1)} %collective-permute-done.15.kv2_ref, ...), custom_call_target="tpu_custom_call" | custom-call | flops 1 | bytes 1 | tf_op jit(solution)/shard_map/attention_first/pallas_call | solution.py:369
  71.9 2.0 %attention_last.1 = (bf16[128,896]{1,0:T(8,128)(2,1)S(1)}, bf16[128,896]{1,0:T(8,128)(2,1)S(1)}) custom-call(s32[4]{0:T(128)S(1)} %pad_add_fusion.info_ref, s32[1,6]{1,0:T(1,128)S(1)} %copy-done.3, bf16[512,896]{1,0:T(8,128)(2,1)S(1)} %q_project.1.q_ref, bf16[512,256]{1,0:T(8,128)(2,1)S(1)} %collective-permute-done.20.kv4_ref.kv_ref, ...), custom_call_target="tpu_custom_call" | custom-call | flops 1 | bytes 1 | tf_op jit(solution)/shard_map/attention_last/pallas_call | solution.py:448
  73.9 0.1 collective-permute-start.21
  74.0 3.2 %collective-permute-start.22 = (bf16[128,896]{1,0:T(8,128)(2,1)S(1)}, bf16[128,896]{1,0:T(8,128)(2,1)S(1)}, u32[]{:S(2)}, u32[]{:S(2)}) collective-permute-start(bf16[128,896]{1,0:T(8,128)(2,1)S(1)} %get-tuple-element.60), channel_id=1, source_target_pairs={{0,7},{1,0},{2,1},{3,2},{4,3},{5,4},{6,5},{7,6},{8,15},{9,8},{10,9... | collective-permute-start | bytes 688136 | tf_op jit(solution)/shard_map/ppermute | solution.py:44
  77.3 4.7 %attention_full.1 = (bf16[128,896]{1,0:T(8,128)(2,1)S(1)}, bf16[128,896]{1,0:T(8,128)(2,1)S(1)}) custom-call(s32[4]{0:T(128)S(1)} %pad_add_fusion.info_ref, s32[1,6]{1,0:T(1,128)S(1)} %copy-done.3, bf16[512,896]{1,0:T(8,128)(2,1)S(1)} %q_project.1.q_ref, bf16[512,256]{1,0:T(8,128)(2,1)S(1)} %collective-permute-done.20.kv4_ref.kv_ref, ...), custom_call_target="tpu_custom_call" | custom-call | flops 1 | bytes 1 | tf_op jit(solution)/shard_map/attention_full/pallas_call | solution.py:402
  81.9 0.9 %collective-permute-done.21.other_top_ref = bf16[128,896]{1,0:T(8,128)(2,1)S(1)} collective-permute-done((bf16[128,896]{1,0:T(8,128)(2,1)S(1)}, bf16[128,896]{1,0:T(8,128)(2,1)S(1)}, u32[]{:S(2)}, u32[]{:S(2)}) %collective-permute-start.21) | collective-permute-done | bytes 229408 | tf_op jit(solution)/shard_map/ppermute | solution.py:44
  82.9 1.5 %output.1 = bf16[256,1792]{1,0:T(8,128)(2,1)} custom-call(s32[4]{0:T(128)S(1)} %pad_add_fusion.info_ref, bf16[128,896]{1,0:T(8,128)(2,1)S(1)} %get-tuple-element.55.own_top_ref, bf16[128,896]{1,0:T(8,128)(2,1)S(1)} %get-tuple-element.56.own_low_ref, bf16[128,896]{1,0:T(8,128)(2,1)S(1)} %collective-permute-done.21.other_top_ref, ...), custom_call_target="tpu_custom_call" | custom-call | flops 1 | bytes 1 | tf_op jit(solution)/shard_map/output/pallas_call | solution.py:137
  (22 shorter events, 0.1 us)
Async XLA Ops:
  0.0 13.9 %copy-start.3 = (s32[1,6]{1,0:T(1,128)S(1)}, s32[1,6]{1,0:T(1,128)}, u32[]{:S(2)}) copy-start(s32[1,6]{1,0:T(1,128)} %lengths_ref.7) | copy-start | bytes 76
  0.0 1.5 %copy-start = (bf16[256,3584]{1,0:T(8,128)(2,1)S(1)}, bf16[256,3584]{1,0:T(8,128)(2,1)}, u32[]{:S(2)}) copy-start(bf16[256,3584]{1,0:T(8,128)(2,1)} %hidden_ref.1) | copy-start | bytes 5505028
  1.5 0.7 copy-start.2
  2.2 7.4 %copy-start.1 = (bf16[112,2304]{1,0:T(8,128)(2,1)S(1)}, bf16[112,2304]{1,0:T(8,128)(2,1)}, u32[]{:S(2)}) copy-start(bf16[112,2304]{1,0:T(8,128)(2,1)} %weight_ref.1) | copy-start | bytes 1548292
  2.2 35.0 %copy-start.4 = (f32[2304]{0:T(1024)S(1)}, f32[2304]{0:T(1024)}, u32[]{:S(2)}) copy-start(f32[2304]{0:T(1024)} %param.8) | copy-start | bytes 27652
  3.5 31.7 %collective-permute-start.4 = (bf16[128,3584]{1,0:T(8,128)(2,1)S(1)}, bf16[128,3584]{1,0:T(8,128)(2,1)S(1)}, u32[]{:S(2)}, u32[]{:S(2)}) collective-permute-start(bf16[128,3584]{1,0:T(8,128)(2,1)S(1)} %get-tuple-element.44.rest_2_), channel_id=1, source_target_pairs={{0,1},{1,2},{2,3},{3,4},{4,5},{5,6},{6,7},{7,0},{8,9},{9,10},{10,1... | collective-permute-start | bytes 2752520 | tf_op jit(solution)/shard_map/ppermute | solution.py:44
  5.5 29.7 %collective-permute-start.5 = (bf16[128,3584]{1,0:T(8,128)(2,1)S(1)}, bf16[128,3584]{1,0:T(8,128)(2,1)}, u32[]{:S(2)}, u32[]{:S(2)}) collective-permute-start(bf16[128,3584]{1,0:T(8,128)(2,1)S(1)} %get-tuple-element.43.rest_1_), channel_id=1, source_target_pairs={{0,7},{1,0},{2,1},{3,2},{4,3},{5,4},{6,5},{7,6},{8,15},{9,8},{10,9... | collective-permute-start | bytes 2752520 | tf_op jit(solution)/shard_map/ppermute | solution.py:44
  10.3 7.9 %collective-permute-start = (bf16[112,1152]{1,0:T(8,128)(2,1)S(1)}, bf16[112,1152]{1,0:T(8,128)(2,1)S(1)}, u32[]{:S(2)}, u32[]{:S(2)}) collective-permute-start(bf16[112,1152]{1,0:T(8,128)(2,1)S(1)} %cut.1.refs_0_), channel_id=1, source_target_pairs={{0,32},{8,136},{16,48},{24,152},{32,0},{40,168},{48,16},{56,184},{... | collective-permute-start | bytes 774152 | tf_op jit(solution)/shard_map/ppermute | solution.py:54
  11.8 7.0 %collective-permute-start.1 = (bf16[112,1152]{1,0:T(8,128)(2,1)S(1)}, bf16[112,1152]{1,0:T(8,128)(2,1)S(1)}, u32[]{:S(2)}, u32[]{:S(2)}) collective-permute-start(bf16[112,1152]{1,0:T(8,128)(2,1)S(1)} %cut.1.refs_0_), channel_id=1, source_target_pairs={{0,16},{8,72},{16,32},{24,88},{32,48},{40,104},{48,0},{56,120},{64... | collective-permute-start | bytes 774152 | tf_op jit(solution)/shard_map/ppermute | solution.py:54
  13.9 7.5 %collective-permute-start.2 = (bf16[112,1152]{1,0:T(8,128)(2,1)S(1)}, bf16[112,1152]{1,0:T(8,128)(2,1)S(1)}, u32[]{:S(2)}, u32[]{:S(2)}) collective-permute-start(bf16[112,1152]{1,0:T(8,128)(2,1)S(1)} %cut.1.refs_0_), channel_id=1, source_target_pairs={{0,48},{8,200},{16,0},{24,216},{32,16},{40,232},{48,32},{56,248},{... | collective-permute-start | bytes 774152 | tf_op jit(solution)/shard_map/ppermute | solution.py:54
  21.5 7.6 %collective-permute-start.3 = (bf16[448,256]{1,0:T(8,128)(2,1)S(1)}, bf16[448,256]{1,0:T(8,128)(2,1)S(1)}, u32[]{:S(2)}, u32[]{:S(2)}) collective-permute-start(bf16[448,256]{1,0:T(8,128)(2,1)S(1)} %get-tuple-element.41.rest_4_), channel_id=1, source_target_pairs={{0,128},{8,40},{16,144},{24,56},{32,160},{40,8},{48,176},{56,24},{... | collective-permute-start | bytes 688136 | tf_op jit(solution)/shard_map/ppermute | solution.py:54
  24.8 7.1 %collective-permute-start.7 = (bf16[448,256]{1,0:T(8,128)(2,1)S(1)}, bf16[448,256]{1,0:T(8,128)(2,1)S(1)}, u32[]{:S(2)}, u32[]{:S(2)}) collective-permute-start(bf16[448,256]{1,0:T(8,128)(2,1)S(1)} %get-tuple-element.41.rest_4_), channel_id=1, source_target_pairs={{0,192},{8,56},{16,208},{24,8},{32,224},{40,24},{48,240},{56,40},{... | collective-permute-start | bytes 688136 | tf_op jit(solution)/shard_map/ppermute | solution.py:54
  25.8 8.8 %collective-permute-start.6 = (bf16[448,256]{1,0:T(8,128)(2,1)S(1)}, bf16[448,256]{1,0:T(8,128)(2,1)S(1)}, u32[]{:S(2)}, u32[]{:S(2)}) collective-permute-start(bf16[448,256]{1,0:T(8,128)(2,1)S(1)} %get-tuple-element.41.rest_4_), channel_id=1, source_target_pairs={{0,64},{8,24},{16,80},{24,40},{32,96},{40,56},{48,112},{56,8},{64,... | collective-permute-start | bytes 688136 | tf_op jit(solution)/shard_map/ppermute | solution.py:54
  29.1 13.4 %collective-permute-start.12 = (bf16[448,896]{1,0:T(8,128)(2,1)S(1)}, bf16[448,896]{1,0:T(8,128)(2,1)S(1)}, u32[]{:S(2)}, u32[]{:S(2)}) collective-permute-start(bf16[448,896]{1,0:T(8,128)(2,1)S(1)} %get-tuple-element.50.rest_0_), channel_id=1, source_target_pairs={{0,64},{8,24},{16,80},{24,40},{32,96},{40,56},{48,112},{56,8},{64,... | collective-permute-start | bytes 2408456 | tf_op jit(solution)/shard_map/ppermute | solution.py:54
  31.9 21.0 %collective-permute-start.13 = (bf16[448,896]{1,0:T(8,128)(2,1)S(1)}, bf16[448,896]{1,0:T(8,128)(2,1)S(1)}, u32[]{:S(2)}, u32[]{:S(2)}) collective-permute-start(bf16[448,896]{1,0:T(8,128)(2,1)S(1)} %get-tuple-element.50.rest_0_), channel_id=1, source_target_pairs={{0,192},{8,56},{16,208},{24,8},{32,224},{40,24},{48,240},{56,40},{... | collective-permute-start | bytes 2408456 | tf_op jit(solution)/shard_map/ppermute | solution.py:54
  34.6 18.3 %collective-permute-start.14 = (bf16[448,896]{1,0:T(8,128)(2,1)S(1)}, bf16[448,896]{1,0:T(8,128)(2,1)S(1)}, u32[]{:S(2)}, u32[]{:S(2)}) collective-permute-start(bf16[448,896]{1,0:T(8,128)(2,1)S(1)} %get-tuple-element.50.rest_0_), channel_id=1, source_target_pairs={{0,128},{8,40},{16,144},{24,56},{32,160},{40,8},{48,176},{56,24},{... | collective-permute-start | bytes 2408456 | tf_op jit(solution)/shard_map/ppermute | solution.py:54
  35.2 1.5 %collective-permute-start.8 = (bf16[448,256]{1,0:T(8,128)(2,1)S(1)}, bf16[448,256]{1,0:T(8,128)(2,1)S(1)}, u32[]{:S(2)}, u32[]{:S(2)}) collective-permute-start(bf16[448,256]{1,0:T(8,128)(2,1)S(1)} %get-tuple-element.41.rest_4_), channel_id=1, source_target_pairs={{0,8},{8,0},{1,9},{9,1},{2,10},{10,2},{3,11},{11,3},{4,12},{12,4},... | collective-permute-start | bytes 688136 | tf_op jit(solution)/shard_map/ppermute | solution.py:44
  35.2 1.8 %collective-permute-start.10 = (bf16[448,256]{1,0:T(8,128)(2,1)S(1)}, bf16[448,256]{1,0:T(8,128)(2,1)S(1)}, u32[]{:S(2)}, u32[]{:S(2)}) collective-permute-start(bf16[448,256]{1,0:T(8,128)(2,1)S(1)} %collective-permute-done.7.rest_6_), channel_id=1, source_target_pairs={{0,8},{8,0},{1,9},{9,1},{2,10},{10,2},{3,11},{11,3},{4,12},{12,4},... | collective-permute-start | bytes 688136 | tf_op jit(solution)/shard_map/ppermute | solution.py:44
  36.7 1.5 %collective-permute-start.9 = (bf16[448,256]{1,0:T(8,128)(2,1)S(1)}, bf16[448,256]{1,0:T(8,128)(2,1)S(1)}, u32[]{:S(2)}, u32[]{:S(2)}) collective-permute-start(bf16[448,256]{1,0:T(8,128)(2,1)S(1)} %collective-permute-done.6.rest_5_), channel_id=1, source_target_pairs={{0,8},{8,0},{1,9},{9,1},{2,10},{10,2},{3,11},{11,3},{4,12},{12,4},... | collective-permute-start | bytes 688136 | tf_op jit(solution)/shard_map/ppermute | solution.py:44
  37.0 1.5 %collective-permute-start.11 = (bf16[448,256]{1,0:T(8,128)(2,1)S(1)}, bf16[448,256]{1,0:T(8,128)(2,1)S(1)}, u32[]{:S(2)}, u32[]{:S(2)}) collective-permute-start(bf16[448,256]{1,0:T(8,128)(2,1)S(1)} %collective-permute-done.3.rest_7_), channel_id=1, source_target_pairs={{0,8},{8,0},{1,9},{9,1},{2,10},{10,2},{3,11},{11,3},{4,12},{12,4},... | collective-permute-start | bytes 688136 | tf_op jit(solution)/shard_map/ppermute | solution.py:44
  41.1 16.4 %collective-permute-start.15 = (bf16[512,256]{1,0:T(8,128)(2,1)S(1)}, bf16[512,256]{1,0:T(8,128)(2,1)S(1)}, u32[]{:S(2)}, u32[]{:S(2)}) collective-permute-start(bf16[512,256]{1,0:T(8,128)(2,1)S(1)} %get-tuple-element.49.kv0_ref), channel_id=1, source_target_pairs={{0,2},{1,3},{2,4},{3,5},{4,6},{5,7},{6,0},{7,1},{8,10},{9,11},{10,... | collective-permute-start | bytes 786440 | tf_op jit(solution)/shard_map/ppermute | solution.py:44
  57.5 2.3 %collective-permute-start.16 = (bf16[448,896]{1,0:T(8,128)(2,1)S(1)}, bf16[448,896]{1,0:T(8,128)(2,1)S(1)}, u32[]{:S(2)}, u32[]{:S(2)}) collective-permute-start(bf16[448,896]{1,0:T(8,128)(2,1)S(1)} %get-tuple-element.50.rest_0_), channel_id=1, source_target_pairs={{0,8},{8,0},{1,9},{9,1},{2,10},{10,2},{3,11},{11,3},{4,12},{12,4},... | collective-permute-start | bytes 2408456 | tf_op jit(solution)/shard_map/ppermute | solution.py:44
  57.5 3.5 %collective-permute-start.17 = (bf16[448,896]{1,0:T(8,128)(2,1)S(1)}, bf16[448,896]{1,0:T(8,128)(2,1)S(1)}, u32[]{:S(2)}, u32[]{:S(2)}) collective-permute-start(bf16[448,896]{1,0:T(8,128)(2,1)S(1)} %collective-permute-done.12.rest_1_), channel_id=1, source_target_pairs={{0,8},{8,0},{1,9},{9,1},{2,10},{10,2},{3,11},{11,3},{4,12},{12,4},... | collective-permute-start | bytes 2408456 | tf_op jit(solution)/shard_map/ppermute | solution.py:44
  58.0 4.1 %collective-permute-start.18 = (bf16[448,896]{1,0:T(8,128)(2,1)S(1)}, bf16[448,896]{1,0:T(8,128)(2,1)S(1)}, u32[]{:S(2)}, u32[]{:S(2)}) collective-permute-start(bf16[448,896]{1,0:T(8,128)(2,1)S(1)} %collective-permute-done.13.rest_2_), channel_id=1, source_target_pairs={{0,8},{8,0},{1,9},{9,1},{2,10},{10,2},{3,11},{11,3},{4,12},{12,4},... | collective-permute-start | bytes 2408456 | tf_op jit(solution)/shard_map/ppermute | solution.py:44
  58.0 5.2 %collective-permute-start.19 = (bf16[448,896]{1,0:T(8,128)(2,1)S(1)}, bf16[448,896]{1,0:T(8,128)(2,1)S(1)}, u32[]{:S(2)}, u32[]{:S(2)}) collective-permute-start(bf16[448,896]{1,0:T(8,128)(2,1)S(1)} %collective-permute-done.14.rest_3_), channel_id=1, source_target_pairs={{0,8},{8,0},{1,9},{9,1},{2,10},{10,2},{3,11},{11,3},{4,12},{12,4},... | collective-permute-start | bytes 2408456 | tf_op jit(solution)/shard_map/ppermute | solution.py:44
  58.5 13.4 %collective-permute-start.20 = (bf16[512,256]{1,0:T(8,128)(2,1)S(1)}, bf16[512,256]{1,0:T(8,128)(2,1)S(1)}, u32[]{:S(2)}, u32[]{:S(2)}) collective-permute-start(bf16[512,256]{1,0:T(8,128)(2,1)S(1)} %collective-permute-done.15.kv2_ref), channel_id=1, source_target_pairs={{0,2},{1,3},{2,4},{3,5},{4,6},{5,7},{6,0},{7,1},{8,10},{9,11},{10,... | collective-permute-start | bytes 786440 | tf_op jit(solution)/shard_map/ppermute | solution.py:44
  73.9 8.9 %collective-permute-start.21 = (bf16[128,896]{1,0:T(8,128)(2,1)S(1)}, bf16[128,896]{1,0:T(8,128)(2,1)S(1)}, u32[]{:S(2)}, u32[]{:S(2)}) collective-permute-start(bf16[128,896]{1,0:T(8,128)(2,1)S(1)} %get-tuple-element.59), channel_id=1, source_target_pairs={{0,1},{1,2},{2,3},{3,4},{4,5},{5,6},{6,7},{7,0},{8,9},{9,10},{10,1... | collective-permute-start | bytes 688136 | tf_op jit(solution)/shard_map/ppermute | solution.py:44
  74.0 8.8 %collective-permute-start.22 = (bf16[128,896]{1,0:T(8,128)(2,1)S(1)}, bf16[128,896]{1,0:T(8,128)(2,1)S(1)}, u32[]{:S(2)}, u32[]{:S(2)}) collective-permute-start(bf16[128,896]{1,0:T(8,128)(2,1)S(1)} %get-tuple-element.60), channel_id=1, source_target_pairs={{0,7},{1,0},{2,1},{3,2},{4,3},{5,4},{6,5},{7,6},{8,15},{9,8},{10,9... | collective-permute-start | bytes 688136 | tf_op jit(solution)/shard_map/ppermute | solution.py:44

commit v5 on v4

--- a/solution.py
+++ b/solution.py
@@ -303,25 +303,49 @@
     return jnp.where((key <= pos) & (key >= starts(lengths_ref, pos)), 0.0, MASKED)
 
 
+def masks_kernel(info_ref, lengths_ref, out_ref):
+    for tile in range(4):
+        mask = mask_of(info_ref, lengths_ref, tile, HALF * tile, 1152)
+        out_ref[HALF * tile : HALF * (tile + 1), :] = mask
+
+
+def make_masks(info, lengths):
+    return pl.pallas_call(
+        masks_kernel,
+        out_shape=jax.ShapeDtypeStruct((ROWS, 1152), jnp.float32),
+        in_specs=[SM, SM],
+        out_specs=VM,
+        compiler_params=params(6),
+        cost_estimate=SMALL,
+        name="masks",
+    )(info, lengths)
+
+
+def mask_view(mask_ref, tile, from_row, count):
+    first = from_row - HALF * tile
+    return mask_ref.at[HALF * tile : HALF * (tile + 1), first : first + count]
+
+
 def score(q_ref, tile, k, out_ref):
     out_ref[...] = lax.dot_general(
         stacked(q_ref, tile), k, (((1,), (1,)), ((), ())), preferred_element_type=jnp.float32
     )
 
 
-def soften(score_ref, mask, part, top, weight_ref):
+def top_of(score_ref, mask, part):
+    best = None
     for lane in range(0, mask.shape[1], 128):
         lanes = slice(lane, lane + 128)
-        weight = jnp.exp2(score_ref[part, lanes] * SCALE2 + mask[:, lanes] - top)
-        weight_ref[part, lanes] = weight.astype(jnp.bfloat16)
-
-
-def top_of(score_ref, mask, part):
-    best = score_ref[part, 0:128] * SCALE2 + mask[:, 0:128]
-    for lane in range(128, mask.shape[1], 128):
+        value = score_ref[part, lanes] * SCALE2 + mask[:, lanes]
+        score_ref[part, lanes] = value
+        best = value if best is None else jnp.maximum(best, value)
+    return jnp.broadcast_to(jnp.max(best, axis=1, keepdims=True), (HALF, HEAD_DIM))
+
+
+def soften(score_ref, part, top, weight_ref):
+    for lane in range(0, score_ref.shape[1], 128):
         lanes = slice(lane, lane + 128)
-        best = jnp.maximum(best, score_ref[part, lanes] * SCALE2 + mask[:, lanes])
-    return jnp.broadcast_to(jnp.max(best, axis=1, keepdims=True), (HALF, HEAD_DIM))
+        weight_ref[part, lanes] = jnp.exp2(score_ref[part, lanes] - top).astype(jnp.bfloat16)
 
 
 def load_values(v_ref, *blocks):
@@ -332,7 +356,7 @@
     v_ref[:, 128:256] = jnp.ones((at, 128), jnp.bfloat16)
 
 
-def weigh(tiles, kept, from_row, q_ref, k_ref, v_ref, score_refs, weight_refs, info_ref, lengths_ref):
+def weigh(tiles, kept, from_row, q_ref, k_ref, v_ref, score_refs, weight_refs, mask_ref):
     def keys(n):
         first = max(from_row, HALF * tiles[n]) - from_row
         return slice(first, first + kept[n])
@@ -341,30 +365,30 @@
     for n, tile in enumerate(tiles):
         if n + 1 < len(tiles):
             score(q_ref, tiles[n + 1], k_ref[keys(n + 1), :], score_refs[n + 1])
-        mask = mask_of(info_ref, lengths_ref, tile, max(from_row, HALF * tile), kept[n])
+        mask = mask_view(mask_ref, tile, max(from_row, HALF * tile), kept[n])
         tops = []
         for h in range(GROUP):
             part = slice(h * HALF, (h + 1) * HALF)
             top = top_of(score_refs[n], mask, part)
             tops.append(top)
-            soften(score_refs[n], mask, part, top, weight_refs[n])
+            soften(score_refs[n], part, top, weight_refs[n])
         yield n, tops, jnp.dot(weight_refs[n][...], v_ref[keys(n), :], preferred_element_type=jnp.float32)
 
 
-def first_kernel(tiles, info_ref, lengths_ref, q_ref, kv2_ref, kv0_ref, mix_ref, top_ref, k_ref, v_ref, *rest):
+def first_kernel(tiles, mask_ref, q_ref, kv2_ref, kv0_ref, mix_ref, top_ref, k_ref, v_ref, *rest):
     kept, n = [640 + HALF * tile for tile in tiles], len(tiles)
     k_ref[0:512, :] = kv2_ref[:, 0:128]
     k_ref[512:1024, :] = kv0_ref[:, 0:128]
     load_values(v_ref, kv2_ref, kv0_ref)
     for n, tops, mixed in weigh(
-        tiles, kept, 512, q_ref, k_ref, v_ref, rest[:n], rest[n:], info_ref, lengths_ref
+        tiles, kept, 512, q_ref, k_ref, v_ref, rest[:n], rest[n:], mask_ref
     ):
         for h, top in enumerate(tops):
             top_ref[n * STACK + h * HALF : n * STACK + (h + 1) * HALF, :] = top
         mix_ref[n * STACK : (n + 1) * STACK, :] = mixed
 
 
-def attention_first(tiles, info, lengths, q, kv2, kv0):
+def attention_first(tiles, masks, q, kv2, kv0):
     n, kept = len(tiles), [640 + HALF * tile for tile in tiles]
     return pl.pallas_call(
         functools.partial(first_kernel, tiles),
@@ -372,7 +396,7 @@
             jax.ShapeDtypeStruct((n * STACK, 256), jnp.float32),
             jax.ShapeDtypeStruct((n * STACK, 128), jnp.float32),
         ],
-        in_specs=[SM, SM] + [VM] * 3,
+        in_specs=[VM] * 4,
         out_specs=[VM] * 2,
         scratch_shapes=[pltpu.VMEM((1024, 128), jnp.bfloat16), pltpu.VMEM((1024, 256), jnp.bfloat16)]
         + [pltpu.VMEM((STACK, c), jnp.float32) for c in kept]
@@ -380,29 +404,29 @@
         compiler_params=params(18),
         cost_estimate=SMALL,
         name="attention_first",
-    )(info, lengths, q, kv2, kv0)
-
-
-def full_kernel(tiles, info_ref, lengths_ref, q_ref, kv4_ref, kv2_ref, kv0_ref, *rest):
+    )(masks, q, kv2, kv0)
+
+
+def full_kernel(tiles, mask_ref, q_ref, kv4_ref, kv2_ref, kv0_ref, *rest):
     n = len(tiles)
     outs, k_ref, v_ref, rest = rest[:n], rest[n], rest[n + 1], rest[n + 2 :]
     for at, block in enumerate((kv4_ref, kv2_ref, kv0_ref)):
         k_ref[at * 512 : (at + 1) * 512, :] = block[:, 0:128]
     load_values(v_ref, kv4_ref, kv2_ref, kv0_ref)
     for n, _, mixed in weigh(
-        tiles, [1152] * n, 0, q_ref, k_ref, v_ref, rest[:n], rest[n:], info_ref, lengths_ref
+        tiles, [1152] * n, 0, q_ref, k_ref, v_ref, rest[:n], rest[n:], mask_ref
     ):
         value = (mixed[:, 0:128] / mixed[:, 128:256]).astype(jnp.bfloat16)
         for h in range(GROUP):
             outs[n][:, h * HEAD_DIM : (h + 1) * HEAD_DIM] = value[h * HALF : (h + 1) * HALF]
 
 
-def attention_full(tiles, info, lengths, q, kv4, kv2, kv0):
+def attention_full(tiles, masks, q, kv4, kv2, kv0):
     n = len(tiles)
     return pl.pallas_call(
         functools.partial(full_kernel, tiles),
         out_shape=[jax.ShapeDtypeStruct((HALF, QC), jnp.bfloat16)] * n,
-        in_specs=[SM, SM] + [VM] * 4,
+        in_specs=[VM] * 5,
         out_specs=[VM] * n,
         scratch_shapes=[pltpu.VMEM((1536, 128), jnp.bfloat16), pltpu.VMEM((1536, 256), jnp.bfloat16)]
         + [pltpu.VMEM((STACK, 1152), jnp.float32)] * n
@@ -410,10 +434,10 @@
         compiler_params=params(22),
         cost_estimate=SMALL,
         name="attention_full",
-    )(info, lengths, q, kv4, kv2, kv0)
-
-
-def last_kernel(tiles, info_ref, lengths_ref, q_ref, kv_ref, mix_ref, top_ref, *rest):
+    )(masks, q, kv4, kv2, kv0)
+
+
+def last_kernel(tiles, mask_ref, q_ref, kv_ref, mix_ref, top_ref, *rest):
     n = len(tiles)
     outs, v_ref = rest[:n], rest[n]
     score_refs, weight_refs, keep_refs = rest[n + 1 : 2 * n + 1], rest[2 * n + 1 : 3 * n + 1], rest[3 * n + 1 :]
@@ -423,13 +447,13 @@
     for at, (tile, out_ref, score_ref, weight_ref, keep_ref) in enumerate(
         zip(tiles, outs, score_refs, weight_refs, keep_refs)
     ):
-        mask = mask_of(info_ref, lengths_ref, tile, HALF * tile, 512 - HALF * tile)
+        mask = mask_view(mask_ref, tile, HALF * tile, 512 - HALF * tile)
         for h in range(GROUP):
             part = slice(h * HALF, (h + 1) * HALF)
             old = top_ref[at * STACK + h * HALF : at * STACK + (h + 1) * HALF, :]
             top = jnp.maximum(top_of(score_ref, mask, part), old)
             keep_ref[part, :] = jnp.exp2(old - top)
-            soften(score_ref, mask, part, top, weight_ref)
+            soften(score_ref, part, top, weight_ref)
         mixed = jnp.dot(
             weight_ref[...], v_ref[HALF * tile : 512, :], preferred_element_type=jnp.float32
         )
@@ -442,13 +466,13 @@
             out_ref[:, h * HEAD_DIM : (h + 1) * HEAD_DIM] = value.astype(jnp.bfloat16)
 
 
-def attention_last(tiles, info, lengths, q, kv4, state):
+def attention_last(tiles, masks, q, kv4, state):
     n = len(tiles)
     counts = [512 - HALF * tile for tile in tiles]
     return pl.pallas_call(
         functools.partial(last_kernel, tiles),
         out_shape=[jax.ShapeDtypeStruct((HALF, QC), jnp.bfloat16)] * n,
-        in_specs=[SM, SM] + [VM] * 4,
+        in_specs=[VM] * 5,
         out_specs=[VM] * n,
         scratch_shapes=[pltpu.VMEM((512, 256), jnp.bfloat16)]
         + [pltpu.VMEM((STACK, c), jnp.float32) for c in counts]
@@ -457,7 +481,7 @@
         compiler_params=params(12),
         cost_estimate=SMALL,
         name="attention_last",
-    )(info, lengths, q, kv4, *state)
+    )(masks, q, kv4, *state)
 
 
 def body(hidden, norm_gain, qkv_weight, qkv_bias, repo_lengths):
@@ -485,16 +509,17 @@
     kv0, normed = kv_project(info, (before, low, high, after), kv_near, kv_far, bias, cosine, sine)
     kv2 = ring(kv0, "ctx", 2)
 
-    *q_near, kv2 = lax.optimization_barrier((*q_near, kv2))
+    masks = make_masks(info, repo_lengths)
+    *q_near, kv2, masks = lax.optimization_barrier((*q_near, kv2, masks))
     kv4 = ring(kv2, "ctx", 2)
     q_far = [ring(piece, "core", 1) for piece in q_near]
     q = q_project(info, normed, q_near, q_far, bias, cosine, sine)
 
-    state = attention_first((0, 3), info, repo_lengths, q, kv2, kv0)
-    back, ahead = attention_last((0, 3), info, repo_lengths, q, kv4, state)
+    state = attention_first((0, 3), masks, q, kv2, kv0)
+    back, ahead = attention_last((0, 3), masks, q, kv4, state)
     other_top = ring(ahead, "ctx", 1)
     other_low = ring(back, "ctx", -1)
-    own_top, own_low = attention_full((1, 2), info, repo_lengths, q, kv4, kv2, kv0)
+    own_top, own_low = attention_full((1, 2), masks, q, kv4, kv2, kv0)
     return output(info, own_top, own_low, other_top, other_low)
 
 

time: 84.8 us -> 84.8 us (level)
  waiting for transfers between devices: 33.3 us -> 31.7 us
  starting transfers between devices: 25.3 us -> 26.6 us
  local copies, waits for them, and re-layouts: 2.25 us -> 3.28 us
  Pallas kernels: 23.3 us -> 22.4 us
    ppermute x9, waiting for transfers between devices: 20.5 us -> 17.6 us  [hop(): return lax.ppermute(value, ('y', 'x', 'core'), pairs)]
    ppermute x14, waiting for transfers between devices: 12.8 us -> 14.1 us  [ring(): return lax.ppermute(value, axis, [(i, (i + step) % n) for i in range(n)])]
    ppermute x9, starting transfers between devices: 13.9 us -> 15.1 us  [hop(): return lax.ppermute(value, ('y', 'x', 'core'), pairs)]
    pallas_call x0 -> x1, Pallas kernels: none -> 1.04 us  [make_masks(): pl.pallas_call(masks_kernel, out_shape=jax.ShapeDtypeStruct((ROWS, 1152),...]
    unnamed x10, local copies, waits for them, and re-layouts: 2.24 us -> 3.28 us
where the time goes in v5:
time: 84.8 us; the launch traced here: 84.5 us
  waiting for transfers between devices  31.7 us (37%)
  starting transfers between devices  26.6 us (31%)
  Pallas kernels  22.4 us (26%)
  local copies, waits for them, and re-layouts  3.28 us (4%)
    ppermute x9, waiting for transfers between devices, hop(): return lax.ppermute(value, ('y', 'x', 'core'), pairs)  17.6 us
    ppermute x9, starting transfers between devices, hop(): return lax.ppermute(value, ('y', 'x', 'core'), pairs)  15.1 us
    ppermute x14, waiting for transfers between devices, ring(): return lax.ppermute(value, axis, [(i, (i + step) % n) for i in range(n)])  14.1 us
    ppermute x14, starting transfers between devices, ring(): return lax.ppermute(value, axis, [(i, (i + step) % n) for i in range(n)])  11.4 us
    pallas_call x1, Pallas kernels, q_project(): pl.pallas_call(functools.partial(q_kernel, count), out_shape=jax.ShapeDty...  5.13 us
    pallas_call x1, Pallas kernels, attention_full(): pl.pallas_call(functools.partial(full_kernel, tiles), out_shape=[jax.Shap...  4.07 us
    unnamed x10, local copies, waits for them, and re-layouts  3.28 us
    pallas_call x1, Pallas kernels, attention_first(): pl.pallas_call(functools.partial(first_kernel, tiles), out_shape=[jax.Sha...  2.92 us
  transfers between devices with their start and end apart: 23, of which 17 were waited for; matrix products, arithmetic and copies ran while one was open for 0% of the time, Pallas kernels for 22%

profile of v5, /device:TPU:6, one launch (start us, length us, event | category | flops | bytes accessed | tf_op | source)
XLA Modules:
  0.0 84.5 jit_solution(9001073784737477839)
XLA Ops:
  0.0 1.5 %copy-done = bf16[256,3584]{1,0:T(8,128)(2,1)S(1)} copy-done((bf16[256,3584]{1,0:T(8,128)(2,1)S(1)}, bf16[256,3584]{1,0:T(8,128)(2,1)}, u32[]{:S(2)}) %copy-start) | copy-done | bytes 1835032
  1.5 0.7 copy-done.2
  2.2 1.3 %norm.1 = (bf16[128,3584]{1,0:T(8,128)(2,1)S(1)}, bf16[128,3584]{1,0:T(8,128)(2,1)S(1)}) custom-call(bf16[256,3584]{1,0:T(8,128)(2,1)S(1)} %copy-done, f32[28,128]{1,0:T(8,128)S(1)} %bitcast.7), custom_call_target="tpu_custom_call" | custom-call | flops 1 | bytes 1 | tf_op jit(solution)/shard_map/norm/pallas_call | solution.py:185
  3.5 2.0 %collective-permute-start.7 = (bf16[128,3584]{1,0:T(8,128)(2,1)S(1)}, bf16[128,3584]{1,0:T(8,128)(2,1)S(1)}, u32[]{:S(2)}, u32[]{:S(2)}) collective-permute-start(bf16[128,3584]{1,0:T(8,128)(2,1)S(1)} %get-tuple-element.46.rest_2_), channel_id=1, source_target_pairs={{0,1},{1,2},{2,3},{3,4},{4,5},{5,6},{6,7},{7,0},{8,9},{9,10},{10,1... | collective-permute-start | bytes 2752520 | tf_op jit(solution)/shard_map/ppermute | solution.py:44
  5.5 4.0 %collective-permute-start.8 = (bf16[128,3584]{1,0:T(8,128)(2,1)S(1)}, bf16[128,3584]{1,0:T(8,128)(2,1)}, u32[]{:S(2)}, u32[]{:S(2)}) collective-permute-start(bf16[128,3584]{1,0:T(8,128)(2,1)S(1)} %get-tuple-element.45.rest_1_), channel_id=1, source_target_pairs={{0,7},{1,0},{2,1},{3,2},{4,3},{5,4},{6,5},{7,6},{8,15},{9,8},{10,9... | collective-permute-start | bytes 2752520 | tf_op jit(solution)/shard_map/ppermute | solution.py:44
  9.6 1.0 %copy-done.1 = bf16[112,2304]{1,0:T(8,128)(2,1)S(1)} copy-done((bf16[112,2304]{1,0:T(8,128)(2,1)S(1)}, bf16[112,2304]{1,0:T(8,128)(2,1)}, u32[]{:S(2)}) %copy-start.1) | copy-done | bytes 516120
  10.7 0.6 cut.1.refs_0_
  11.3 1.5 %collective-permute-start.2 = (bf16[112,1152]{1,0:T(8,128)(2,1)S(1)}, bf16[112,1152]{1,0:T(8,128)(2,1)S(1)}, u32[]{:S(2)}, u32[]{:S(2)}) collective-permute-start(bf16[112,1152]{1,0:T(8,128)(2,1)S(1)} %cut.1.refs_0_), channel_id=1, source_target_pairs={{0,32},{8,136},{16,48},{24,152},{32,0},{40,168},{48,16},{56,184},{... | collective-permute-start | bytes 774152 | tf_op jit(solution)/shard_map/ppermute | solution.py:54
  12.8 2.1 %collective-permute-start = (bf16[112,1152]{1,0:T(8,128)(2,1)S(1)}, bf16[112,1152]{1,0:T(8,128)(2,1)S(1)}, u32[]{:S(2)}, u32[]{:S(2)}) collective-permute-start(bf16[112,1152]{1,0:T(8,128)(2,1)S(1)} %cut.1.refs_0_), channel_id=1, source_target_pairs={{0,16},{8,72},{16,32},{24,88},{32,48},{40,104},{48,0},{56,120},{64... | collective-permute-start | bytes 774152 | tf_op jit(solution)/shard_map/ppermute | solution.py:54
  15.0 1.8 %tables.1 = (f32[512,128]{1,0:T(8,128)S(1)}, f32[512,128]{1,0:T(8,128)S(1)}) custom-call(s32[4]{0:T(128)S(1)} %pad_add_fusion.info_ref, s32[1,6]{1,0:T(1,128)S(1)} %copy-done.3, f32[1,128]{1,0:T(1,128)S(1)} %maximum_bitcast_fusion.freq_ref), custom_call_target="tpu_custom_call" | custom-call | flops 1 | bytes 1 | tf_op jit(solution)/shard_map/tables/pallas_call | solution.py:210
  16.8 2.4 %collective-permute-done.2.refs_3_ = bf16[112,1152]{1,0:T(8,128)(2,1)S(1)} collective-permute-done((bf16[112,1152]{1,0:T(8,128)(2,1)S(1)}, bf16[112,1152]{1,0:T(8,128)(2,1)S(1)}, u32[]{:S(2)}, u32[]{:S(2)}) %collective-permute-start.2) | collective-permute-done | bytes 258080 | tf_op jit(solution)/shard_map/ppermute | solution.py:54
  19.2 0.6 collective-permute-done.refs_1_
  19.8 2.6 %collective-permute-done.1.refs_2_ = bf16[112,1152]{1,0:T(8,128)(2,1)S(1)} collective-permute-done((bf16[112,1152]{1,0:T(8,128)(2,1)S(1)}, bf16[112,1152]{1,0:T(8,128)(2,1)S(1)}, u32[]{:S(2)}, u32[]{:S(2)}) %collective-permute-start.1) | collective-permute-done | bytes 258080 | tf_op jit(solution)/shard_map/ppermute | solution.py:54
  22.5 3.3 %collective-permute-start.6 = (bf16[448,256]{1,0:T(8,128)(2,1)S(1)}, bf16[448,256]{1,0:T(8,128)(2,1)S(1)}, u32[]{:S(2)}, u32[]{:S(2)}) collective-permute-start(bf16[448,256]{1,0:T(8,128)(2,1)S(1)} %get-tuple-element.43.rest_4_), channel_id=1, source_target_pairs={{0,128},{8,40},{16,144},{24,56},{32,160},{40,8},{48,176},{56,24},{... | collective-permute-start | bytes 688136 | tf_op jit(solution)/shard_map/ppermute | solution.py:54
  25.8 0.7 collective-permute-start.9
  26.5 2.6 %collective-permute-start.10 = (bf16[448,256]{1,0:T(8,128)(2,1)S(1)}, bf16[448,256]{1,0:T(8,128)(2,1)S(1)}, u32[]{:S(2)}, u32[]{:S(2)}) collective-permute-start(bf16[448,256]{1,0:T(8,128)(2,1)S(1)} %get-tuple-element.43.rest_4_), channel_id=1, source_target_pairs={{0,192},{8,56},{16,208},{24,8},{32,224},{40,24},{48,240},{56,40},{... | collective-permute-start | bytes 688136 | tf_op jit(solution)/shard_map/ppermute | solution.py:54
  29.0 1.1 %collective-permute-done.6.rest_7_ = bf16[448,256]{1,0:T(8,128)(2,1)S(1)} collective-permute-done((bf16[448,256]{1,0:T(8,128)(2,1)S(1)}, bf16[448,256]{1,0:T(8,128)(2,1)S(1)}, u32[]{:S(2)}, u32[]{:S(2)}) %collective-permute-start.6) | collective-permute-done | bytes 229408 | tf_op jit(solution)/shard_map/ppermute | solution.py:54
  30.1 1.7 %collective-permute-start.3 = (bf16[448,896]{1,0:T(8,128)(2,1)S(1)}, bf16[448,896]{1,0:T(8,128)(2,1)S(1)}, u32[]{:S(2)}, u32[]{:S(2)}) collective-permute-start(bf16[448,896]{1,0:T(8,128)(2,1)S(1)} %get-tuple-element.52.rest_0_), channel_id=1, source_target_pairs={{0,64},{8,24},{16,80},{24,40},{32,96},{40,56},{48,112},{56,8},{64,... | collective-permute-start | bytes 2408456 | tf_op jit(solution)/shard_map/ppermute | solution.py:54
  31.8 1.2 %collective-permute-done.9.rest_5_ = bf16[448,256]{1,0:T(8,128)(2,1)S(1)} collective-permute-done((bf16[448,256]{1,0:T(8,128)(2,1)S(1)}, bf16[448,256]{1,0:T(8,128)(2,1)S(1)}, u32[]{:S(2)}, u32[]{:S(2)}) %collective-permute-start.9) | collective-permute-done | bytes 229408 | tf_op jit(solution)/shard_map/ppermute | solution.py:54
  33.0 0.3 collective-permute-start.4
  33.4 3.0 %collective-permute-start.5 = (bf16[448,896]{1,0:T(8,128)(2,1)S(1)}, bf16[448,896]{1,0:T(8,128)(2,1)S(1)}, u32[]{:S(2)}, u32[]{:S(2)}) collective-permute-start(bf16[448,896]{1,0:T(8,128)(2,1)S(1)} %get-tuple-element.52.rest_0_), channel_id=1, source_target_pairs={{0,128},{8,40},{16,144},{24,56},{32,160},{40,8},{48,176},{56,24},{... | collective-permute-start | bytes 2408456 | tf_op jit(solution)/shard_map/ppermute | solution.py:54
  36.4 0.5 collective-permute-start.12
  36.9 1.0 %collective-permute-done.11.rest_8_ = bf16[448,256]{1,0:T(8,128)(2,1)S(1)} collective-permute-done((bf16[448,256]{1,0:T(8,128)(2,1)S(1)}, bf16[448,256]{1,0:T(8,128)(2,1)S(1)}, u32[]{:S(2)}, u32[]{:S(2)}) %collective-permute-start.11) | collective-permute-done | bytes 229408 | tf_op jit(solution)/shard_map/ppermute | solution.py:44
  37.9 0.1 collective-permute-start.13
  38.0 0.2 collective-permute-done.12.rest_9_
  38.2 0.2 collective-permute-start.14
  38.4 1.0 %collective-permute-done.13.rest_10_ = bf16[448,256]{1,0:T(8,128)(2,1)S(1)} collective-permute-done((bf16[448,256]{1,0:T(8,128)(2,1)S(1)}, bf16[448,256]{1,0:T(8,128)(2,1)S(1)}, u32[]{:S(2)}, u32[]{:S(2)}) %collective-permute-start.13) | collective-permute-done | bytes 229408 | tf_op jit(solution)/shard_map/ppermute | solution.py:44
  39.4 0.3 collective-permute-done.14.rest_11_
  39.7 2.6 %kv_project.1 = (bf16[512,256]{1,0:T(8,128)(2,1)S(1)}, bf16[512,3584]{1,0:T(8,128)(2,1)S(1)}) custom-call(s32[4]{0:T(128)S(1)} %pad_add_fusion.info_ref, f32[1,2304]{1,0:T(1,128)S(1)} %reshape.10.bias_ref, f32[512,128]{1,0:T(8,128)S(1)} %get-tuple-element.38.cos_ref, f32[512,128]{1,0:T(8,128)S(1)} %get-tuple-element.39.sin_ref, ...), custom_call_target="tpu_custom_call" | custom-call | flops 1 | bytes 1 | tf_op jit(solution)/shard_map/kv_project/pallas_call | solution.py:247
  42.3 0.3 collective-permute-start.15
  42.6 1.0 %masks.1.mask_ref = f32[512,1152]{1,0:T(8,128)S(1)} custom-call(s32[4]{0:T(128)S(1)} %pad_add_fusion.info_ref, s32[1,6]{1,0:T(1,128)S(1)} %copy-done.3), custom_call_target="tpu_custom_call" | custom-call | flops 1 | bytes 1 | tf_op jit(solution)/shard_map/masks/pallas_call | solution.py:313
  43.7 1.5 %collective-permute-done.4.rest_2_ = bf16[448,896]{1,0:T(8,128)(2,1)S(1)} collective-permute-done((bf16[448,896]{1,0:T(8,128)(2,1)S(1)}, bf16[448,896]{1,0:T(8,128)(2,1)S(1)}, u32[]{:S(2)}, u32[]{:S(2)}) %collective-permute-start.4) | collective-permute-done | bytes 802848 | tf_op jit(solution)/shard_map/ppermute | solution.py:54
  45.2 8.2 %collective-permute-done.5.rest_3_ = bf16[448,896]{1,0:T(8,128)(2,1)S(1)} collective-permute-done((bf16[448,896]{1,0:T(8,128)(2,1)S(1)}, bf16[448,896]{1,0:T(8,128)(2,1)S(1)}, u32[]{:S(2)}, u32[]{:S(2)}) %collective-permute-start.5) | collective-permute-done | bytes 802848 | tf_op jit(solution)/shard_map/ppermute | solution.py:54
  53.3 5.4 %collective-permute-done.15.kv2_ref = bf16[512,256]{1,0:T(8,128)(2,1)S(1)} collective-permute-done((bf16[512,256]{1,0:T(8,128)(2,1)S(1)}, bf16[512,256]{1,0:T(8,128)(2,1)S(1)}, u32[]{:S(2)}, u32[]{:S(2)}) %collective-permute-start.15) | collective-permute-done | bytes 262176 | tf_op jit(solution)/shard_map/ppermute | solution.py:44
  58.7 0.5 collective-permute-start.17
  59.2 0.5 collective-permute-start.19
  59.7 1.3 %collective-permute-done.16.rest_4_ = bf16[448,896]{1,0:T(8,128)(2,1)S(1)} collective-permute-done((bf16[448,896]{1,0:T(8,128)(2,1)S(1)}, bf16[448,896]{1,0:T(8,128)(2,1)S(1)}, u32[]{:S(2)}, u32[]{:S(2)}) %collective-permute-start.16) | collective-permute-done | bytes 802848 | tf_op jit(solution)/shard_map/ppermute | solution.py:44
  61.0 1.1 %collective-permute-done.17.rest_5_ = bf16[448,896]{1,0:T(8,128)(2,1)S(1)} collective-permute-done((bf16[448,896]{1,0:T(8,128)(2,1)S(1)}, bf16[448,896]{1,0:T(8,128)(2,1)S(1)}, u32[]{:S(2)}, u32[]{:S(2)}) %collective-permute-start.17) | collective-permute-done | bytes 802848 | tf_op jit(solution)/shard_map/ppermute | solution.py:44
  62.2 1.1 %collective-permute-done.18.rest_6_ = bf16[448,896]{1,0:T(8,128)(2,1)S(1)} collective-permute-done((bf16[448,896]{1,0:T(8,128)(2,1)S(1)}, bf16[448,896]{1,0:T(8,128)(2,1)S(1)}, u32[]{:S(2)}, u32[]{:S(2)}) %collective-permute-start.18) | collective-permute-done | bytes 802848 | tf_op jit(solution)/shard_map/ppermute | solution.py:44
  63.3 1.1 %collective-permute-done.19.rest_7_ = bf16[448,896]{1,0:T(8,128)(2,1)S(1)} collective-permute-done((bf16[448,896]{1,0:T(8,128)(2,1)S(1)}, bf16[448,896]{1,0:T(8,128)(2,1)S(1)}, u32[]{:S(2)}, u32[]{:S(2)}) %collective-permute-start.19) | collective-permute-done | bytes 802848 | tf_op jit(solution)/shard_map/ppermute | solution.py:44
  64.5 5.1 %q_project.1.q_ref = bf16[512,896]{1,0:T(8,128)(2,1)S(1)} custom-call(s32[4]{0:T(128)S(1)} %pad_add_fusion.info_ref, bf16[512,3584]{1,0:T(8,128)(2,1)S(1)} %get-tuple-element.51.x_ref, f32[1,2304]{1,0:T(1,128)S(1)} %reshape.10.bias_ref, f32[512,128]{1,0:T(8,128)S(1)} %get-tuple-element.38.cos_ref, f32[512,128]{1,0:T(8,128)S(1)} %get-tuple-element.39.sin_ref, ...), custom_call_target="tpu_custom_call" | custom-call | flops 1 | bytes 1 | tf_op jit(solution)/shard_map/q_project/pallas_call | solution.py:276
  69.6 2.9 %attention_first.1 = (f32[1792,256]{1,0:T(8,128)S(1)}, f32[1792,128]{1,0:T(8,128)S(1)}) custom-call(f32[512,1152]{1,0:T(8,128)S(1)} %masks.1.mask_ref, bf16[512,896]{1,0:T(8,128)(2,1)S(1)} %q_project.1.q_ref, bf16[512,256]{1,0:T(8,128)(2,1)S(1)} %collective-permute-done.15.kv2_ref, bf16[512,256]{1,0:T(8,128)(2,1)S(1)} %get-tuple-element.49.kv0_ref), custom_call_target="tpu_custom_call" | custom-call | flops 1 | bytes 1 | tf_op jit(solution)/shard_map/attention_first/pallas_call | solution.py:393
  72.5 1.4 %attention_last.1 = (bf16[128,896]{1,0:T(8,128)(2,1)S(1)}, bf16[128,896]{1,0:T(8,128)(2,1)S(1)}) custom-call(f32[512,1152]{1,0:T(8,128)S(1)} %masks.1.mask_ref, bf16[512,896]{1,0:T(8,128)(2,1)S(1)} %q_project.1.q_ref, bf16[512,256]{1,0:T(8,128)(2,1)S(1)} %collective-permute-done.20.kv4_ref.kv_ref, f32[1792,256]{1,0:T(8,128)S(1)} %get-tuple-element.59.mix_ref, ...), custom_call_target="tpu_custom_call" | custom-call | flops 1 | bytes 1 | tf_op jit(solution)/shard_map/attention_last/pallas_call | solution.py:472
  73.9 0.1 collective-permute-start.21
  74.0 3.2 %collective-permute-start.22 = (bf16[128,896]{1,0:T(8,128)(2,1)S(1)}, bf16[128,896]{1,0:T(8,128)(2,1)S(1)}, u32[]{:S(2)}, u32[]{:S(2)}) collective-permute-start(bf16[128,896]{1,0:T(8,128)(2,1)S(1)} %get-tuple-element.62), channel_id=1, source_target_pairs={{0,7},{1,0},{2,1},{3,2},{4,3},{5,4},{6,5},{7,6},{8,15},{9,8},{10,9... | collective-permute-start | bytes 688136 | tf_op jit(solution)/shard_map/ppermute | solution.py:44
  77.2 4.1 %attention_full.1 = (bf16[128,896]{1,0:T(8,128)(2,1)S(1)}, bf16[128,896]{1,0:T(8,128)(2,1)S(1)}) custom-call(f32[512,1152]{1,0:T(8,128)S(1)} %masks.1.mask_ref, bf16[512,896]{1,0:T(8,128)(2,1)S(1)} %q_project.1.q_ref, bf16[512,256]{1,0:T(8,128)(2,1)S(1)} %collective-permute-done.20.kv4_ref.kv_ref, bf16[512,256]{1,0:T(8,128)(2,1)S(1)} %collective-permute-done.15.kv2_ref, ...), custom_call_target="tpu_custom_call" | custom-call | flops 1 | bytes 1 | tf_op jit(solution)/shard_map/attention_full/pallas_call | solution.py:426
  81.3 1.5 %collective-permute-done.21.other_top_ref = bf16[128,896]{1,0:T(8,128)(2,1)S(1)} collective-permute-done((bf16[128,896]{1,0:T(8,128)(2,1)S(1)}, bf16[128,896]{1,0:T(8,128)(2,1)S(1)}, u32[]{:S(2)}, u32[]{:S(2)}) %collective-permute-start.21) | collective-permute-done | bytes 229408 | tf_op jit(solution)/shard_map/ppermute | solution.py:44
  82.8 1.5 %output.1 = bf16[256,1792]{1,0:T(8,128)(2,1)} custom-call(s32[4]{0:T(128)S(1)} %pad_add_fusion.info_ref, bf16[128,896]{1,0:T(8,128)(2,1)S(1)} %get-tuple-element.57.own_top_ref, bf16[128,896]{1,0:T(8,128)(2,1)S(1)} %get-tuple-element.58.own_low_ref, bf16[128,896]{1,0:T(8,128)(2,1)S(1)} %collective-permute-done.21.other_top_ref, ...), custom_call_target="tpu_custom_call" | custom-call | flops 1 | bytes 1 | tf_op jit(solution)/shard_map/output/pallas_call | solution.py:137
  (23 shorter events, 0.3 us)
Async XLA Ops:
  0.0 15.0 %copy-start.3 = (s32[1,6]{1,0:T(1,128)S(1)}, s32[1,6]{1,0:T(1,128)}, u32[]{:S(2)}) copy-start(s32[1,6]{1,0:T(1,128)} %lengths_ref.3) | copy-start | bytes 76
  0.0 1.5 %copy-start = (bf16[256,3584]{1,0:T(8,128)(2,1)S(1)}, bf16[256,3584]{1,0:T(8,128)(2,1)}, u32[]{:S(2)}) copy-start(bf16[256,3584]{1,0:T(8,128)(2,1)} %hidden_ref.1) | copy-start | bytes 5505028
  1.5 0.7 copy-start.2
  2.2 36.2 %copy-start.4 = (f32[2304]{0:T(1024)S(1)}, f32[2304]{0:T(1024)}, u32[]{:S(2)}) copy-start(f32[2304]{0:T(1024)} %param.8) | copy-start | bytes 27652
  3.5 32.9 %collective-permute-start.7 = (bf16[128,3584]{1,0:T(8,128)(2,1)S(1)}, bf16[128,3584]{1,0:T(8,128)(2,1)S(1)}, u32[]{:S(2)}, u32[]{:S(2)}) collective-permute-start(bf16[128,3584]{1,0:T(8,128)(2,1)S(1)} %get-tuple-element.46.rest_2_), channel_id=1, source_target_pairs={{0,1},{1,2},{2,3},{3,4},{4,5},{5,6},{6,7},{7,0},{8,9},{9,10},{10,1... | collective-permute-start | bytes 2752520 | tf_op jit(solution)/shard_map/ppermute | solution.py:44
  5.5 30.9 %collective-permute-start.8 = (bf16[128,3584]{1,0:T(8,128)(2,1)S(1)}, bf16[128,3584]{1,0:T(8,128)(2,1)}, u32[]{:S(2)}, u32[]{:S(2)}) collective-permute-start(bf16[128,3584]{1,0:T(8,128)(2,1)S(1)} %get-tuple-element.45.rest_1_), channel_id=1, source_target_pairs={{0,7},{1,0},{2,1},{3,2},{4,3},{5,4},{6,5},{7,6},{8,15},{9,8},{10,9... | collective-permute-start | bytes 2752520 | tf_op jit(solution)/shard_map/ppermute | solution.py:44
  9.6 1.0 %copy-start.1 = (bf16[112,2304]{1,0:T(8,128)(2,1)S(1)}, bf16[112,2304]{1,0:T(8,128)(2,1)}, u32[]{:S(2)}) copy-start(bf16[112,2304]{1,0:T(8,128)(2,1)} %weight_ref.1) | copy-start | bytes 1548292
  11.3 7.9 %collective-permute-start.2 = (bf16[112,1152]{1,0:T(8,128)(2,1)S(1)}, bf16[112,1152]{1,0:T(8,128)(2,1)S(1)}, u32[]{:S(2)}, u32[]{:S(2)}) collective-permute-start(bf16[112,1152]{1,0:T(8,128)(2,1)S(1)} %cut.1.refs_0_), channel_id=1, source_target_pairs={{0,32},{8,136},{16,48},{24,152},{32,0},{40,168},{48,16},{56,184},{... | collective-permute-start | bytes 774152 | tf_op jit(solution)/shard_map/ppermute | solution.py:54
  12.8 7.0 %collective-permute-start = (bf16[112,1152]{1,0:T(8,128)(2,1)S(1)}, bf16[112,1152]{1,0:T(8,128)(2,1)S(1)}, u32[]{:S(2)}, u32[]{:S(2)}) collective-permute-start(bf16[112,1152]{1,0:T(8,128)(2,1)S(1)} %cut.1.refs_0_), channel_id=1, source_target_pairs={{0,16},{8,72},{16,32},{24,88},{32,48},{40,104},{48,0},{56,120},{64... | collective-permute-start | bytes 774152 | tf_op jit(solution)/shard_map/ppermute | solution.py:54
  14.9 7.5 %collective-permute-start.1 = (bf16[112,1152]{1,0:T(8,128)(2,1)S(1)}, bf16[112,1152]{1,0:T(8,128)(2,1)S(1)}, u32[]{:S(2)}, u32[]{:S(2)}) collective-permute-start(bf16[112,1152]{1,0:T(8,128)(2,1)S(1)} %cut.1.refs_0_), channel_id=1, source_target_pairs={{0,48},{8,200},{16,0},{24,216},{32,16},{40,232},{48,32},{56,248},{... | collective-permute-start | bytes 774152 | tf_op jit(solution)/shard_map/ppermute | solution.py:54
  22.5 7.6 %collective-permute-start.6 = (bf16[448,256]{1,0:T(8,128)(2,1)S(1)}, bf16[448,256]{1,0:T(8,128)(2,1)S(1)}, u32[]{:S(2)}, u32[]{:S(2)}) collective-permute-start(bf16[448,256]{1,0:T(8,128)(2,1)S(1)} %get-tuple-element.43.rest_4_), channel_id=1, source_target_pairs={{0,128},{8,40},{16,144},{24,56},{32,160},{40,8},{48,176},{56,24},{... | collective-permute-start | bytes 688136 | tf_op jit(solution)/shard_map/ppermute | solution.py:54
  25.8 7.2 %collective-permute-start.9 = (bf16[448,256]{1,0:T(8,128)(2,1)S(1)}, bf16[448,256]{1,0:T(8,128)(2,1)S(1)}, u32[]{:S(2)}, u32[]{:S(2)}) collective-permute-start(bf16[448,256]{1,0:T(8,128)(2,1)S(1)} %get-tuple-element.43.rest_4_), channel_id=1, source_target_pairs={{0,64},{8,24},{16,80},{24,40},{32,96},{40,56},{48,112},{56,8},{64,... | collective-permute-start | bytes 688136 | tf_op jit(solution)/shard_map/ppermute | solution.py:54
  26.5 6.9 %collective-permute-start.10 = (bf16[448,256]{1,0:T(8,128)(2,1)S(1)}, bf16[448,256]{1,0:T(8,128)(2,1)S(1)}, u32[]{:S(2)}, u32[]{:S(2)}) collective-permute-start(bf16[448,256]{1,0:T(8,128)(2,1)S(1)} %get-tuple-element.43.rest_4_), channel_id=1, source_target_pairs={{0,192},{8,56},{16,208},{24,8},{32,224},{40,24},{48,240},{56,40},{... | collective-permute-start | bytes 688136 | tf_op jit(solution)/shard_map/ppermute | solution.py:54
  30.1 13.5 %collective-permute-start.3 = (bf16[448,896]{1,0:T(8,128)(2,1)S(1)}, bf16[448,896]{1,0:T(8,128)(2,1)S(1)}, u32[]{:S(2)}, u32[]{:S(2)}) collective-permute-start(bf16[448,896]{1,0:T(8,128)(2,1)S(1)} %get-tuple-element.52.rest_0_), channel_id=1, source_target_pairs={{0,64},{8,24},{16,80},{24,40},{32,96},{40,56},{48,112},{56,8},{64,... | collective-permute-start | bytes 2408456 | tf_op jit(solution)/shard_map/ppermute | solution.py:54
  33.0 12.2 %collective-permute-start.4 = (bf16[448,896]{1,0:T(8,128)(2,1)S(1)}, bf16[448,896]{1,0:T(8,128)(2,1)S(1)}, u32[]{:S(2)}, u32[]{:S(2)}) collective-permute-start(bf16[448,896]{1,0:T(8,128)(2,1)S(1)} %get-tuple-element.52.rest_0_), channel_id=1, source_target_pairs={{0,192},{8,56},{16,208},{24,8},{32,224},{40,24},{48,240},{56,40},{... | collective-permute-start | bytes 2408456 | tf_op jit(solution)/shard_map/ppermute | solution.py:54
  33.4 20.0 %collective-permute-start.5 = (bf16[448,896]{1,0:T(8,128)(2,1)S(1)}, bf16[448,896]{1,0:T(8,128)(2,1)S(1)}, u32[]{:S(2)}, u32[]{:S(2)}) collective-permute-start(bf16[448,896]{1,0:T(8,128)(2,1)S(1)} %get-tuple-element.52.rest_0_), channel_id=1, source_target_pairs={{0,128},{8,40},{16,144},{24,56},{32,160},{40,8},{48,176},{56,24},{... | collective-permute-start | bytes 2408456 | tf_op jit(solution)/shard_map/ppermute | solution.py:54
  36.4 1.5 %collective-permute-start.11 = (bf16[448,256]{1,0:T(8,128)(2,1)S(1)}, bf16[448,256]{1,0:T(8,128)(2,1)S(1)}, u32[]{:S(2)}, u32[]{:S(2)}) collective-permute-start(bf16[448,256]{1,0:T(8,128)(2,1)S(1)} %get-tuple-element.43.rest_4_), channel_id=1, source_target_pairs={{0,8},{8,0},{1,9},{9,1},{2,10},{10,2},{3,11},{11,3},{4,12},{12,4},... | collective-permute-start | bytes 688136 | tf_op jit(solution)/shard_map/ppermute | solution.py:44
  36.4 1.8 %collective-permute-start.12 = (bf16[448,256]{1,0:T(8,128)(2,1)S(1)}, bf16[448,256]{1,0:T(8,128)(2,1)S(1)}, u32[]{:S(2)}, u32[]{:S(2)}) collective-permute-start(bf16[448,256]{1,0:T(8,128)(2,1)S(1)} %collective-permute-done.9.rest_5_), channel_id=1, source_target_pairs={{0,8},{8,0},{1,9},{9,1},{2,10},{10,2},{3,11},{11,3},{4,12},{12,4},... | collective-permute-start | bytes 688136 | tf_op jit(solution)/shard_map/ppermute | solution.py:44
  37.9 1.5 %collective-permute-start.13 = (bf16[448,256]{1,0:T(8,128)(2,1)S(1)}, bf16[448,256]{1,0:T(8,128)(2,1)S(1)}, u32[]{:S(2)}, u32[]{:S(2)}) collective-permute-start(bf16[448,256]{1,0:T(8,128)(2,1)S(1)} %collective-permute-done.10.rest_6_), channel_id=1, source_target_pairs={{0,8},{8,0},{1,9},{9,1},{2,10},{10,2},{3,11},{11,3},{4,12},{12,4},... | collective-permute-start | bytes 688136 | tf_op jit(solution)/shard_map/ppermute | solution.py:44
  38.2 1.5 %collective-permute-start.14 = (bf16[448,256]{1,0:T(8,128)(2,1)S(1)}, bf16[448,256]{1,0:T(8,128)(2,1)S(1)}, u32[]{:S(2)}, u32[]{:S(2)}) collective-permute-start(bf16[448,256]{1,0:T(8,128)(2,1)S(1)} %collective-permute-done.6.rest_7_), channel_id=1, source_target_pairs={{0,8},{8,0},{1,9},{9,1},{2,10},{10,2},{3,11},{11,3},{4,12},{12,4},... | collective-permute-start | bytes 688136 | tf_op jit(solution)/shard_map/ppermute | solution.py:44
  42.3 16.4 %collective-permute-start.15 = (bf16[512,256]{1,0:T(8,128)(2,1)S(1)}, bf16[512,256]{1,0:T(8,128)(2,1)S(1)}, u32[]{:S(2)}, u32[]{:S(2)}) collective-permute-start(bf16[512,256]{1,0:T(8,128)(2,1)S(1)} %get-tuple-element.49.kv0_ref), channel_id=1, source_target_pairs={{0,2},{1,3},{2,4},{3,5},{4,6},{5,7},{6,0},{7,1},{8,10},{9,11},{10,... | collective-permute-start | bytes 786440 | tf_op jit(solution)/shard_map/ppermute | solution.py:44
  58.7 2.3 %collective-permute-start.16 = (bf16[448,896]{1,0:T(8,128)(2,1)S(1)}, bf16[448,896]{1,0:T(8,128)(2,1)S(1)}, u32[]{:S(2)}, u32[]{:S(2)}) collective-permute-start(bf16[448,896]{1,0:T(8,128)(2,1)S(1)} %get-tuple-element.52.rest_0_), channel_id=1, source_target_pairs={{0,8},{8,0},{1,9},{9,1},{2,10},{10,2},{3,11},{11,3},{4,12},{12,4},... | collective-permute-start | bytes 2408456 | tf_op jit(solution)/shard_map/ppermute | solution.py:44
  58.7 3.5 %collective-permute-start.17 = (bf16[448,896]{1,0:T(8,128)(2,1)S(1)}, bf16[448,896]{1,0:T(8,128)(2,1)S(1)}, u32[]{:S(2)}, u32[]{:S(2)}) collective-permute-start(bf16[448,896]{1,0:T(8,128)(2,1)S(1)} %collective-permute-done.3.rest_1_), channel_id=1, source_target_pairs={{0,8},{8,0},{1,9},{9,1},{2,10},{10,2},{3,11},{11,3},{4,12},{12,4},... | collective-permute-start | bytes 2408456 | tf_op jit(solution)/shard_map/ppermute | solution.py:44
  59.2 4.1 %collective-permute-start.18 = (bf16[448,896]{1,0:T(8,128)(2,1)S(1)}, bf16[448,896]{1,0:T(8,128)(2,1)S(1)}, u32[]{:S(2)}, u32[]{:S(2)}) collective-permute-start(bf16[448,896]{1,0:T(8,128)(2,1)S(1)} %collective-permute-done.4.rest_2_), channel_id=1, source_target_pairs={{0,8},{8,0},{1,9},{9,1},{2,10},{10,2},{3,11},{11,3},{4,12},{12,4},... | collective-permute-start | bytes 2408456 | tf_op jit(solution)/shard_map/ppermute | solution.py:44
  59.2 5.2 %collective-permute-start.19 = (bf16[448,896]{1,0:T(8,128)(2,1)S(1)}, bf16[448,896]{1,0:T(8,128)(2,1)S(1)}, u32[]{:S(2)}, u32[]{:S(2)}) collective-permute-start(bf16[448,896]{1,0:T(8,128)(2,1)S(1)} %collective-permute-done.5.rest_3_), channel_id=1, source_target_pairs={{0,8},{8,0},{1,9},{9,1},{2,10},{10,2},{3,11},{11,3},{4,12},{12,4},... | collective-permute-start | bytes 2408456 | tf_op jit(solution)/shard_map/ppermute | solution.py:44
  59.7 12.8 %collective-permute-start.20 = (bf16[512,256]{1,0:T(8,128)(2,1)S(1)}, bf16[512,256]{1,0:T(8,128)(2,1)S(1)}, u32[]{:S(2)}, u32[]{:S(2)}) collective-permute-start(bf16[512,256]{1,0:T(8,128)(2,1)S(1)} %collective-permute-done.15.kv2_ref), channel_id=1, source_target_pairs={{0,2},{1,3},{2,4},{3,5},{4,6},{5,7},{6,0},{7,1},{8,10},{9,11},{10,... | collective-permute-start | bytes 786440 | tf_op jit(solution)/shard_map/ppermute | solution.py:44
  73.9 8.9 %collective-permute-start.21 = (bf16[128,896]{1,0:T(8,128)(2,1)S(1)}, bf16[128,896]{1,0:T(8,128)(2,1)S(1)}, u32[]{:S(2)}, u32[]{:S(2)}) collective-permute-start(bf16[128,896]{1,0:T(8,128)(2,1)S(1)} %get-tuple-element.61), channel_id=1, source_target_pairs={{0,1},{1,2},{2,3},{3,4},{4,5},{5,6},{6,7},{7,0},{8,9},{9,10},{10,1... | collective-permute-start | bytes 688136 | tf_op jit(solution)/shard_map/ppermute | solution.py:44
  74.0 8.9 %collective-permute-start.22 = (bf16[128,896]{1,0:T(8,128)(2,1)S(1)}, bf16[128,896]{1,0:T(8,128)(2,1)S(1)}, u32[]{:S(2)}, u32[]{:S(2)}) collective-permute-start(bf16[128,896]{1,0:T(8,128)(2,1)S(1)} %get-tuple-element.62), channel_id=1, source_target_pairs={{0,7},{1,0},{2,1},{3,2},{4,3},{5,4},{6,5},{7,6},{8,15},{9,8},{10,9... | collective-permute-start | bytes 688136 | tf_op jit(solution)/shard_map/ppermute | solution.py:44
